TPU v7x, 128 devices: a whole 4x4x4 slice. The times are simulated.
128 devices in a mesh: lat: 16 (over x, z), lon: 8 (over y, core).
Axes of the slice: x: 4, y: 4, z: 4, core: 2. Of those that a mesh axis runs over, the one named last changes fastest.
Arguments:
- thickness: float32 [2, 2048, 8192], P(None, 'lat', 'lon'), may hold values from 0.5 to 1.5
- winds: float32 [2, 2, 2048, 8192], P(None, None, 'lat', 'lon'), may hold values from -3 to 3
- terrain: float32 [2048, 8192], P('lat', 'lon'), may hold values from -1.5 to 1.5
- cutoffs: int32 [682], replicated, may hold values from 1 to 4096, as said below
Outputs:
- new_thickness: float32 [2, 2048, 8192], P(None, 'lat', 'lon')
- new_winds: float32 [2, 2, 2048, 8192], P(None, None, 'lat', 'lon')
Inputs may be any that keep to these rules, and one draw needn't show every extreme that they name: cutoffs[p] is the count of the lowest zonal wavenumbers kept on cap row p (the 341 southernmost rows from south to north, then the 341 northernmost).
All inputs are finite; a program needn't handle non-finite values.
Results may differ from a plain program's by a relative error of at most 0.0003.
Values sent between devices are 32-bit elements; how exact they have to be, the bound alone decides.
No kernel may reach another device: no remote copies, remote signals or barrier semaphores. Data moves between devices by JAX's collectives and lax.ppermute only.
A program may use at most 128 MiB of HBM per device.

v0:
```python
import math

import jax
import jax.numpy as jnp
from jax import lax
from jax.sharding import PartitionSpec as P

GRAVITY = 1.0
DENSITY_RATIO = 0.9
CORIOLIS = 1.0


def padded_2(cells, sides, width, closed):
    for axis, dim in sides:
        count = lax.axis_size(axis)
        ends = count if closed else count - 1
        head = lax.slice_in_dim(cells, 0, width, axis=dim)
        tail = lax.slice_in_dim(cells, cells.shape[dim] - width, cells.shape[dim], axis=dim)
        cells = jnp.concatenate(
            [
                lax.ppermute(tail, axis, [(i, (i + 1) % count) for i in range(ends)]),
                cells,
                lax.ppermute(head, axis, [((i + 1) % count, i) for i in range(ends)]),
            ],
            axis=dim,
        )
    return cells


def stencil_tendency(padded, row_start, total_rows, circle):
    row_count = padded.shape[1] - 2
    thickness = padded[0:2]
    zonal_wind = padded[2:4]
    ground = padded[6]
    row_ids = row_start - 1 + jnp.arange(row_count + 2, dtype=jnp.int32)
    spacing = math.pi / total_rows
    centre_lat = -0.5 * math.pi + (row_ids.astype(jnp.float32) + 0.5) * spacing
    face_lat = -0.5 * math.pi + (row_ids.astype(jnp.float32) + 1.0) * spacing
    face_live = jnp.where((row_ids >= 0) & (row_ids < total_rows - 1), 1.0, 0.0).astype(jnp.float32)
    centre_cos = jnp.cos(centre_lat)
    face_cos = jnp.cos(face_lat) * face_live
    face_inverse = face_live / (face_cos + (1.0 - face_live))
    merid_step = circle / (2.0 * total_rows)
    merid_wind = padded[4:6] * face_live[None, :, None]
    inner_cosine = centre_cos[1:-1][None, :, None]
    flux_east = 0.5 * (thickness[:, :, :-1] + thickness[:, :, 1:]) * zonal_wind[:, :, :-1]
    flux_north = (
        0.5
        * (thickness[:, :-1, :] + thickness[:, 1:, :])
        * merid_wind[:, :-1, :]
        * face_cos[:-1][None, :, None]
    )
    converge = (
        flux_east[:, 1:-1, 1:]
        - flux_east[:, 1:-1, :-1]
        + (flux_north[:, 1:, 1:-1] - flux_north[:, :-1, 1:-1]) / merid_step
    )
    thick_tend = -converge / inner_cosine
    kinetic = 0.25 * (
        zonal_wind[:, 1:, 1:] ** 2
        + zonal_wind[:, 1:, :-1] ** 2
        + merid_wind[:, 1:, 1:] ** 2
        + merid_wind[:, :-1, 1:] ** 2
    )
    upper_layer = thickness[0, 1:, 1:]
    lower_layer = thickness[1, 1:, 1:]
    surface = ground[1:, 1:]
    potential = jnp.stack(
        [
            GRAVITY * (upper_layer + lower_layer + surface),
            GRAVITY * (DENSITY_RATIO * upper_layer + lower_layer + surface),
        ]
    )
    energy = kinetic + potential
    merid_diff = merid_wind[:, :-1, 1:] - merid_wind[:, :-1, :-1]
    zonal_diff = (
        zonal_wind[:, 1:, :-1] * centre_cos[1:][None, :, None]
        - zonal_wind[:, :-1, :-1] * centre_cos[:-1][None, :, None]
    )
    absolute = (
        CORIOLIS * jnp.sin(face_lat[:-1])[None, :, None]
        + (merid_diff - zonal_diff / merid_step) * face_inverse[:-1][None, :, None]
    )
    merid_mean = 0.25 * (
        merid_wind[:, 1:-1, 1:-1]
        + merid_wind[:, 1:-1, 2:]
        + merid_wind[:, :-2, 1:-1]
        + merid_wind[:, :-2, 2:]
    )
    zonal_mean = 0.25 * (
        zonal_wind[:, 1:-1, 1:-1]
        + zonal_wind[:, 1:-1, :-2]
        + zonal_wind[:, 2:, 1:-1]
        + zonal_wind[:, 2:, :-2]
    )
    centre_energy = energy[:, :-1, :-1]
    east_energy = energy[:, :-1, 1:]
    north_energy = energy[:, 1:, :-1]
    zonal_tend = (
        0.5 * (absolute[:, 1:, 1:] + absolute[:, :-1, 1:]) * merid_mean
        - (east_energy - centre_energy) / inner_cosine
    )
    merid_tend = (
        -0.5 * (absolute[:, 1:, 1:] + absolute[:, 1:, :-1]) * zonal_mean
        - (north_energy - centre_energy) / merid_step
    ) * face_live[1:-1][None, :, None]
    return jnp.concatenate([thick_tend, zonal_tend, merid_tend], axis=0)


def spectral_filter(flat, keep_count):
    circle = flat.shape[1]
    second = 128
    first = circle // second
    index_first = jnp.arange(first, dtype=jnp.int32)
    index_second = jnp.arange(second, dtype=jnp.int32)
    angle_first = (
        2.0
        * math.pi
        / first
        * (index_first[:, None] * index_first[None, :] % first).astype(jnp.float32)
    )
    angle_second = (
        2.0
        * math.pi
        / second
        * (index_second[:, None] * index_second[None, :] % second).astype(jnp.float32)
    )
    angle_twist = (
        2.0
        * math.pi
        / circle
        * (index_first[:, None] * index_second[None, :] % circle).astype(jnp.float32)
    )
    cos_first, sin_first = (jnp.cos(angle_first), jnp.sin(angle_first))
    cos_second, sin_second = (jnp.cos(angle_second), jnp.sin(angle_second))
    cos_twist, sin_twist = (jnp.cos(angle_twist), jnp.sin(angle_twist))
    highest = lax.Precision.HIGHEST
    grid = flat.reshape(flat.shape[0], first, second)
    part_real = jnp.einsum("mab,ak->mkb", grid, cos_first, precision=highest)
    part_imag = -jnp.einsum("mab,ak->mkb", grid, sin_first, precision=highest)
    twist_real = part_real * cos_twist + part_imag * sin_twist
    twist_imag = part_imag * cos_twist - part_real * sin_twist
    spec_real = jnp.einsum("mkb,bl->mkl", twist_real, cos_second, precision=highest) + jnp.einsum(
        "mkb,bl->mkl", twist_imag, sin_second, precision=highest
    )
    spec_imag = jnp.einsum("mkb,bl->mkl", twist_imag, cos_second, precision=highest) - jnp.einsum(
        "mkb,bl->mkl", twist_real, sin_second, precision=highest
    )
    wavenumber = index_first[:, None] + first * index_second[None, :]
    folded = jnp.minimum(wavenumber, circle - wavenumber)
    keep = folded[None] < keep_count[:, None, None]
    spec_real = jnp.where(keep, spec_real, 0.0)
    spec_imag = jnp.where(keep, spec_imag, 0.0)
    back_real = jnp.einsum("mkl,lb->mkb", spec_real, cos_second, precision=highest) - jnp.einsum(
        "mkl,lb->mkb", spec_imag, sin_second, precision=highest
    )
    back_imag = jnp.einsum("mkl,lb->mkb", spec_real, sin_second, precision=highest) + jnp.einsum(
        "mkl,lb->mkb", spec_imag, cos_second, precision=highest
    )
    turn_real = back_real * cos_twist - back_imag * sin_twist
    turn_imag = back_real * sin_twist + back_imag * cos_twist
    signal = jnp.einsum("mkb,ka->mab", turn_real, cos_first, precision=highest) - jnp.einsum(
        "mkb,ka->mab", turn_imag, sin_first, precision=highest
    )
    return (signal / circle).reshape(flat.shape)


def filter_rows(circles, global_rows, cutoffs, total_rows, polar):
    channels = circles.shape[0]
    circle = circles.shape[-1]
    row_list = global_rows.reshape(-1)
    is_polar = (row_list < polar) | (row_list >= total_rows - polar)
    position = jnp.where(row_list < polar, row_list, row_list - (total_rows - 2 * polar))
    table_ids = jnp.arange(2 * polar, dtype=jnp.int32)
    keep_count = jnp.sum(
        jnp.where(position[:, None] == table_ids[None, :], cutoffs[None, :], 0),
        axis=1,
        dtype=jnp.int32,
    )
    flat = circles.reshape(channels * row_list.shape[0], circle)
    counts_all = jnp.tile(keep_count, channels)
    polar_all = jnp.tile(is_polar, channels)
    filtered = spectral_filter(flat, counts_all)
    return jnp.where(polar_all[:, None], filtered, flat).reshape(circles.shape)


def cap_filter(tendency, cutoffs, row_count, col_count, total_rows, polar):
    channels = tendency.shape[0]
    lat_count = lax.axis_size("lat")
    lon_count = lax.axis_size("lon")
    circle = col_count * lon_count
    device_count = lat_count * lon_count
    groups = row_count // device_count
    device_rank = lax.axis_index("lat") * lon_count + lax.axis_index("lon")
    outgoing = tendency.reshape(channels, groups, device_count, col_count)
    incoming = lax.all_to_all(outgoing, ("lat", "lon"), split_axis=2, concat_axis=2, tiled=True)
    circles = incoming.reshape(channels, groups, lat_count, circle)
    band_ids = jnp.arange(lat_count, dtype=jnp.int32)
    group_ids = jnp.arange(groups, dtype=jnp.int32)
    global_rows = band_ids[None, :] * row_count + group_ids[:, None] * device_count + device_rank
    cap_bands = min(lat_count, (polar + row_count - 1) // row_count)
    southern = filter_rows(
        circles[:, :, :cap_bands], global_rows[:, :cap_bands], cutoffs, total_rows, polar
    )
    northern = filter_rows(
        circles[:, :, lat_count - cap_bands :],
        global_rows[:, lat_count - cap_bands :],
        cutoffs,
        total_rows,
        polar,
    )
    filtered = jnp.concatenate(
        [southern, circles[:, :, cap_bands : lat_count - cap_bands], northern], axis=2
    )
    returning = lax.all_to_all(
        filtered.reshape(channels, groups, device_count, col_count),
        ("lat", "lon"),
        split_axis=2,
        concat_axis=2,
        tiled=True,
    )
    return returning.reshape(channels, row_count, col_count)


def body(thickness, winds, terrain, cutoffs):
    row_count = thickness.shape[1]
    col_count = thickness.shape[2]
    total_rows = row_count * lax.axis_size("lat")
    circle = col_count * lax.axis_size("lon")
    polar = (total_rows + 2) // 6
    row_start = lax.axis_index("lat") * row_count
    global_rows = row_start + jnp.arange(row_count, dtype=jnp.int32)
    live = jnp.where(global_rows < total_rows - 1, 1.0, 0.0).astype(jnp.float32)
    current = jnp.concatenate([thickness, winds[0], winds[1] * live[None, :, None]], axis=0)
    step_size = 0.1 * min(1.0, circle / (2.0 * total_rows))
    anchor = current
    for fraction in (1.0 / 3.0, 0.5, 1.0):
        stacked = jnp.concatenate([current, terrain[None]], axis=0)
        lat_rims = padded_2(stacked, (("lat", 1),), 1, False)
        padded = padded_2(lat_rims, (("lon", 2),), 1, True)
        tendency = stencil_tendency(padded, row_start, total_rows, circle)
        tendency = cap_filter(tendency, cutoffs, row_count, col_count, total_rows, polar)
        current = anchor + fraction * step_size * tendency
    return (current[0:2], current[2:6].reshape(2, 2, row_count, col_count))


def solution(mesh):
    in_specs = (P(None, "lat", "lon"), P(None, None, "lat", "lon"), P("lat", "lon"), P())
    out_specs = (P(None, "lat", "lon"), P(None, None, "lat", "lon"))
    return jax.shard_map(body, mesh=mesh, in_specs=in_specs, out_specs=out_specs, check_vma=False)
```

profile of v0, /device:TPU:1, one launch (start us, length us, event | category | flops | bytes accessed | tf_op | source)
XLA Modules:
  0.0 642.8 jit_solution(16085716456518876196)
XLA Ops:
  6.8 4.4 collective-permute-start
  12.6 3.3 collective-permute-done.1
  23.2 6.7 %collective-permute-done.3 = f32[7,130,1]{2,1,0:T(8,128)S(1)} collective-permute-done((f32[7,130,1]{2,1,0:T(8,128)S(1)}, f32[7,130,1]{2,1,0:T(8,128)S(1)}, u32[]{:S(2)}, u32[]{:S(2)}) %collective-permute-start.3) | collective-permute-done | bytes 3672 | tf_op jit(solution)/shard_map/ppermute | solution.py:23
  29.9 6.6 %concatenate.105 = f32[7,130,1026]{2,1,0:T(8,128)} concatenate(f32[7,130,1]{2,1,0:T(8,128)} %collective-permute-done.2, f32[7,130,1024]{2,1,0:T(8,128)} %copy-done.18, f32[7,130,1]{2,1,0:T(8,128)S(1)} %collective-permute-done.3), dimensions={2} | concatenate | bytes 7469280 | tf_op jit(solution)/shard_map/concatenate | solution.py:19
  39.3 6.4 fusion.11
  52.2 4.9 copy.100
  57.1 10.5 %all-to-all-start = ((f32[6,1,128,1024]{3,1,0,2:T(1,128)}), f32[6,1,128,1024]{3,1,0,2:T(1,128)S(1)}, u32[]{:S(2)}, u32[]{:S(2)}) async-start(f32[6,1,128,1024]{3,1,0,2:T(1,128)} %copy.100), calls=%async_computation | async-start | bytes 6291456 | tf_op jit(solution)/shard_map/all_to_all | solution.py:196
  68.3 40.9 %all-to-all-done = f32[6,1,128,1024]{3,1,0,2:T(1,128)S(1)} async-done(((f32[6,1,128,1024]{3,1,0,2:T(1,128)}), f32[6,1,128,1024]{3,1,0,2:T(1,128)S(1)}, u32[]{:S(2)}, u32[]{:S(2)}) %all-to-all-start) | async-done | bytes 3145760 | tf_op jit(solution)/shard_map/all_to_all | solution.py:196
  111.9 3.4 reshape.250
  165.7 3.1 reshape.254
  168.8 3.2 copy.102
  172.1 46.0 %all_to_all.30 = f32[6,1,128,1024]{3,1,0,2:T(1,128)S(1)} all-to-all(f32[6,1,128,1024]{3,1,0,2:T(1,128)S(1)} %copy.102), channel_id=1, replica_groups=mesh['lat'=16,'lon'=8] {'lat','lon'}, dimensions={2} | all-to-all | bytes 6291456 | tf_op jit(solution)/shard_map/all_to_all | solution.py:215
  223.5 3.3 collective-permute-done.5
  232.6 5.5 collective-permute-done.7
  238.3 6.7 %concatenate.113 = f32[7,130,1026]{2,1,0:T(8,128)} concatenate(f32[7,130,1]{2,1,0:T(8,128)} %collective-permute-done.6, f32[7,130,1024]{2,1,0:T(8,128)} %copy-done.19, f32[7,130,1]{2,1,0:T(8,128)} %collective-permute-done.7), dimensions={2} | concatenate | bytes 7469280 | tf_op jit(solution)/shard_map/concatenate | solution.py:19
  249.7 8.8 %fusion.14 = (f32[7,130,1025]{2,1,0:T(8,128)S(1)}, f32[7,130,1025]{2,1,0:T(8,128)S(1)}) fusion(f32[1,128,1024]{2,1,0:T(8,128)S(1)} %bitcast.380, f32[7,1,1024]{2,1,0:T(1,128)S(1)} %collective-permute-done.5, f32[6,128,1024]{2,1,0:T(8,128)S(1)} %bitcast_add_fusion.2, f32[7,1,1024]{2,1,0:T(1,128)S(1)} %collective-permute-done.4, ...), kind=kLoop, calls=%fused_computation.25 | loop fusion | flops 7462000 | bytes 11196640 | tf_op jit(solution)/shard_map/concatenate | solution.py:19
  260.4 3.1 fusion.117
  264.7 3.2 copy.104
  267.9 52.4 %all_to_all.31 = f32[6,1,128,1024]{3,1,0,2:T(1,128)S(1)} all-to-all(f32[6,1,128,1024]{3,1,0,2:T(1,128)S(1)} %copy.104), channel_id=1, replica_groups=mesh['lat'=16,'lon'=8] {'lat','lon'}, dimensions={2} | all-to-all | bytes 6291456 | tf_op jit(solution)/shard_map/all_to_all | solution.py:196
  376.5 3.3 reshape.259
  379.8 3.2 copy.106
  383.0 46.0 %all_to_all.32 = f32[6,1,128,1024]{3,1,0,2:T(1,128)S(1)} all-to-all(f32[6,1,128,1024]{3,1,0,2:T(1,128)S(1)} %copy.106), channel_id=1, replica_groups=mesh['lat'=16,'lon'=8] {'lat','lon'}, dimensions={2} | all-to-all | bytes 6291456 | tf_op jit(solution)/shard_map/all_to_all | solution.py:215
  433.6 3.3 collective-permute-done.9
  442.7 5.5 collective-permute-done.11
  448.4 6.7 %concatenate.121 = f32[7,130,1026]{2,1,0:T(8,128)} concatenate(f32[7,130,1]{2,1,0:T(8,128)} %collective-permute-done.10, f32[7,130,1024]{2,1,0:T(8,128)} %copy-done.20, f32[7,130,1]{2,1,0:T(8,128)} %collective-permute-done.11), dimensions={2} | concatenate | bytes 7469280 | tf_op jit(solution)/shard_map/concatenate | solution.py:19
  459.8 8.6 %fusion.17 = (f32[7,130,1025]{2,1,0:T(8,128)S(1)}, f32[7,130,1025]{2,1,0:T(8,128)S(1)}) fusion(f32[1,128,1024]{2,1,0:T(8,128)S(1)} %bitcast.383, f32[7,1,1024]{2,1,0:T(1,128)S(1)} %collective-permute-done.9, f32[6,128,1024]{2,1,0:T(8,128)S(1)} %bitcast_add_fusion.1, f32[7,1,1024]{2,1,0:T(1,128)S(1)} %collective-permute-done.8, ...), kind=kLoop, calls=%fused_computation.28 | loop fusion | flops 7462000 | bytes 11196640 | tf_op jit(solution)/shard_map/concatenate | solution.py:19
  470.2 3.1 fusion.106
  474.5 3.2 copy.108
  477.8 52.4 %all_to_all.33 = f32[6,1,128,1024]{3,1,0,2:T(1,128)S(1)} all-to-all(f32[6,1,128,1024]{3,1,0,2:T(1,128)S(1)} %copy.108), channel_id=1, replica_groups=mesh['lat'=16,'lon'=8] {'lat','lon'}, dimensions={2} | all-to-all | bytes 6291456 | tf_op jit(solution)/shard_map/all_to_all | solution.py:196
  532.8 3.1 reshape.261
  589.6 3.2 copy.110
  592.9 46.0 %all_to_all.34 = f32[6,1,128,1024]{3,1,0,2:T(1,128)S(1)} all-to-all(f32[6,1,128,1024]{3,1,0,2:T(1,128)S(1)} %copy.110), channel_id=1, replica_groups=mesh['lat'=16,'lon'=8] {'lat','lon'}, dimensions={2} | all-to-all | bytes 6291456 | tf_op jit(solution)/shard_map/all_to_all | solution.py:215
  (252 shorter events, 230.6 us)
Async XLA Ops:
  2.1 48.9 %copy-start = (f32[2,128,1024]{2,1,0:T(8,128)}, f32[2,128,1024]{2,1,0:T(8,128)S(1)}, u32[]{:S(2)}) copy-start(f32[2,128,1024]{2,1,0:T(8,128)S(1)} %slice_bitcast_fusion) | copy-start | bytes 3145732
  3.8 47.1 %copy-start.4 = (f32[2,128,1024]{2,1,0:T(8,128)}, f32[2,128,1024]{2,1,0:T(8,128)S(1)}, u32[]{:S(2)}) copy-start(f32[2,128,1024]{2,1,0:T(8,128)S(1)} %bitcast_multiply_fusion) | copy-start | bytes 3145732
  6.8 5.9 collective-permute-start
  11.1 4.8 collective-permute-start.1
  19.9 10.0 %collective-permute-start.3 = (f32[7,130,1]{2,1,0:T(8,128)S(1)}, f32[7,130,1]{2,1,0:T(8,128)S(1)}, u32[]{:S(2)}, u32[]{:S(2)}) collective-permute-start(f32[7,130,1]{2,1,0:T(8,128)S(1)} %get-tuple-element.24), channel_id=1, source_target_pairs={{1,0},{2,1},{3,2},{4,3},{5,4},{6,5},{7,6},{0,7},{9,8},{10,9},{11,1... | collective-permute-start | bytes 10928 | tf_op jit(solution)/shard_map/ppermute | solution.py:23
  21.8 8.1 %collective-permute-start.2 = (f32[7,130,1]{2,1,0:T(8,128)S(1)}, f32[7,130,1]{2,1,0:T(8,128)}, u32[]{:S(2)}, u32[]{:S(2)}) collective-permute-start(f32[7,130,1]{2,1,0:T(8,128)S(1)} %get-tuple-element.25), channel_id=1, source_target_pairs={{0,1},{1,2},{2,3},{3,4},{4,5},{5,6},{6,7},{7,0},{8,9},{9,10},{10,1... | collective-permute-start | bytes 10928 | tf_op jit(solution)/shard_map/ppermute | solution.py:21
  37.7 8.5 %slice-start = ((s8[4386816]{0:T(1024)(128)(4,1)}), s8[4194304]{0:T(1024)(128)(4,1)S(1)}, s32[]{:S(2)}) async-start(s8[4386816]{0:T(1024)(128)(4,1)} %bitcast.385), calls=%async_computation.6 | async-start | bytes 8388608
  39.3 6.9 %slice-start.1 = ((s8[4386816]{0:T(1024)(128)(4,1)}), s8[192512]{0:T(1024)(128)(4,1)S(1)}, s32[]{:S(2)}) async-start(s8[4386816]{0:T(1024)(128)(4,1)} %bitcast.385), calls=%async_computation.7 | async-start | bytes 385024
  57.1 10.6 %copy-start.33 = (s32[682]{0:T(1024)S(1)}, s32[682]{0:T(1024)}, u32[]{:S(2)}) copy-start(s32[682]{0:T(1024)} %param.7) | copy-start | bytes 8188
  57.1 52.2 %all-to-all-start = ((f32[6,1,128,1024]{3,1,0,2:T(1,128)}), f32[6,1,128,1024]{3,1,0,2:T(1,128)S(1)}, u32[]{:S(2)}, u32[]{:S(2)}) async-start(f32[6,1,128,1024]{3,1,0,2:T(1,128)} %copy.100), calls=%async_computation | async-start | bytes 6291456 | tf_op jit(solution)/shard_map/all_to_all | solution.py:196
  151.3 4.3 copy-start.31
  172.1 46.1 %copy-start.1 = (f32[2,128,1024]{2,1,0:T(8,128)S(1)}, f32[2,128,1024]{2,1,0:T(8,128)}, u32[]{:S(2)}) copy-start(f32[2,128,1024]{2,1,0:T(8,128)} %copy-done) | copy-start | bytes 3145732
  172.1 46.1 %copy-start.5 = (f32[2,128,1024]{2,1,0:T(8,128)S(1)}, f32[2,128,1024]{2,1,0:T(8,128)}, u32[]{:S(2)}) copy-start(f32[2,128,1024]{2,1,0:T(8,128)} %copy-done.4) | copy-start | bytes 3145732
  172.1 46.0 %copy-start.15 = (f32[2,128,1024]{2,1,0:T(8,128)S(1)}, f32[2,128,1024]{2,1,0:T(8,128)}, u32[]{:S(2)}) copy-start(f32[2,128,1024]{2,1,0:T(8,128)} %param.4) | copy-start | bytes 3145732
  220.4 3.1 collective-permute-start.4
  222.2 4.6 collective-permute-start.5
  229.5 8.6 %collective-permute-start.7 = (f32[7,130,1]{2,1,0:T(8,128)S(1)}, f32[7,130,1]{2,1,0:T(8,128)}, u32[]{:S(2)}, u32[]{:S(2)}) collective-permute-start(f32[7,130,1]{2,1,0:T(8,128)S(1)} %get-tuple-element.22), channel_id=1, source_target_pairs={{1,0},{2,1},{3,2},{4,3},{5,4},{6,5},{7,6},{0,7},{9,8},{10,9},{11,1... | collective-permute-start | bytes 10928 | tf_op jit(solution)/shard_map/ppermute | solution.py:23
  232.6 5.7 collective-permute-start.6
  342.1 3.6 copy-start.25
  362.0 4.3 copy-start.32
  383.0 46.0 %copy-start.2 = (f32[2,128,1024]{2,1,0:T(8,128)S(1)}, f32[2,128,1024]{2,1,0:T(8,128)}, u32[]{:S(2)}) copy-start(f32[2,128,1024]{2,1,0:T(8,128)} %copy-done) | copy-start | bytes 3145732
  383.0 46.0 %copy-start.6 = (f32[2,128,1024]{2,1,0:T(8,128)S(1)}, f32[2,128,1024]{2,1,0:T(8,128)}, u32[]{:S(2)}) copy-start(f32[2,128,1024]{2,1,0:T(8,128)} %copy-done.4) | copy-start | bytes 3145732
  383.0 46.0 %copy-start.16 = (f32[2,128,1024]{2,1,0:T(8,128)S(1)}, f32[2,128,1024]{2,1,0:T(8,128)}, u32[]{:S(2)}) copy-start(f32[2,128,1024]{2,1,0:T(8,128)} %param.4) | copy-start | bytes 3145732
  430.3 6.6 %copy-start.11 = (f32[128,1024]{1,0:T(8,128)S(1)}, f32[128,1024]{1,0:T(8,128)}, u32[]{:S(2)}) copy-start(f32[128,1024]{1,0:T(8,128)} %param.6) | copy-start | bytes 1572868
  430.3 3.2 collective-permute-start.8
  432.3 4.6 collective-permute-start.9
  439.6 8.6 %collective-permute-start.11 = (f32[7,130,1]{2,1,0:T(8,128)S(1)}, f32[7,130,1]{2,1,0:T(8,128)}, u32[]{:S(2)}, u32[]{:S(2)}) collective-permute-start(f32[7,130,1]{2,1,0:T(8,128)S(1)} %get-tuple-element.20), channel_id=1, source_target_pairs={{1,0},{2,1},{3,2},{4,3},{5,4},{6,5},{7,6},{0,7},{9,8},{10,9},{11,1... | collective-permute-start | bytes 10928 | tf_op jit(solution)/shard_map/ppermute | solution.py:23
  442.7 5.7 collective-permute-start.10
  572.1 4.3 copy-start.30
  592.9 46.1 %copy-start.3 = (f32[2,128,1024]{2,1,0:T(8,128)S(1)}, f32[2,128,1024]{2,1,0:T(8,128)}, u32[]{:S(2)}) copy-start(f32[2,128,1024]{2,1,0:T(8,128)} %copy-done) | copy-start | bytes 3145732
  592.9 46.0 %copy-start.7 = (f32[2,128,1024]{2,1,0:T(8,128)S(1)}, f32[2,128,1024]{2,1,0:T(8,128)}, u32[]{:S(2)}) copy-start(f32[2,128,1024]{2,1,0:T(8,128)} %copy-done.4) | copy-start | bytes 3145732
  592.9 46.0 %copy-start.17 = (f32[2,128,1024]{2,1,0:T(8,128)S(1)}, f32[2,128,1024]{2,1,0:T(8,128)}, u32[]{:S(2)}) copy-start(f32[2,128,1024]{2,1,0:T(8,128)} %param.4) | copy-start | bytes 3145732
  (17 other events, 48.3 us)
where the time goes:
time: 649 us; the launch traced here: 643 us
  blocking collectives  243 us (37%)
  local copies, waits for them, and re-layouts  121 us (19%)
  matrix products  99.3 us (15%)
  other arithmetic  76.6 us (12%)
  waiting for transfers between devices  69 us (11%)
  starting transfers between devices  31.8 us (5%)
    all_to_all x3, blocking collectives, cap_filter(): lax.all_to_all(filtered.reshape(channels, groups, device_count, col_count...  138 us
    all_to_all x2, blocking collectives, cap_filter(): lax.all_to_all(outgoing, ('lat', 'lon'), split_axis=2, concat_axis=2, til...  105 us
    all_to_all x1, waiting for transfers between devices, cap_filter(): lax.all_to_all(outgoing, ('lat', 'lon'), split_axis=2, concat_axis=2, til...  40.9 us
    ppermute x6, waiting for transfers between devices, padded_2(): lax.ppermute(head, axis, [((i + 1) % count, i) for i in range(ends)])  27.6 us
    concatenate x6, other arithmetic, padded_2(): jnp.concatenate([lax.ppermute(tail, axis, [(i, (i + 1) % count) for i in...  26.7 us
    concatenate x3, local copies, waits for them, and re-layouts, padded_2(): jnp.concatenate([lax.ppermute(tail, axis, [(i, (i + 1) % count) for i in...  20 us
    reshape x6, local copies, waits for them, and re-layouts, cap_filter(): filtered.reshape(channels, groups, device_count, col_count)  19.1 us
    another operation x6, local copies, waits for them, and re-layouts, spectral_filter(): grid = flat.reshape(flat.shape[0], first, second)  14.3 us
  transfers between devices with their start and end apart: 13, of which 9 were waited for; matrix products, arithmetic and copies ran while one was open for 0% of the time, Pallas kernels for 0%

commit v1 on v0

v1 whole, which is shorter than its diff:
```python
import functools
import math

import jax
import jax.numpy as jnp
import ml_dtypes
import numpy as np
from jax import lax
from jax.experimental import pallas as pl
from jax.experimental.pallas import tpu as pltpu
from jax.sharding import PartitionSpec as P

DENSITY_RATIO = 0.9
HALO = 3
SUB = 8
LANES = 128
RADIX = 64
HALF = RADIX // 2
SPEC_BLOCKS = HALF + 2
UNCUT = 1 << 20
TILE_ROWS = 128
PAIR = 16
COEFS = 7


def twisted(real, imag, k, n):
    angle = 2.0 * math.pi * k / n
    c, s = math.cos(angle), math.sin(angle)
    if k == 0:
        return real, imag
    if 8 * k == n:
        return (real + imag) * c, (imag - real) * c
    if 8 * k == 3 * n:
        return (imag - real) * s, -(real + imag) * s
    return real * c + imag * s, imag * c - real * s


def real_fft(x):
    n = len(x)
    if n == 1:
        return [x[0]], [None]
    er, ei = real_fft(x[0::2])
    odr, odi = real_fft(x[1::2])
    half = n // 2
    re, im = [None] * (half + 1), [None] * (half + 1)
    re[0], re[half] = er[0] + odr[0], er[0] - odr[0]
    for k in range(1, half // 2 + 1):
        if 2 * k == half:
            re[k], im[k] = er[k], -odr[k]
            continue
        tr, ti = twisted(odr[k], odi[k], k, n)
        re[k], im[k] = er[k] + tr, ei[k] + ti
        re[half - k], im[half - k] = er[k] - tr, ti - ei[k]
    return re, im


def real_ifft(re, im):
    n = 2 * (len(re) - 1)
    if n == 0:
        return [re[0]]
    half = n // 2
    if n == 2:
        return [re[0] + re[1], re[0] - re[1]]
    quarter = half // 2
    er, ei = [None] * (quarter + 1), [None] * (quarter + 1)
    odr, odi = [None] * (quarter + 1), [None] * (quarter + 1)
    er[0], odr[0] = re[0] + re[half], re[0] - re[half]
    for k in range(1, quarter + 1):
        if k == quarter:
            er[k], odr[k] = 2.0 * re[k], -2.0 * im[k]
            continue
        sr, si = re[k] + re[half - k], im[k] - im[half - k]
        dr, di = re[k] - re[half - k], im[k] + im[half - k]
        er[k], ei[k] = sr, si
        odi[k], odr[k] = twisted(di, dr, k, n)
    even = real_ifft(er, ei)
    odd = real_ifft(odr, odi)
    out = [None] * n
    out[0::2], out[1::2] = even, odd
    return out


def filter_tables():
    b = np.arange(LANES)
    angle = 2.0 * np.pi * (np.outer(b, b) % LANES) / LANES
    c, s = np.cos(angle), np.sin(angle)
    forward = np.block([[c, -s], [s, c]])
    backward = forward.T / (RADIX * LANES)

    def split(w):
        hi = w.astype(np.float32).astype(ml_dtypes.bfloat16)
        lo = (w - hi.astype(np.float64)).astype(np.float32).astype(ml_dtypes.bfloat16)
        return hi, lo

    k1 = np.arange(40)[:, None]
    twist = 2.0 * np.pi * k1 * b[None, :] / (RADIX * LANES)
    return (
        *split(forward),
        *split(backward),
        np.cos(twist).astype(np.float32),
        np.sin(twist).astype(np.float32),
    )


def pack_kernel(bands, lat_ref, th_ref, wi_ref, te_ref, south_ref, north_ref, out_ref):
    groups = out_ref.shape[0]
    height = out_ref.shape[2] // SUB
    own = height - 2 * HALO
    rows = groups * own

    def put(g, f, dst, count, read):
        for s in range(SUB):
            out_ref[g, f, pl.ds(dst * SUB + s, count, stride=SUB), :] = read(s)

    for f in range(7):
        if f < 2:
            src = th_ref.at[f]
        elif f < 6:
            src = wi_ref.at[f - 2]
        else:
            src = te_ref

        def rows_of(start, count, src=src):
            return lambda s: src[pl.ds(start, count), s * LANES : (s + 1) * LANES]

        for g in range(groups):
            for m in range(own // SUB):
                put(g, f, HALO + m * SUB, SUB, rows_of(g * own + m * SUB, SUB))
            if g > 0:
                put(g, f, 0, HALO, rows_of(g * own - HALO, HALO))
            else:
                put(g, f, 0, HALO, lambda s, f=f: south_ref[f, :, s * LANES : (s + 1) * LANES])
            if g < groups - 1:
                put(g, f, HALO + own, HALO, rows_of((g + 1) * own, HALO))
            else:
                put(g, f, HALO + own, HALO, lambda s, f=f: north_ref[f, :, s * LANES : (s + 1) * LANES])

    @pl.when(lat_ref[0] == bands - 1)
    def _():
        for f in (4, 5):
            out_ref[groups - 1, f, pl.ds((HALO + own - 1) * SUB, SUB), :] = jnp.zeros((SUB, LANES), jnp.float32)


def unpack_kernel(in_ref, th_ref, wi_ref):
    groups = in_ref.shape[0]
    own = in_ref.shape[2] // SUB
    for f in range(6):
        dst = th_ref.at[f] if f < 2 else wi_ref.at[f - 2]
        for g in range(groups):
            for m in range(own // SUB):
                for s in range(SUB):
                    dst[pl.ds(g * own + m * SUB, SUB), s * LANES : (s + 1) * LANES] = in_ref[
                        g, f, pl.ds(m * SUB * SUB + s, SUB, stride=SUB), :
                    ]


def step_kernel(
    merid_step,
    step_size,
    coef,
    flags,
    x_ref,
    cut_ref,
    wfh_ref,
    wfl_ref,
    wbh_ref,
    wbl_ref,
    twc_ref,
    tws_ref,
    out_ref,
    s_ref,
    t_ref,
    e_ref,
    z_ref,
    uu_ref,
    vv_ref,
    y_ref,
):
    chunks = x_ref.shape[0]
    height = x_ref.shape[1] // 7
    own = height - 2 * HALO
    lane = lax.broadcasted_iota(jnp.int32, (SUB, LANES), 1)
    sub = lax.broadcasted_iota(jnp.int32, (SUB, LANES), 0)
    last_lane, first_lane = lane == LANES - 1, lane == 0
    last_sub, first_sub = sub == SUB - 1, sub == 0
    dy_inv = 1.0 / merid_step

    def east(xs):
        y = [pltpu.roll(x, LANES - 1, 1) for x in xs]
        r = [pltpu.roll(v, SUB - 1, 0) for v in y]
        return [
            jnp.where(last_lane, jnp.where(last_sub, r[(d + 1) % chunks], r[d]), y[d])
            for d in range(chunks)
        ]

    def west(xs):
        y = [pltpu.roll(x, 1, 1) for x in xs]
        r = [pltpu.roll(v, 1, 0) for v in y]
        return [
            jnp.where(first_lane, jnp.where(first_sub, r[d - 1], r[d]), y[d]) for d in range(chunks)
        ]

    def stage(src, in_lo, fraction, final):
        in_hi = height - 1 - in_lo
        lo, hi = in_lo + 1, in_hi - 1
        count = hi - lo + 1

        def get(f, r):
            return [src[d, f * height + r] for d in range(chunks)]

        def terrain(r):
            return [x_ref[d, 6 * height + r] for d in range(chunks)]

        def corners(r, carry):
            rn = jnp.minimum(r + 1, in_hi)
            rs = jnp.maximum(r - 1, in_lo)
            c_half, cn_half = coef[0, r] * dy_inv, coef[0, rn] * dy_inv
            e_inv, sine = coef[2, r], coef[3, r]
            h0, h1, ground = get(0, r), get(1, r), terrain(r)
            base = [a + b for a, b in zip(h1, ground)]
            for k in range(2):
                u, v = get(2 + k, r), get(4 + k, r)
                uw, ve = west(u), east(v)
                un, vs = get(2 + k, rn), get(4 + k, rs)
                for d in range(chunks):
                    at = (r * 2 + k) * chunks + d
                    uu_ref[at] = u[d] + uw[d]
                    vv_ref[at] = v[d] + ve[d]
                    kin = 0.25 * (u[d] * u[d] + uw[d] * uw[d] + (v[d] * v[d] + vs[d] * vs[d]))
                    e_ref[at] = kin + (base[d] + (h0[d] if k == 0 else DENSITY_RATIO * h0[d]))
                    curl = (ve[d] - v[d]) - (un[d] * cn_half - u[d] * c_half)
                    z_ref[at] = sine + curl * e_inv
            return carry

        lax.fori_loop(in_lo, in_hi + 1, corners, 0)

        def tendencies(r, carry):
            c_inv = coef[1, r]
            fn, fs = coef[4, r] * (0.5 * dy_inv), coef[4, r - 1] * (0.5 * dy_inv)
            live = coef[5, r]
            for k in range(2):

                def face(ref, row):
                    return [ref[(row * 2 + k) * chunks + d] for d in range(chunks)]

                h, hn, hs = get(k, r), get(k, r + 1), get(k, r - 1)
                u, v, vs = get(2 + k, r), get(4 + k, r), get(4 + k, r - 1)
                he = east(h)
                fx = [0.5 * (h[d] + he[d]) * u[d] for d in range(chunks)]
                fxw = west(fx)
                en, ec = face(e_ref, r + 1), face(e_ref, r)
                ee = east(ec)
                z, zs = face(z_ref, r), face(z_ref, r - 1)
                zw = west(z)
                uu, uun = face(uu_ref, r), face(uu_ref, r + 1)
                vv, vvs = face(vv_ref, r), face(vv_ref, r - 1)
                for d in range(chunks):

                    def at(f):
                        return pl.ds(
                            pl.multiple_of((d * TILE_ROWS + f * count + (r - lo)) * SUB, SUB), SUB
                        )

                    north = (h[d] + hn[d]) * (v[d] * fn) - (h[d] + hs[d]) * (vs[d] * fs)
                    t_ref[at(k), :] = ((fxw[d] - fx[d]) - north) * c_inv
                    t_ref[at(2 + k), :] = (0.125 * (z[d] + zs[d])) * (vv[d] + vvs[d]) - (ee[d] - ec[d]) * c_inv
                    t_ref[at(4 + k), :] = live * (
                        (-0.125 * (z[d] + zw[d])) * (uu[d] + uun[d]) - dy_inv * (en[d] - ec[d])
                    )
            return carry

        lax.fori_loop(lo, hi + 1, tendencies, 0)

        def circle_filter(p, carry):
            @pl.when(flags[in_lo, p] > 0)
            def _():
                def place(a, half):
                    d, s = a // SUB, a % SUB
                    start = (d * TILE_ROWS + p * PAIR + half * SUB) * SUB + s
                    return pl.ds(start, SUB, stride=SUB)

                for half in range(2):
                    re, im = real_fft([t_ref[place(a, half), :] for a in range(RADIX)])
                    for k in range(HALF + 1):
                        c, s = twc_ref[k : k + 1, :], tws_ref[k : k + 1, :]
                        if im[k] is None:
                            yr, yi = (re[k], jnp.zeros_like(re[k])) if k == 0 else (re[k] * c, -(re[k] * s))
                        else:
                            yr, yi = re[k] * c + im[k] * s, im[k] * c - re[k] * s
                        at = pl.ds((k * 2 + half) * SUB, SUB)
                        y_ref[at, 0:LANES] = yr
                        y_ref[at, LANES : 2 * LANES] = yi
                cut = cut_ref[in_lo, pl.ds(pl.multiple_of(p * PAIR, PAIR), PAIR), :]
                cut2 = jnp.concatenate([cut, cut], axis=1)
                wave = lax.broadcasted_iota(jnp.int32, (PAIR, 2 * LANES), 1)
                wave = RADIX * jnp.where(wave >= LANES, wave - LANES, wave)

                def product(y, whi, wlo):
                    hi_part = y.astype(jnp.bfloat16)
                    lo_part = (y - hi_part.astype(jnp.float32)).astype(jnp.bfloat16)
                    dot = functools.partial(jnp.dot, preferred_element_type=jnp.float32)
                    return dot(hi_part, whi) + (dot(lo_part, whi) + dot(hi_part, wlo))

                block = 3
                for start in range(0, HALF + 1, block):
                    rows = slice(start * PAIR, (start + block) * PAIR)
                    spec = product(y_ref[rows, :], wfh_ref[...], wfl_ref[...])
                    keep = []
                    for k in range(start, start + block):
                        folded = jnp.minimum(wave + k, RADIX * LANES - k - wave)
                        keep.append(folded < cut2)
                    spec = jnp.where(jnp.concatenate(keep, axis=0), spec, 0.0)
                    y_ref[rows, :] = product(spec, wbh_ref[...], wbl_ref[...])
                for half in range(2):
                    re, im = [], []
                    for k in range(HALF + 1):
                        c, s = twc_ref[k : k + 1, :], tws_ref[k : k + 1, :]
                        at = pl.ds((k * 2 + half) * SUB, SUB)
                        yr = y_ref[at, 0:LANES]
                        if k == 0:
                            re.append(yr)
                            im.append(None)
                            continue
                        yi = y_ref[at, LANES : 2 * LANES]
                        re.append(yr * c - yi * s)
                        im.append(None if k == HALF else yr * s + yi * c)
                    circles = real_ifft(re, im)
                    polar = cut[half * SUB : (half + 1) * SUB] < UNCUT
                    for a in range(RADIX):
                        at = place(a, half)
                        t_ref[at, :] = jnp.where(polar, circles[a], t_ref[at, :])

            return carry

        lax.fori_loop(0, -(-6 * count // PAIR), circle_filter, 0)

        def update(r, carry):
            inside = coef[6, r]
            for f in range(6):
                for d in range(chunks):
                    at = pl.ds(pl.multiple_of((d * TILE_ROWS + f * count + (r - lo)) * SUB, SUB), SUB)
                    value = inside * (x_ref[d, f * height + r] + (fraction * step_size) * t_ref[at, :])
                    if final:
                        out_ref[d, f * own + (r - HALO)] = value
                    else:
                        s_ref[d, f * height + r] = value
            return carry

        lax.fori_loop(lo, hi + 1, update, 0)

    stage(x_ref, 0, 1.0 / 3.0, False)
    stage(s_ref, 1, 0.5, False)
    stage(s_ref, 2, 1.0, True)


def row_tables(cutoffs, row_start, height, total_rows, polar):
    row_ids = row_start - HALO + jnp.arange(height, dtype=jnp.int32)
    spacing = math.pi / total_rows
    centre_lat = -0.5 * math.pi + (row_ids.astype(jnp.float32) + 0.5) * spacing
    face_lat = -0.5 * math.pi + (row_ids.astype(jnp.float32) + 1.0) * spacing
    inside = jnp.where((row_ids >= 0) & (row_ids < total_rows), 1.0, 0.0).astype(jnp.float32)
    live = jnp.where((row_ids >= 0) & (row_ids < total_rows - 1), 1.0, 0.0).astype(jnp.float32)
    centre_cos = jnp.cos(centre_lat)
    face_cos = jnp.cos(face_lat) * live
    face_inverse = live / (face_cos + (1.0 - live))
    coef = jnp.stack(
        [centre_cos, 1.0 / centre_cos, face_inverse, jnp.sin(face_lat), face_cos, live, inside]
    )
    capped = ((row_ids >= 0) & (row_ids < polar)) | (
        (row_ids >= total_rows - polar) & (row_ids < total_rows)
    )
    position = jnp.where(row_ids < polar, row_ids, row_ids - (total_rows - 2 * polar))
    table_ids = jnp.arange(2 * polar, dtype=jnp.int32)
    cut = jnp.sum(
        jnp.where(position[:, None] == table_ids[None, :], cutoffs[None, :], 0), axis=1, dtype=jnp.int32
    )
    cut = jnp.where(capped, cut, UNCUT)
    stages = []
    for in_lo in range(3):
        rows = jnp.tile(cut[in_lo + 1 : height - 1 - in_lo], 6)
        stages.append(jnp.pad(rows, (0, TILE_ROWS - rows.shape[0]), constant_values=UNCUT))
    cuts = jnp.stack(stages)
    flags = jnp.any(cuts.reshape(3, TILE_ROWS // PAIR, PAIR) < UNCUT, axis=2).astype(jnp.int32)
    return coef, flags, jnp.broadcast_to(cuts[:, :, None], (3, TILE_ROWS, LANES))


def body(thickness, winds, terrain, cutoffs):
    row_count, col_count = thickness.shape[1], thickness.shape[2]
    bands, sectors = lax.axis_size("lat"), lax.axis_size("lon")
    total_rows, circle = row_count * bands, col_count * sectors
    polar = (total_rows + 2) // 6
    own = row_count // sectors
    height = own + 2 * HALO
    merid_step = circle / (2.0 * total_rows)
    step_size = 0.1 * min(1.0, merid_step)
    lat = lax.axis_index("lat")
    flat = winds.reshape(4, row_count, col_count)

    tail = jnp.concatenate(
        [thickness[:, -HALO:], flat[:, -HALO:], terrain[None, -HALO:]], axis=0
    )
    head = jnp.concatenate([thickness[:, :HALO], flat[:, :HALO], terrain[None, :HALO]], axis=0)
    south = lax.ppermute(tail, "lat", [(i, i + 1) for i in range(bands - 1)])
    north = lax.ppermute(head, "lat", [(i + 1, i) for i in range(bands - 1)])

    vmem = pl.BlockSpec(memory_space=pltpu.VMEM)
    smem = pl.BlockSpec(memory_space=pltpu.SMEM)
    packed = pl.pallas_call(
        functools.partial(pack_kernel, bands),
        out_shape=jax.ShapeDtypeStruct((sectors, 7, height * SUB, LANES), jnp.float32),
        in_specs=[smem] + [vmem] * 5,
        out_specs=vmem,
        compiler_params=pltpu.CompilerParams(vmem_limit_bytes=40 << 20),
        name="pack",
    )(lat.reshape(1).astype(jnp.int32), thickness, flat, terrain, south, north)
    circles = lax.all_to_all(packed, "lon", 0, 0)

    row_start = lat * row_count + lax.axis_index("lon") * own
    coef, flags, cuts = row_tables(cutoffs, row_start, height, total_rows, polar)
    tables = [jnp.asarray(t) for t in filter_tables()]
    stepped = pl.pallas_call(
        functools.partial(step_kernel, merid_step, step_size),
        out_shape=jax.ShapeDtypeStruct((sectors, 6 * own, SUB, LANES), jnp.float32),
        in_specs=[smem, smem] + [vmem] * 8,
        out_specs=vmem,
        scratch_shapes=[
            pltpu.VMEM((sectors, 6 * height, SUB, LANES), jnp.float32),
            pltpu.VMEM((sectors * TILE_ROWS * SUB, LANES), jnp.float32),
        ]
        + [pltpu.VMEM((height * 2 * sectors, SUB, LANES), jnp.float32)] * 4
        + [pltpu.VMEM(((HALF + 1) * PAIR, 2 * LANES), jnp.float32)],
        compiler_params=pltpu.CompilerParams(vmem_limit_bytes=56 << 20),
        name="step",
    )(coef, flags, circles.reshape(sectors, 7 * height, SUB, LANES), cuts, *tables)
    returned = lax.all_to_all(stepped.reshape(sectors, 6, own * SUB, LANES), "lon", 0, 0)
    new_thickness, new_winds = pl.pallas_call(
        unpack_kernel,
        out_shape=(
            jax.ShapeDtypeStruct(thickness.shape, jnp.float32),
            jax.ShapeDtypeStruct(flat.shape, jnp.float32),
        ),
        in_specs=[vmem],
        out_specs=(vmem, vmem),
        compiler_params=pltpu.CompilerParams(vmem_limit_bytes=40 << 20),
        name="unpack",
    )(returned)
    return new_thickness, new_winds.reshape(winds.shape)


def solution(mesh):
    in_specs = (P(None, "lat", "lon"), P(None, None, "lat", "lon"), P("lat", "lon"), P())
    out_specs = (P(None, "lat", "lon"), P(None, None, "lat", "lon"))
    return jax.shard_map(body, mesh=mesh, in_specs=in_specs, out_specs=out_specs, check_vma=False)
```

time: 649 us -> 192 us (0.30)
  blocking collectives: 243 us -> 42.3 us
  local copies, waits for them, and re-layouts: 121 us -> 10.9 us
  matrix products: 99.3 us -> 0 us
  other arithmetic: 76.6 us -> 1.17 us
  Pallas kernels: 0 us -> 64.2 us
  starting transfers between devices: 31.8 us -> 12.2 us
  waiting for transfers between devices: 69 us -> 60 us
    all_to_all x5 -> x1, blocking collectives: 243 us -> 42.3 us  [body(): lax.all_to_all(stepped.reshape(sectors, 6, own * SUB, LANES), 'lon', 0, 0)]
    dot_general x72 -> x0, matrix products: 99.3 us -> none  [the longest x6 13.5 us: spectral_filter(): part_imag = -jnp.einsum('mab,ak->mkb', grid, sin_first, precision=highest)]
    pallas_call x0 -> x3, Pallas kernels: none -> 64.2 us  [the longest x1 61 us: body(): pl.pallas_call(functools.partial(step_kernel, merid_step, step_size), out...]
    reshape x18 -> x0, local copies, waits for them, and re-layouts: 53.5 us -> none  [the longest x6 19.1 us: cap_filter(): filtered.reshape(channels, groups, device_count, col_count)]
    concatenate x11 -> x2, other arithmetic: 34.4 us -> 0.06 us  [the longest x1 0.03 us: body(): jnp.concatenate([thickness[:, -HALO:], flat[:, -HALO:], terrain[None, -HA...]
    ppermute x12 -> x2, waiting for transfers between devices: 28 us -> 4.41 us  [the longest x1 3.98 us: body(): north = lax.ppermute(head, 'lat', [(i + 1, i) for i in range(bands - 1)])]
    concatenate x3 -> x0, local copies, waits for them, and re-layouts: 20 us -> none  [padded_2(): jnp.concatenate([lax.ppermute(tail, axis, [(i, (i + 1) % count) for i in...]
    ppermute x12 -> x2, starting transfers between devices: 21.3 us -> 5.67 us  [the longest x1 4.38 us: body(): south = lax.ppermute(tail, 'lat', [(i, i + 1) for i in range(bands - 1)])]
  transfers between devices with their start and end apart: 13 -> 3, of which waited for: 9 -> 3; matrix products, arithmetic and copies ran while one was open for 0% -> 1% of each run, Pallas kernels for 0% -> 0%
where the time goes in v1:
time: 192 us
  Pallas kernels  64.2 us (33%)
  waiting for transfers between devices  60 us (31%)
  blocking collectives  42.3 us (22%)
  starting transfers between devices  12.2 us (6%)
  local copies, waits for them, and re-layouts  10.9 us (6%)
    pallas_call x1, Pallas kernels, body(): pl.pallas_call(functools.partial(step_kernel, merid_step, step_size), out...  61 us
    all_to_all x1, waiting for transfers between devices, body(): circles = lax.all_to_all(packed, 'lon', 0, 0)  55.6 us
    all_to_all x1, blocking collectives, body(): lax.all_to_all(stepped.reshape(sectors, 6, own * SUB, LANES), 'lon', 0, 0)  42.3 us
    all_to_all x1, starting transfers between devices, body(): circles = lax.all_to_all(packed, 'lon', 0, 0)  6.57 us
    unnamed x10, local copies, waits for them, and re-layouts  6.13 us
    ppermute x1, starting transfers between devices, body(): south = lax.ppermute(tail, 'lat', [(i, i + 1) for i in range(bands - 1)])  4.38 us
    ppermute x1, waiting for transfers between devices, body(): north = lax.ppermute(head, 'lat', [(i + 1, i) for i in range(bands - 1)])  3.98 us
  transfers between devices with their start and end apart: 3, of which 3 were waited for; matrix products, arithmetic and copies ran while one was open for 1% of the time, Pallas kernels for 0%

profile of v1, /device:TPU:1, one launch (start us, length us, event | category | flops | bytes accessed | tf_op | source)
XLA Modules:
  0.0 191.6 jit_solution(2319788105384385476)
XLA Ops:
  0.6 0.8 slice_bitcast_fusion
  1.4 1.0 fusion.4
  2.4 0.9 fusion.5
  3.3 4.4 %collective-permute-start = (f32[7,3,1024]{2,1,0:T(4,128)S(1)}, f32[7,3,1024]{2,1,0:T(4,128)S(1)}, u32[]{:S(2)}, u32[]{:S(2)}) collective-permute-start(f32[7,3,1024]{2,1,0:T(4,128)S(1)} %pad_maximum_fusion), channel_id=1, source_target_pairs={{0,8},{8,16},{16,24},{24,32},{32,40},{40,48},{48,56},{56,64},{64,7... | collective-permute-start | bytes 258056 | tf_op jit(solution)/shard_map/ppermute | solution.py:403
  7.8 1.3 collective-permute-start.1
  9.1 0.4 collective-permute-done.south_ref
  9.5 4.0 %collective-permute-done.1.north_ref = f32[7,3,1024]{2,1,0:T(4,128)S(1)} collective-permute-done((f32[7,3,1024]{2,1,0:T(4,128)S(1)}, f32[7,3,1024]{2,1,0:T(4,128)S(1)}, u32[]{:S(2)}, u32[]{:S(2)}) %collective-permute-start.1) | collective-permute-done | bytes 86048 | tf_op jit(solution)/shard_map/ppermute | solution.py:404
  13.5 1.6 copy-done.1
  15.1 1.2 copy-done.2
  16.3 1.0 copy-done.3
  17.3 1.0 pack.1
  18.3 2.3 %copy-done = f32[8,7,176,128]{3,2,1,0:T(8,128)} copy-done((f32[8,7,176,128]{3,2,1,0:T(8,128)}, f32[8,7,176,128]{3,2,1,0:T(8,128)S(1)}, u32[]{:S(2)}) %copy-start) | copy-done | bytes 5046296
  20.6 6.6 %all-to-all-start = ((f32[8,7,176,128]{3,2,1,0:T(8,128)}), f32[8,7,176,128]{3,2,1,0:T(8,128)}, u32[]{:S(2)}, u32[]{:S(2)}) async-start(f32[8,7,176,128]{3,2,1,0:T(8,128)} %copy-done), calls=%async_computation | async-start | bytes 10092544 | tf_op jit(solution)/shard_map/all_to_all | solution.py:416
  27.2 0.2 select_reduce_fusion
  27.4 0.1 slice.29
  27.5 0.1 slice.28
  27.5 0.1 slice.27
  27.6 0.1 tile.32
  27.7 0.1 tile.30
  27.8 0.1 stack.33
  27.9 0.1 stack.32
  27.9 0.1 tile.13
  28.0 0.1 stack.31
  28.1 0.2 fusion
  28.3 0.6 convert_element_type.31.flags
  29.0 0.1 add_divide_fusion
  29.0 0.6 stack.30.coef
  29.7 55.6 %all-to-all-done = f32[8,7,176,128]{3,2,1,0:T(8,128)} async-done(((f32[8,7,176,128]{3,2,1,0:T(8,128)}), f32[8,7,176,128]{3,2,1,0:T(8,128)}, u32[]{:S(2)}, u32[]{:S(2)}) %all-to-all-start) | async-done | bytes 5046304 | tf_op jit(solution)/shard_map/all_to_all | solution.py:416
  85.2 0.8 broadcast_in_dim.45.cut_ref
  86.0 61.0 %step.1 = f32[8,96,8,128]{3,2,1,0:T(8,128)} custom-call(f32[7,22]{1,0:T(8,128)} %stack.30.coef, s32[3,8]{1,0:T(4,128)} %convert_element_type.31.flags, f32[8,154,8,128]{3,2,1,0:T(8,128)} %bitcast.4.x_ref, s32[3,128,128]{2,1,0:T(8,128)} %broadcast_in_dim.45.cut_ref, bf16[256,256]{1,0:T(8,128)(2,1)} %constant.58.clone.wfh_ref, ...), custom_call_target="tpu_custom_call" | custom-call | tf_op jit(solution)/shard_map/step/pallas_call | solution.py:421
  147.0 42.3 %all_to_all.10.in_ref = f32[8,6,128,128]{3,2,1,0:T(8,128)S(1)} all-to-all(f32[8,6,128,128]{3,2,1,0:T(8,128)} %bitcast.17), channel_id=1, replica_groups=mesh['lat'=16,'lon'=8] {'lon'}, dimensions={0} | all-to-all | bytes 6291456 | tf_op jit(solution)/shard_map/all_to_all | solution.py:435
  189.3 2.3 %unpack.1 = (f32[2,128,1024]{2,1,0:T(8,128)}, f32[4,128,1024]{2,1,0:T(8,128)}) custom-call(f32[8,6,128,128]{3,2,1,0:T(8,128)S(1)} %all_to_all.10.in_ref), custom_call_target="tpu_custom_call" | custom-call | tf_op jit(solution)/shard_map/unpack/pallas_call | solution.py:436
  (19 shorter events, 0.2 us)
Async XLA Ops:
  3.3 6.2 %collective-permute-start = (f32[7,3,1024]{2,1,0:T(4,128)S(1)}, f32[7,3,1024]{2,1,0:T(4,128)S(1)}, u32[]{:S(2)}, u32[]{:S(2)}) collective-permute-start(f32[7,3,1024]{2,1,0:T(4,128)S(1)} %pad_maximum_fusion), channel_id=1, source_target_pairs={{0,8},{8,16},{16,24},{24,32},{32,40},{40,48},{48,56},{56,64},{64,7... | collective-permute-start | bytes 258056 | tf_op jit(solution)/shard_map/ppermute | solution.py:403
  7.8 5.7 %collective-permute-start.1 = (f32[7,3,1024]{2,1,0:T(4,128)S(1)}, f32[7,3,1024]{2,1,0:T(4,128)S(1)}, u32[]{:S(2)}, u32[]{:S(2)}) collective-permute-start(f32[7,3,1024]{2,1,0:T(4,128)S(1)} %pad_maximum_fusion.1), channel_id=1, source_target_pairs={{8,0},{16,8},{24,16},{32,24},{40,32},{48,40},{56,48},{64,56},{72,6... | collective-permute-start | bytes 258056 | tf_op jit(solution)/shard_map/ppermute | solution.py:404
  13.5 1.6 copy-start.1
  15.1 1.2 copy-start.2
  16.3 1.0 copy-start.3
  18.3 2.3 %copy-start = (f32[8,7,176,128]{3,2,1,0:T(8,128)}, f32[8,7,176,128]{3,2,1,0:T(8,128)S(1)}, u32[]{:S(2)}) copy-start(f32[8,7,176,128]{3,2,1,0:T(8,128)S(1)} %pack.1) | copy-start | bytes 15138820
  20.6 6.6 %copy-start.4 = (s32[682]{0:T(1024)S(1)}, s32[682]{0:T(1024)}, u32[]{:S(2)}) copy-start(s32[682]{0:T(1024)} %param.13) | copy-start | bytes 8188
  20.6 64.6 %all-to-all-start = ((f32[8,7,176,128]{3,2,1,0:T(8,128)}), f32[8,7,176,128]{3,2,1,0:T(8,128)}, u32[]{:S(2)}, u32[]{:S(2)}) async-start(f32[8,7,176,128]{3,2,1,0:T(8,128)} %copy-done), calls=%async_computation | async-start | bytes 10092544 | tf_op jit(solution)/shard_map/all_to_all | solution.py:416

commit v2 on v1

v2 whole, which is shorter than its diff:
```python
import functools
import math

import jax
import jax.numpy as jnp
import ml_dtypes
import numpy as np
from jax import lax
from jax.experimental import pallas as pl
from jax.experimental.pallas import tpu as pltpu
from jax.sharding import PartitionSpec as P

DENSITY_RATIO = 0.9
HALO = 3
SUB = 8
LANES = 128
RADIX = 64
HALF = RADIX // 2
SPEC_BLOCKS = HALF + 2
UNCUT = 1 << 20
TILE_ROWS = 128
PAIR = 16
UNITS = 2
BLOCK = 11
COEFS = 7


def twisted(real, imag, k, n):
    angle = 2.0 * math.pi * k / n
    c, s = math.cos(angle), math.sin(angle)
    if k == 0:
        return real, imag
    if 8 * k == n:
        return (real + imag) * c, (imag - real) * c
    if 8 * k == 3 * n:
        return (imag - real) * s, -(real + imag) * s
    return real * c + imag * s, imag * c - real * s


def real_fft(x):
    n = len(x)
    if n == 1:
        return [x[0]], [None]
    er, ei = real_fft(x[0::2])
    odr, odi = real_fft(x[1::2])
    half = n // 2
    re, im = [None] * (half + 1), [None] * (half + 1)
    re[0], re[half] = er[0] + odr[0], er[0] - odr[0]
    for k in range(1, half // 2 + 1):
        if 2 * k == half:
            re[k], im[k] = er[k], -odr[k]
            continue
        tr, ti = twisted(odr[k], odi[k], k, n)
        re[k], im[k] = er[k] + tr, ei[k] + ti
        re[half - k], im[half - k] = er[k] - tr, ti - ei[k]
    return re, im


def real_ifft(re, im):
    n = 2 * (len(re) - 1)
    if n == 0:
        return [re[0]]
    half = n // 2
    if n == 2:
        return [re[0] + re[1], re[0] - re[1]]
    quarter = half // 2
    er, ei = [None] * (quarter + 1), [None] * (quarter + 1)
    odr, odi = [None] * (quarter + 1), [None] * (quarter + 1)
    er[0], odr[0] = re[0] + re[half], re[0] - re[half]
    for k in range(1, quarter + 1):
        if k == quarter:
            er[k], odr[k] = 2.0 * re[k], -2.0 * im[k]
            continue
        sr, si = re[k] + re[half - k], im[k] - im[half - k]
        dr, di = re[k] - re[half - k], im[k] + im[half - k]
        er[k], ei[k] = sr, si
        odi[k], odr[k] = twisted(di, dr, k, n)
    even = real_ifft(er, ei)
    odd = real_ifft(odr, odi)
    out = [None] * n
    out[0::2], out[1::2] = even, odd
    return out


def filter_tables():
    b = np.arange(LANES)
    angle = 2.0 * np.pi * (np.outer(b, b) % LANES) / LANES
    c, s = np.cos(angle), np.sin(angle)
    forward = np.block([[c, -s], [s, c]])
    backward = forward.T / (RADIX * LANES)

    def split(w):
        hi = w.astype(np.float32).astype(ml_dtypes.bfloat16)
        lo = (w - hi.astype(np.float64)).astype(np.float32).astype(ml_dtypes.bfloat16)
        return hi, lo

    k1 = np.arange(40)[:, None]
    twist = 2.0 * np.pi * k1 * b[None, :] / (RADIX * LANES)
    return (
        *split(forward),
        *split(backward),
        np.cos(twist).astype(np.float32),
        np.sin(twist).astype(np.float32),
    )


def edge_kernel(th_ref, wi_ref, te_ref, tail_ref, head_ref, tile_ref, sems):
    rows = te_ref.shape[0]

    def copies(f):
        src = th_ref.at[f] if f < 2 else wi_ref.at[f - 2] if f < 6 else te_ref
        return [
            pltpu.make_async_copy(src.at[pl.ds(start, SUB)], tile_ref.at[i, f], sems.at[i, f])
            for i, start in enumerate((rows - SUB, 0))
        ]

    for f in range(7):
        for copy in copies(f):
            copy.start()
    for f in range(7):
        for i, copy in enumerate(copies(f)):
            copy.wait()
            out_ref, start = ((tail_ref, SUB - HALO), (head_ref, 0))[i]
            for s in range(SUB):
                out_ref[pl.ds(f * SUB + s, HALO, stride=7 * SUB), :] = tile_ref[
                    i, f, start : start + HALO, s * LANES : (s + 1) * LANES
                ]


def pack_kernel(bands, lat_ref, th_ref, wi_ref, te_ref, out_ref, piece_ref, sems):
    groups = out_ref.shape[0]
    height = out_ref.shape[1] // (7 * SUB)
    own = height - 2 * HALO

    for g in range(groups):
        for f in range(7):
            src = th_ref.at[f] if f < 2 else wi_ref.at[f - 2] if f < 6 else te_ref

            def put(dst, start, count):
                for s in range(SUB):
                    piece_ref[g, pl.ds((dst * 7 + f) * SUB + s, count, stride=7 * SUB), :] = src[
                        pl.ds(start, count), s * LANES : (s + 1) * LANES
                    ]

            for m in range(own // SUB):
                put(HALO + m * SUB, g * own + m * SUB, SUB)
            if g > 0:
                put(0, g * own - HALO, HALO)
            if g < groups - 1:
                put(HALO + own, (g + 1) * own, HALO)
        if g == groups - 1:

            @pl.when(lat_ref[0] == bands - 1)
            def _():
                for f in (4, 5):
                    at = pl.ds(((HALO + own - 1) * 7 + f) * SUB, SUB)
                    piece_ref[g, at, :] = jnp.zeros((SUB, LANES), jnp.float32)

        first = 0 if g > 0 else HALO * 7 * SUB
        last = (height if g < groups - 1 else HALO + own) * 7 * SUB
        span = pl.ds(first, last - first)
        pltpu.make_async_copy(piece_ref.at[g, span], out_ref.at[g, span], sems.at[g]).start()
    for g in range(groups):
        first = 0 if g > 0 else HALO * 7 * SUB
        last = (height if g < groups - 1 else HALO + own) * 7 * SUB
        span = pl.ds(first, last - first)
        pltpu.make_async_copy(piece_ref.at[g, span], out_ref.at[g, span], sems.at[g]).wait()


def rim_kernel(south_ref, north_ref, packed_ref, out_ref, sems):
    groups, length = out_ref.shape[0], out_ref.shape[1]
    rim = HALO * 7 * SUB
    low = pltpu.make_async_copy(south_ref, out_ref.at[0, pl.ds(0, rim)], sems.at[0])
    high = pltpu.make_async_copy(north_ref, out_ref.at[groups - 1, pl.ds(length - rim, rim)], sems.at[1])
    low.start()
    high.start()
    low.wait()
    high.wait()


def unpack_kernel(in_ref, th_ref, wi_ref):
    groups = in_ref.shape[0]
    own = in_ref.shape[1] // (6 * SUB)
    for f in range(6):
        dst = th_ref.at[f] if f < 2 else wi_ref.at[f - 2]
        for g in range(groups):
            for m in range(own // SUB):
                for s in range(SUB):
                    dst[pl.ds(g * own + m * SUB, SUB), s * LANES : (s + 1) * LANES] = in_ref[
                        g, pl.ds((m * SUB * 6 + f) * SUB + s, SUB, stride=6 * SUB), :
                    ]


def step_kernel(
    merid_step,
    step_size,
    coef,
    flags,
    x_hbm,
    cut_ref,
    wfh_ref,
    wfl_ref,
    wbh_ref,
    wbl_ref,
    twc_ref,
    tws_ref,
    out_hbm,
    x_ref,
    s_ref,
    out_ref,
    t_ref,
    in_sems,
    out_sems,
    e_ref,
    z_ref,
    uu_ref,
    vv_ref,
    *y_refs,
):
    chunks = x_ref.shape[0]
    height = x_ref.shape[1] // 7
    own = height - 2 * HALO
    lane = lax.broadcasted_iota(jnp.int32, (SUB, LANES), 1)
    sub = lax.broadcasted_iota(jnp.int32, (SUB, LANES), 0)
    last_lane, first_lane = lane == LANES - 1, lane == 0
    last_sub, first_sub = sub == SUB - 1, sub == 0
    dy_inv = 1.0 / merid_step

    def east(xs):
        y = [pltpu.roll(x, LANES - 1, 1) for x in xs]
        r = [pltpu.roll(v, SUB - 1, 0) for v in y]
        return [
            jnp.where(last_lane, jnp.where(last_sub, r[(d + 1) % chunks], r[d]), y[d])
            for d in range(chunks)
        ]

    def west(xs):
        y = [pltpu.roll(x, 1, 1) for x in xs]
        r = [pltpu.roll(v, 1, 0) for v in y]
        return [
            jnp.where(first_lane, jnp.where(first_sub, r[d - 1], r[d]), y[d]) for d in range(chunks)
        ]

    cuts_in = (0, height // 3, 2 * height // 3, height)

    def arrival(i):
        rows = pl.ds(cuts_in[i] * 7, (cuts_in[i + 1] - cuts_in[i]) * 7)
        return pltpu.make_async_copy(x_hbm.at[:, rows], x_ref.at[:, rows], in_sems.at[i])

    def departure(i):
        rows = pl.ds(i * (own // 2) * 6, (own // 2) * 6)
        return pltpu.make_async_copy(out_ref.at[:, rows], out_hbm.at[:, rows], out_sems.at[i])

    for i in range(3):
        arrival(i).start()

    def stage(src, in_lo, fraction, final):
        fields = 7 if in_lo == 0 else 6
        in_hi = height - 1 - in_lo
        lo, hi = in_lo + 1, in_hi - 1
        count = hi - lo + 1

        def get(f, r):
            return [src[d, r * fields + f] for d in range(chunks)]

        def terrain(r):
            return [x_ref[d, r * 7 + 6] for d in range(chunks)]

        def corners(r, carry):
            rn = jnp.minimum(r + 1, in_hi)
            rs = jnp.maximum(r - 1, in_lo)
            c_half, cn_half = coef[0, r] * dy_inv, coef[0, rn] * dy_inv
            e_inv, sine = coef[2, r], coef[3, r]
            h0, h1, ground = get(0, r), get(1, r), terrain(r)
            base = [a + b for a, b in zip(h1, ground)]
            for k in range(2):
                u, v = get(2 + k, r), get(4 + k, r)
                uw, ve = west(u), east(v)
                un, vs = get(2 + k, rn), get(4 + k, rs)
                for d in range(chunks):
                    at = (r * 2 + k) * chunks + d
                    uu_ref[at] = u[d] + uw[d]
                    vv_ref[at] = v[d] + ve[d]
                    kin = 0.25 * (u[d] * u[d] + uw[d] * uw[d] + (v[d] * v[d] + vs[d] * vs[d]))
                    e_ref[at] = kin + (base[d] + (h0[d] if k == 0 else DENSITY_RATIO * h0[d]))
                    curl = (ve[d] - v[d]) - (un[d] * cn_half - u[d] * c_half)
                    z_ref[at] = sine + curl * e_inv
            return carry

        if in_lo == 0:
            for i in range(3):
                arrival(i).wait()
                first, last = cuts_in[i] - 1, cuts_in[i + 1] - 1
                lax.fori_loop(max(first, 0), height if i == 2 else last, corners, 0)
        else:
            lax.fori_loop(in_lo, in_hi + 1, corners, 0)

        def tendencies(r, carry):
            c_inv = coef[1, r]
            fn, fs = coef[4, r] * (0.5 * dy_inv), coef[4, r - 1] * (0.5 * dy_inv)
            live = coef[5, r]
            for k in range(2):

                def face(ref, row):
                    return [ref[(row * 2 + k) * chunks + d] for d in range(chunks)]

                def put(f, d, value):
                    start = (d * TILE_ROWS + (r - lo) * 6 + f) * SUB
                    t_ref[pl.ds(pl.multiple_of(start, SUB), SUB), :] = value

                h, hn, hs = get(k, r), get(k, r + 1), get(k, r - 1)
                u, v, vs = get(2 + k, r), get(4 + k, r), get(4 + k, r - 1)
                he = east(h)
                fx = [0.5 * (h[d] + he[d]) * u[d] for d in range(chunks)]
                fxw = west(fx)
                for d in range(chunks):
                    north = (h[d] + hn[d]) * (v[d] * fn) - (h[d] + hs[d]) * (vs[d] * fs)
                    put(k, d, ((fxw[d] - fx[d]) - north) * c_inv)
                z, zs, ec = face(z_ref, r), face(z_ref, r - 1), face(e_ref, r)
                vv, vvs = face(vv_ref, r), face(vv_ref, r - 1)
                ee = east(ec)
                for d in range(chunks):
                    turn = (0.125 * (z[d] + zs[d])) * (vv[d] + vvs[d])
                    put(2 + k, d, turn - (ee[d] - ec[d]) * c_inv)
                en, uu, uun = face(e_ref, r + 1), face(uu_ref, r), face(uu_ref, r + 1)
                zw = west(z)
                for d in range(chunks):
                    turn = (0.125 * (z[d] + zw[d])) * (uu[d] + uun[d])
                    put(4 + k, d, live * (dy_inv * (ec[d] - en[d]) - turn))
            return carry

        lax.fori_loop(lo, hi + 1, tendencies, 0)

        def circle_filter(p, carry):
            wave = lax.broadcasted_iota(jnp.int32, (PAIR, 2 * LANES), 1)
            wave = RADIX * jnp.where(wave >= LANES, wave - LANES, wave)

            def place(unit, a, half):
                d, s = a // SUB, a % SUB
                start = (d * TILE_ROWS + (p * UNITS + unit) * PAIR + half * SUB) * SUB + s
                return pl.ds(start, SUB, stride=SUB)

            def cut_of(unit):
                at = pl.multiple_of((p * UNITS + unit) * PAIR, PAIR)
                return cut_ref[in_lo, pl.ds(at, PAIR), :]

            def analyse(unit, half):
                re, im = real_fft([t_ref[place(unit, a, half), :] for a in range(RADIX)])
                for k in range(HALF + 1):
                    c, s = twc_ref[k : k + 1, :], tws_ref[k : k + 1, :]
                    if k == 0:
                        yr, yi = re[k], jnp.zeros_like(re[k])
                    elif im[k] is None:
                        yr, yi = re[k] * c, -(re[k] * s)
                    else:
                        yr, yi = re[k] * c + im[k] * s, im[k] * c - re[k] * s
                    at = pl.ds((k * 2 + half) * SUB, SUB)
                    y_refs[unit][at, 0:LANES] = yr
                    y_refs[unit][at, LANES : 2 * LANES] = yi

            def product(y, whi, wlo):
                n = y.shape[0]
                hi_part = y.astype(jnp.bfloat16)
                lo_part = (y - hi_part.astype(jnp.float32)).astype(jnp.bfloat16)
                dot = functools.partial(jnp.dot, preferred_element_type=jnp.float32)
                both = dot(jnp.concatenate([hi_part, lo_part], axis=0), whi)
                return both[:n] + both[n:] + dot(hi_part, wlo)

            def mask(unit, start):
                cut = cut_of(unit)
                cut2 = jnp.concatenate([cut, cut], axis=1)
                rows = slice(start * PAIR, (start + BLOCK) * PAIR)
                spec = product(y_refs[unit][rows, :], wfh_ref[...], wfl_ref[...])
                keep = []
                for k in range(start, start + BLOCK):
                    folded = jnp.minimum(wave + k, RADIX * LANES - k - wave)
                    keep.append(folded < cut2)
                spec = jnp.where(jnp.concatenate(keep, axis=0), spec, 0.0)
                y_refs[unit][rows, :] = product(spec, wbh_ref[...], wbl_ref[...])

            def synthesise(unit, half):
                re, im = [], []
                for k in range(HALF + 1):
                    c, s = twc_ref[k : k + 1, :], tws_ref[k : k + 1, :]
                    at = pl.ds((k * 2 + half) * SUB, SUB)
                    yr = y_refs[unit][at, 0:LANES]
                    if k == 0:
                        re.append(yr)
                        im.append(None)
                        continue
                    yi = y_refs[unit][at, LANES : 2 * LANES]
                    re.append(yr * c - yi * s)
                    im.append(None if k == HALF else yr * s + yi * c)
                circles = real_ifft(re, im)
                polar = cut_of(unit)[half * SUB : (half + 1) * SUB] < UNCUT
                for a in range(RADIX):
                    at = place(unit, a, half)
                    t_ref[at, :] = jnp.where(polar, circles[a], t_ref[at, :])

            for unit in range(UNITS):
                for half in range(2):
                    analyse(unit, half)
            for start in range(0, HALF + 1, BLOCK):
                for unit in range(UNITS):
                    mask(unit, start)
            for unit in range(UNITS):
                for half in range(2):
                    synthesise(unit, half)
            return carry

        @pl.when(flags[in_lo] > 0)
        def _():
            lax.fori_loop(0, -(-6 * count // (PAIR * UNITS)), circle_filter, 0)

        def update(r, carry):
            inside = coef[6, r]
            for f in range(6):
                for d in range(chunks):
                    start = (d * TILE_ROWS + (r - lo) * 6 + f) * SUB
                    change = t_ref[pl.ds(pl.multiple_of(start, SUB), SUB), :]
                    value = inside * (x_ref[d, r * 7 + f] + (fraction * step_size) * change)
                    if final:
                        out_ref[d, (r - HALO) * 6 + f] = value
                    else:
                        s_ref[d, r * 6 + f] = value
            return carry

        if final:
            for i in range(2):
                lax.fori_loop(lo + i * (own // 2), lo + (i + 1) * (own // 2), update, 0)
                departure(i).start()
            for i in range(2):
                departure(i).wait()
        else:
            lax.fori_loop(lo, hi + 1, update, 0)

    stage(x_ref, 0, 1.0 / 3.0, False)
    stage(s_ref, 1, 0.5, False)
    stage(s_ref, 2, 1.0, True)


def row_tables(cutoffs, row_start, height, total_rows, polar):
    row_ids = row_start - HALO + jnp.arange(height, dtype=jnp.int32)
    spacing = math.pi / total_rows
    centre_lat = -0.5 * math.pi + (row_ids.astype(jnp.float32) + 0.5) * spacing
    face_lat = -0.5 * math.pi + (row_ids.astype(jnp.float32) + 1.0) * spacing
    inside = jnp.where((row_ids >= 0) & (row_ids < total_rows), 1.0, 0.0).astype(jnp.float32)
    live = jnp.where((row_ids >= 0) & (row_ids < total_rows - 1), 1.0, 0.0).astype(jnp.float32)
    centre_cos = jnp.cos(centre_lat)
    face_cos = jnp.cos(face_lat) * live
    face_inverse = live / (face_cos + (1.0 - live))
    coef = jnp.stack(
        [centre_cos, 1.0 / centre_cos, face_inverse, jnp.sin(face_lat), face_cos, live, inside]
    )
    capped = ((row_ids >= 0) & (row_ids < polar)) | (
        (row_ids >= total_rows - polar) & (row_ids < total_rows)
    )
    position = jnp.where(row_ids < polar, row_ids, row_ids - (total_rows - 2 * polar))
    table_ids = jnp.arange(2 * polar, dtype=jnp.int32)
    cut = jnp.sum(
        jnp.where(position[:, None] == table_ids[None, :], cutoffs[None, :], 0), axis=1, dtype=jnp.int32
    )
    cut = jnp.where(capped, cut, UNCUT)
    stages = []
    for in_lo in range(3):
        rows = jnp.repeat(cut[in_lo + 1 : height - 1 - in_lo], 6)
        stages.append(jnp.pad(rows, (0, TILE_ROWS - rows.shape[0]), constant_values=UNCUT))
    cuts = jnp.stack(stages)
    flags = jnp.any(cuts < UNCUT, axis=1).astype(jnp.int32)
    return coef, flags, jnp.broadcast_to(cuts[:, :, None], (3, TILE_ROWS, LANES))


def body(thickness, winds, terrain, cutoffs):
    row_count, col_count = thickness.shape[1], thickness.shape[2]
    bands, sectors = lax.axis_size("lat"), lax.axis_size("lon")
    total_rows, circle = row_count * bands, col_count * sectors
    polar = (total_rows + 2) // 6
    own = row_count // sectors
    height = own + 2 * HALO
    merid_step = circle / (2.0 * total_rows)
    step_size = 0.1 * min(1.0, merid_step)
    lat = lax.axis_index("lat")
    flat = winds.reshape(4, row_count, col_count)

    vmem = pl.BlockSpec(memory_space=pltpu.VMEM)
    smem = pl.BlockSpec(memory_space=pltpu.SMEM)
    hbm = pl.BlockSpec(memory_space=pltpu.HBM)
    rim = jax.ShapeDtypeStruct((HALO * 7 * SUB, LANES), jnp.float32)
    tail, head = pl.pallas_call(
        edge_kernel,
        out_shape=(rim, rim),
        in_specs=[hbm] * 3,
        out_specs=(vmem, vmem),
        scratch_shapes=[
            pltpu.VMEM((2, 7, SUB, col_count), jnp.float32),
            pltpu.SemaphoreType.DMA((2, 7)),
        ],
        name="edge",
    )(thickness, flat, terrain)
    south = lax.ppermute(tail, "lat", [(i, i + 1) for i in range(bands - 1)])
    north = lax.ppermute(head, "lat", [(i + 1, i) for i in range(bands - 1)])

    piece = (sectors, height * 7 * SUB, LANES)
    packed = pl.pallas_call(
        functools.partial(pack_kernel, bands),
        out_shape=jax.ShapeDtypeStruct(piece, jnp.float32),
        in_specs=[smem] + [vmem] * 3,
        out_specs=hbm,
        scratch_shapes=[pltpu.VMEM(piece, jnp.float32), pltpu.SemaphoreType.DMA((sectors,))],
        compiler_params=pltpu.CompilerParams(vmem_limit_bytes=16 << 20),
        cost_estimate=pl.CostEstimate(flops=0, bytes_accessed=16 << 20, transcendentals=0),
        name="pack",
    )(lat.reshape(1).astype(jnp.int32), thickness, flat, terrain)
    packed = pl.pallas_call(
        rim_kernel,
        out_shape=jax.ShapeDtypeStruct(piece, jnp.float32),
        in_specs=[vmem, vmem, hbm],
        out_specs=hbm,
        scratch_shapes=[pltpu.SemaphoreType.DMA((2,))],
        input_output_aliases={2: 0},
        name="rim",
    )(south, north, packed)
    circles = lax.all_to_all(packed, "lon", 0, 0)

    row_start = lat * row_count + lax.axis_index("lon") * own
    coef, flags, cuts = row_tables(cutoffs, row_start, height, total_rows, polar)
    tables = [jnp.asarray(t) for t in filter_tables()]
    stepped = pl.pallas_call(
        functools.partial(step_kernel, merid_step, step_size),
        out_shape=jax.ShapeDtypeStruct((sectors, 6 * own, SUB, LANES), jnp.float32),
        in_specs=[smem, smem, hbm] + [vmem] * 7,
        out_specs=hbm,
        scratch_shapes=[
            pltpu.VMEM((sectors, 7 * height, SUB, LANES), jnp.float32),
            pltpu.VMEM((sectors, 6 * height, SUB, LANES), jnp.float32),
            pltpu.VMEM((sectors, 6 * own, SUB, LANES), jnp.float32),
            pltpu.VMEM((sectors * TILE_ROWS * SUB, LANES), jnp.float32),
            pltpu.SemaphoreType.DMA((3,)),
            pltpu.SemaphoreType.DMA((2,)),
        ]
        + [pltpu.VMEM((height * 2 * sectors, SUB, LANES), jnp.float32)] * 4
        + [pltpu.VMEM(((HALF + 1) * PAIR, 2 * LANES), jnp.float32)] * UNITS,
        compiler_params=pltpu.CompilerParams(vmem_limit_bytes=56 << 20),
        name="step",
    )(coef, flags, circles.reshape(sectors, 7 * height, SUB, LANES), cuts, *tables)
    returned = lax.all_to_all(stepped.reshape(sectors, 6 * own * SUB, LANES), "lon", 0, 0)
    new_thickness, new_winds = pl.pallas_call(
        unpack_kernel,
        out_shape=(
            jax.ShapeDtypeStruct(thickness.shape, jnp.float32),
            jax.ShapeDtypeStruct(flat.shape, jnp.float32),
        ),
        in_specs=[vmem],
        out_specs=(vmem, vmem),
        compiler_params=pltpu.CompilerParams(vmem_limit_bytes=40 << 20),
        name="unpack",
    )(returned)
    return new_thickness, new_winds.reshape(winds.shape)


def solution(mesh):
    in_specs = (P(None, "lat", "lon"), P(None, None, "lat", "lon"), P("lat", "lon"), P())
    out_specs = (P(None, "lat", "lon"), P(None, None, "lat", "lon"))
    return jax.shard_map(body, mesh=mesh, in_specs=in_specs, out_specs=out_specs, check_vma=False)
```

time: 192 us -> 171 us (0.89)
  Pallas kernels: 64.2 us -> 52.6 us
  waiting for transfers between devices: 60 us -> 55.7 us
  local copies, waits for them, and re-layouts: 10.9 us -> 6.72 us
    pallas_call x1, Pallas kernels: 61 us -> 44.2 us  [body(): pl.pallas_call(functools.partial(step_kernel, merid_step, step_size), out...]
    ppermute x1, waiting for transfers between devices: 3.98 us -> 0.01 us  [body(): north = lax.ppermute(head, 'lat', [(i + 1, i) for i in range(bands - 1)])]
    pallas_call x0 -> x2, Pallas kernels: none -> 3.52 us  [the longest x1 1.9 us: body(): pl.pallas_call(edge_kernel, out_shape=(rim, rim), in_specs=[hbm] * 3, out...]
    unnamed x10 -> x14, local copies, waits for them, and re-layouts: 6.13 us -> 4.59 us
  transfers between devices with their start and end apart: 3 -> 3, of which waited for: 3 -> 1; matrix products, arithmetic and copies ran while one was open for 1% -> 1% of each run, Pallas kernels for 0% -> 1%
where the time goes in v2:
time: 171 us; the launch traced here: 170 us
  waiting for transfers between devices  55.7 us (33%)
  Pallas kernels  52.6 us (31%)
  blocking collectives  42.3 us (25%)
  starting transfers between devices  11.2 us (7%)
  local copies, waits for them, and re-layouts  6.72 us (4%)
    all_to_all x1, waiting for transfers between devices, body(): circles = lax.all_to_all(packed, 'lon', 0, 0)  55.7 us
    pallas_call x1, Pallas kernels, body(): pl.pallas_call(functools.partial(step_kernel, merid_step, step_size), out...  44.2 us
    all_to_all x1, blocking collectives, body(): lax.all_to_all(stepped.reshape(sectors, 6 * own * SUB, LANES), 'lon', 0, 0)  42.3 us
    all_to_all x1, starting transfers between devices, body(): circles = lax.all_to_all(packed, 'lon', 0, 0)  5.48 us
    unnamed x14, local copies, waits for them, and re-layouts  4.59 us
    ppermute x1, starting transfers between devices, body(): south = lax.ppermute(tail, 'lat', [(i, i + 1) for i in range(bands - 1)])  4.38 us
  transfers between devices with their start and end apart: 3, of which 1 were waited for; matrix products, arithmetic and copies ran while one was open for 1% of the time, Pallas kernels for 1%

profile of v2, /device:TPU:1, one launch (start us, length us, event | category | flops | bytes accessed | tf_op | source)
XLA Modules:
  0.0 170.3 jit_solution(1367322953949123546)
XLA Ops:
  0.6 1.9 %edge.1 = (f32[168,128]{1,0:T(8,128)}, f32[168,128]{1,0:T(8,128)}) custom-call(f32[2,128,1024]{2,1,0:T(8,128)} %th_ref.3, f32[4,128,1024]{2,1,0:T(8,128)} %bitcast.11, f32[128,1024]{1,0:T(8,128)} %te_ref.3), custom_call_target="tpu_custom_call" | custom-call | tf_op jit(solution)/shard_map/edge/pallas_call | solution.py:489
  2.6 4.4 %collective-permute-start = (f32[168,128]{1,0:T(8,128)}, f32[168,128]{1,0:T(8,128)S(1)}, u32[]{:S(2)}, u32[]{:S(2)}) collective-permute-start(f32[168,128]{1,0:T(8,128)} %get-tuple-element.6), channel_id=1, source_target_pairs={{0,8},{8,16},{16,24},{24,32},{32,40},{40,48},{48,56},{56,64},{64,7... | collective-permute-start | bytes 258056 | tf_op jit(solution)/shard_map/ppermute | solution.py:500
  6.9 1.3 collective-permute-start.1
  8.3 0.0 copy-start.3
  8.3 1.0 copy-done.3
  9.3 2.2 %pack.1.packed_ref = f32[8,1232,128]{2,1,0:T(8,128)S(1)} custom-call(s32[1]{0:T(128)} %bitcast.4.lat_ref, f32[2,128,1024]{2,1,0:T(8,128)S(1)} %copy-done.2, f32[4,128,1024]{2,1,0:T(8,128)S(1)} %bitcast.12, f32[128,1024]{1,0:T(8,128)S(1)} %copy-done.3), custom_call_target="tpu_custom_call" | custom-call | bytes 16777216 | tf_op jit(solution)/shard_map/pack/pallas_call | solution.py:504
  11.6 2.3 %copy-done = f32[8,1232,128]{2,1,0:T(8,128)} copy-done((f32[8,1232,128]{2,1,0:T(8,128)}, f32[8,1232,128]{2,1,0:T(8,128)S(1)}, u32[]{:S(2)}) %copy-start) | copy-done | bytes 5046296
  13.8 0.0 collective-permute-done.south_ref
  13.9 0.6 copy-done.4
  14.5 0.6 copy-done.5
  15.1 1.6 rim.1
  16.8 0.0 copy-start.6
  16.8 5.5 %all-to-all-start = ((f32[8,1232,128]{2,1,0:T(8,128)}), f32[8,1232,128]{2,1,0:T(8,128)}, u32[]{:S(2)}, u32[]{:S(2)}) async-start(f32[8,1232,128]{2,1,0:T(8,128)} %rim.1), calls=%async_computation | async-start | bytes 10092544 | tf_op jit(solution)/shard_map/all_to_all | solution.py:523
  22.3 0.2 select_reduce_fusion
  22.5 0.1 slice.11
  22.5 0.1 slice.10
  22.6 0.1 slice.9
  22.7 0.1 broadcast_in_dim.48
  22.7 0.1 reshape.118
  22.8 0.1 broadcast_in_dim.47
  22.9 0.1 reshape.117
  23.0 0.1 broadcast_in_dim.46
  23.1 0.1 reshape.116
  23.2 0.1 compare_reduce_fusion
  23.3 0.5 convert_element_type.31.flags
  23.9 0.1 add_divide_fusion
  24.0 0.6 stack.10.coef
  24.6 55.7 %all-to-all-done = f32[8,1232,128]{2,1,0:T(8,128)} async-done(((f32[8,1232,128]{2,1,0:T(8,128)}), f32[8,1232,128]{2,1,0:T(8,128)}, u32[]{:S(2)}, u32[]{:S(2)}) %all-to-all-start) | async-done | bytes 5046304 | tf_op jit(solution)/shard_map/all_to_all | solution.py:523
  80.3 0.8 broadcast_in_dim.49.cut_ref
  81.1 44.2 %step.1 = f32[8,96,8,128]{3,2,1,0:T(8,128)} custom-call(f32[7,22]{1,0:T(8,128)} %stack.10.coef, s32[3]{0:T(128)} %convert_element_type.31.flags, f32[8,154,8,128]{3,2,1,0:T(8,128)} %bitcast.5.x_hbm, s32[3,128,128]{2,1,0:T(8,128)} %broadcast_in_dim.49.cut_ref, bf16[256,256]{1,0:T(8,128)(2,1)} %constant.58.clone.wfh_ref, ...), custom_call_target="tpu_custom_call" | custom-call | tf_op jit(solution)/shard_map/step/pallas_call | solution.py:528
  125.3 42.3 %all_to_all.10.in_ref = f32[8,768,128]{2,1,0:T(8,128)S(1)} all-to-all(f32[8,768,128]{2,1,0:T(8,128)} %bitcast.13), channel_id=1, replica_groups=mesh['lat'=16,'lon'=8] {'lon'}, dimensions={0} | all-to-all | bytes 6291456 | tf_op jit(solution)/shard_map/all_to_all | solution.py:546
  167.6 2.7 %unpack.1 = (f32[2,128,1024]{2,1,0:T(8,128)}, f32[4,128,1024]{2,1,0:T(8,128)}) custom-call(f32[8,768,128]{2,1,0:T(8,128)S(1)} %all_to_all.10.in_ref), custom_call_target="tpu_custom_call" | custom-call | tf_op jit(solution)/shard_map/unpack/pallas_call | solution.py:547
  (17 shorter events, 0.2 us)
Async XLA Ops:
  0.6 7.6 %copy-start.2 = (f32[2,128,1024]{2,1,0:T(8,128)S(1)}, f32[2,128,1024]{2,1,0:T(8,128)}, u32[]{:S(2)}) copy-start(f32[2,128,1024]{2,1,0:T(8,128)} %th_ref.3) | copy-start | bytes 3145732
  0.6 7.6 %copy-start.1 = (f32[2,2,128,1024]{3,2,1,0:T(8,128)S(1)}, f32[2,2,128,1024]{3,2,1,0:T(8,128)}, u32[]{:S(2)}) copy-start(f32[2,2,128,1024]{3,2,1,0:T(8,128)} %param.11) | copy-start | bytes 6291460
  2.6 11.3 %collective-permute-start = (f32[168,128]{1,0:T(8,128)}, f32[168,128]{1,0:T(8,128)S(1)}, u32[]{:S(2)}, u32[]{:S(2)}) collective-permute-start(f32[168,128]{1,0:T(8,128)} %get-tuple-element.6), channel_id=1, source_target_pairs={{0,8},{8,16},{16,24},{24,32},{32,40},{40,48},{48,56},{56,64},{64,7... | collective-permute-start | bytes 258056 | tf_op jit(solution)/shard_map/ppermute | solution.py:500
  6.9 6.9 %collective-permute-start.1 = (f32[168,128]{1,0:T(8,128)}, f32[168,128]{1,0:T(8,128)S(1)}, u32[]{:S(2)}, u32[]{:S(2)}) collective-permute-start(f32[168,128]{1,0:T(8,128)} %get-tuple-element.7), channel_id=1, source_target_pairs={{8,0},{16,8},{24,16},{32,24},{40,32},{48,40},{56,48},{64,56},{72,6... | collective-permute-start | bytes 258056 | tf_op jit(solution)/shard_map/ppermute | solution.py:501
  8.3 1.0 copy-start.3
  11.6 2.3 %copy-start = (f32[8,1232,128]{2,1,0:T(8,128)}, f32[8,1232,128]{2,1,0:T(8,128)S(1)}, u32[]{:S(2)}) copy-start(f32[8,1232,128]{2,1,0:T(8,128)S(1)} %pack.1.packed_ref) | copy-start | bytes 15138820
  13.8 0.6 copy-start.4
  14.5 0.6 copy-start.5
  16.8 5.5 %copy-start.6 = (s32[682]{0:T(1024)S(1)}, s32[682]{0:T(1024)}, u32[]{:S(2)}) copy-start(s32[682]{0:T(1024)} %param.13) | copy-start | bytes 8188
  16.8 63.5 %all-to-all-start = ((f32[8,1232,128]{2,1,0:T(8,128)}), f32[8,1232,128]{2,1,0:T(8,128)}, u32[]{:S(2)}, u32[]{:S(2)}) async-start(f32[8,1232,128]{2,1,0:T(8,128)} %rim.1), calls=%async_computation | async-start | bytes 10092544 | tf_op jit(solution)/shard_map/all_to_all | solution.py:523

commit v3 on v2

--- a/solution.py
+++ b/solution.py
@@ -16,13 +16,12 @@
 LANES = 128
 RADIX = 64
 HALF = RADIX // 2
-SPEC_BLOCKS = HALF + 2
 UNCUT = 1 << 20
-TILE_ROWS = 128
+TILE_ROWS = 64
 PAIR = 16
-UNITS = 2
+UNITS = 3
 BLOCK = 11
-COEFS = 7
+CUT = 12
 
 
 def twisted(real, imag, k, n):
@@ -127,10 +126,20 @@
                 ]
 
 
-def pack_kernel(bands, lat_ref, th_ref, wi_ref, te_ref, out_ref, piece_ref, sems):
-    groups = out_ref.shape[0]
-    height = out_ref.shape[1] // (7 * SUB)
+def pack_kernel(bands, lat_ref, th_ref, wi_ref, te_ref, a_hbm, b_hbm, piece_ref, sems):
+    groups = piece_ref.shape[0]
+    height = piece_ref.shape[1] // (7 * SUB)
     own = height - 2 * HALO
+    split = CUT * 7 * SUB
+
+    def departures(g):
+        a_first = 0 if g > 0 else HALO * 7 * SUB
+        b_last = (height if g < groups - 1 else HALO + own) * 7 * SUB
+        a, b = pl.ds(a_first, split - a_first), pl.ds(split, b_last - split)
+        return (
+            pltpu.make_async_copy(piece_ref.at[g, a], a_hbm.at[g, a], sems.at[0, g]),
+            pltpu.make_async_copy(piece_ref.at[g, b], b_hbm.at[g, pl.ds(0, b_last - split)], sems.at[1, g]),
+        )
 
     for g in range(groups):
         for f in range(7):
@@ -156,70 +165,58 @@
                     at = pl.ds(((HALO + own - 1) * 7 + f) * SUB, SUB)
                     piece_ref[g, at, :] = jnp.zeros((SUB, LANES), jnp.float32)
 
-        first = 0 if g > 0 else HALO * 7 * SUB
-        last = (height if g < groups - 1 else HALO + own) * 7 * SUB
-        span = pl.ds(first, last - first)
-        pltpu.make_async_copy(piece_ref.at[g, span], out_ref.at[g, span], sems.at[g]).start()
+        for copy in departures(g):
+            copy.start()
     for g in range(groups):
-        first = 0 if g > 0 else HALO * 7 * SUB
-        last = (height if g < groups - 1 else HALO + own) * 7 * SUB
-        span = pl.ds(first, last - first)
-        pltpu.make_async_copy(piece_ref.at[g, span], out_ref.at[g, span], sems.at[g]).wait()
-
-
-def rim_kernel(south_ref, north_ref, packed_ref, out_ref, sems):
-    groups, length = out_ref.shape[0], out_ref.shape[1]
-    rim = HALO * 7 * SUB
-    low = pltpu.make_async_copy(south_ref, out_ref.at[0, pl.ds(0, rim)], sems.at[0])
-    high = pltpu.make_async_copy(north_ref, out_ref.at[groups - 1, pl.ds(length - rim, rim)], sems.at[1])
-    low.start()
-    high.start()
-    low.wait()
-    high.wait()
-
-
-def unpack_kernel(in_ref, th_ref, wi_ref):
-    groups = in_ref.shape[0]
-    own = in_ref.shape[1] // (6 * SUB)
+        for copy in departures(g):
+            copy.wait()
+
+
+def rim_kernel(group, start, rim_ref, packed_ref, out_ref, sem):
+    copy = pltpu.make_async_copy(rim_ref, out_ref.at[group, pl.ds(start, rim_ref.shape[0])], sem)
+    copy.start()
+    copy.wait()
+
+
+def unpack_kernel(a_ref, b_ref, th_ref, wi_ref):
+    groups = a_ref.shape[0]
+    spans = [(r.shape[1] // (6 * SUB), r) for r in (a_ref, b_ref)]
+    own = spans[0][0] + spans[1][0]
     for f in range(6):
         dst = th_ref.at[f] if f < 2 else wi_ref.at[f - 2]
         for g in range(groups):
-            for m in range(own // SUB):
-                for s in range(SUB):
-                    dst[pl.ds(g * own + m * SUB, SUB), s * LANES : (s + 1) * LANES] = in_ref[
-                        g, pl.ds((m * SUB * 6 + f) * SUB + s, SUB, stride=6 * SUB), :
-                    ]
-
-
-def step_kernel(
-    merid_step,
-    step_size,
-    coef,
-    flags,
-    x_hbm,
-    cut_ref,
-    wfh_ref,
-    wfl_ref,
-    wbh_ref,
-    wbl_ref,
-    twc_ref,
-    tws_ref,
-    out_hbm,
-    x_ref,
-    s_ref,
-    out_ref,
-    t_ref,
-    in_sems,
-    out_sems,
-    e_ref,
-    z_ref,
-    uu_ref,
-    vv_ref,
-    *y_refs,
-):
+            row = g * own
+            for rows, src in spans:
+                for first in range(0, rows, SUB):
+                    count = min(SUB, rows - first)
+                    for s in range(SUB):
+                        dst[pl.ds(row + first, count), s * LANES : (s + 1) * LANES] = src[
+                            g, pl.ds((first * 6 + f) * SUB + s, count, stride=6 * SUB), :
+                        ]
+                row += rows
+
+
+def stage_rows(height, upper):
+    if upper:
+        return [(CUT - 1 - k, height - 2 - k) for k in range(3)]
+    return [(1 + k, CUT - 2 - k) for k in range(3)]
+
+
+def step_kernel(upper, height, merid_step, step_size, coef, flags, *refs):
+    if upper:
+        x_low, x_high, s1_hbm, s2_hbm, *refs = refs
+    else:
+        x_low, *refs = refs
+    cut_ref, wfh_ref, wfl_ref, wbh_ref, wbl_ref, twc_ref, tws_ref, *refs = refs
+    out_hbm, *refs = refs
+    if not upper:
+        s1_hbm, s2_hbm, *refs = refs
+    x_ref, s1_ref, s2_ref, out_ref, t_ref, in_sems, out_sems, edge_sems, *refs = refs
+    e_ref, z_ref, uu_ref, vv_ref, *y_refs = refs
     chunks = x_ref.shape[0]
-    height = x_ref.shape[1] // 7
-    own = height - 2 * HALO
+    ranges = stage_rows(height, upper)
+    out_lo, out_hi = ranges[2]
+    out_rows = out_hi - out_lo + 1
     lane = lax.broadcasted_iota(jnp.int32, (SUB, LANES), 1)
     sub = lax.broadcasted_iota(jnp.int32, (SUB, LANES), 0)
     last_lane, first_lane = lane == LANES - 1, lane == 0
@@ -241,23 +238,44 @@
             jnp.where(first_lane, jnp.where(first_sub, r[d - 1], r[d]), y[d]) for d in range(chunks)
         ]
 
-    cuts_in = (0, height // 3, 2 * height // 3, height)
-
-    def arrival(i):
-        rows = pl.ds(cuts_in[i] * 7, (cuts_in[i + 1] - cuts_in[i]) * 7)
-        return pltpu.make_async_copy(x_hbm.at[:, rows], x_ref.at[:, rows], in_sems.at[i])
+    def x_copy(i, src, src_row, row, count):
+        return pltpu.make_async_copy(
+            src.at[:, pl.ds(src_row * 7, count * 7)], x_ref.at[:, pl.ds(row * 7, count * 7)], in_sems.at[i]
+        )
+
+    if upper:
+        half = (height - CUT) // 2
+        arrivals = [
+            x_copy(0, x_low, CUT - HALO, CUT - HALO, HALO),
+            x_copy(1, x_high, 0, CUT, half),
+            x_copy(2, x_high, half, CUT + half, height - CUT - half),
+        ]
+        in_edges = (CUT, CUT + half, height)
+    else:
+        arrivals = [x_copy(i, x_low, i * CUT // 3, i * CUT // 3, CUT // 3) for i in range(3)]
+        in_edges = tuple((i + 1) * CUT // 3 for i in range(3))
 
     def departure(i):
-        rows = pl.ds(i * (own // 2) * 6, (own // 2) * 6)
+        rows = pl.ds(i * (out_rows // 2) * 6, (out_rows // 2) * 6)
         return pltpu.make_async_copy(out_ref.at[:, rows], out_hbm.at[:, rows], out_sems.at[i])
 
-    for i in range(3):
-        arrival(i).start()
-
-    def stage(src, in_lo, fraction, final):
-        fields = 7 if in_lo == 0 else 6
-        in_hi = height - 1 - in_lo
-        lo, hi = in_lo + 1, in_hi - 1
+    def edge(i):
+        hbm, ref = ((s1_hbm, s1_ref), (s2_hbm, s2_ref))[i]
+        ref = ref.at[:, pl.ds((CUT - 3 - i) * 6, 12)]
+        src, dst = (hbm, ref) if upper else (ref, hbm)
+        return pltpu.make_async_copy(src, dst, edge_sems.at[i])
+
+    for copy in arrivals:
+        copy.start()
+    if upper:
+        edge(0).start()
+        edge(1).start()
+
+    def stage(src, dst, index, fraction):
+        fields = 7 if index == 0 else 6
+        final = index == 2
+        lo, hi = ranges[index]
+        in_lo, in_hi = lo - 1, hi + 1
         count = hi - lo + 1
 
         def get(f, r):
@@ -287,12 +305,16 @@
                     z_ref[at] = sine + curl * e_inv
             return carry
 
-        if in_lo == 0:
+        if index == 0:
+            first = in_lo
             for i in range(3):
-                arrival(i).wait()
-                first, last = cuts_in[i] - 1, cuts_in[i + 1] - 1
-                lax.fori_loop(max(first, 0), height if i == 2 else last, corners, 0)
+                arrivals[i].wait()
+                last = in_edges[i] - 1 if i < 2 else in_edges[i]
+                lax.fori_loop(first, last, corners, 0)
+                first = last
         else:
+            if upper:
+                edge(index - 1).wait()
             lax.fori_loop(in_lo, in_hi + 1, corners, 0)
 
         def tendencies(r, carry):
@@ -331,18 +353,21 @@
 
         lax.fori_loop(lo, hi + 1, tendencies, 0)
 
+        total = -(-6 * count // PAIR)
+        units = 3 if total % 3 == 0 else 2
+
         def circle_filter(p, carry):
             wave = lax.broadcasted_iota(jnp.int32, (PAIR, 2 * LANES), 1)
             wave = RADIX * jnp.where(wave >= LANES, wave - LANES, wave)
 
             def place(unit, a, half):
                 d, s = a // SUB, a % SUB
-                start = (d * TILE_ROWS + (p * UNITS + unit) * PAIR + half * SUB) * SUB + s
+                start = (d * TILE_ROWS + (p * units + unit) * PAIR + half * SUB) * SUB + s
                 return pl.ds(start, SUB, stride=SUB)
 
             def cut_of(unit):
-                at = pl.multiple_of((p * UNITS + unit) * PAIR, PAIR)
-                return cut_ref[in_lo, pl.ds(at, PAIR), :]
+                at = pl.multiple_of((p * units + unit) * PAIR, PAIR)
+                return cut_ref[index, pl.ds(at, PAIR), :]
 
             def analyse(unit, half):
                 re, im = real_fft([t_ref[place(unit, a, half), :] for a in range(RADIX)])
@@ -397,20 +422,20 @@
                     at = place(unit, a, half)
                     t_ref[at, :] = jnp.where(polar, circles[a], t_ref[at, :])
 
-            for unit in range(UNITS):
+            for unit in range(units):
                 for half in range(2):
                     analyse(unit, half)
             for start in range(0, HALF + 1, BLOCK):
-                for unit in range(UNITS):
+                for unit in range(units):
                     mask(unit, start)
-            for unit in range(UNITS):
+            for unit in range(units):
                 for half in range(2):
                     synthesise(unit, half)
             return carry
 
-        @pl.when(flags[in_lo] > 0)
+        @pl.when(flags[index] > 0)
         def _():
-            lax.fori_loop(0, -(-6 * count // (PAIR * UNITS)), circle_filter, 0)
+            lax.fori_loop(0, -(-total // units), circle_filter, 0)
 
         def update(r, carry):
             inside = coef[6, r]
@@ -420,23 +445,27 @@
                     change = t_ref[pl.ds(pl.multiple_of(start, SUB), SUB), :]
                     value = inside * (x_ref[d, r * 7 + f] + (fraction * step_size) * change)
                     if final:
-                        out_ref[d, (r - HALO) * 6 + f] = value
+                        out_ref[d, (r - lo) * 6 + f] = value
                     else:
-                        s_ref[d, r * 6 + f] = value
+                        dst[d, r * 6 + f] = value
             return carry
 
         if final:
             for i in range(2):
-                lax.fori_loop(lo + i * (own // 2), lo + (i + 1) * (own // 2), update, 0)
+                lax.fori_loop(lo + i * (count // 2), lo + (i + 1) * (count // 2), update, 0)
                 departure(i).start()
-            for i in range(2):
-                departure(i).wait()
         else:
             lax.fori_loop(lo, hi + 1, update, 0)
-
-    stage(x_ref, 0, 1.0 / 3.0, False)
-    stage(s_ref, 1, 0.5, False)
-    stage(s_ref, 2, 1.0, True)
+            if not upper:
+                edge(index).start()
+
+    stage(x_ref, s1_ref, 0, 1.0 / 3.0)
+    stage(s1_ref, s2_ref, 1, 0.5)
+    stage(s2_ref, None, 2, 1.0)
+    for i in range(2):
+        departure(i).wait()
+        if not upper:
+            edge(i).wait()
 
 
 def row_tables(cutoffs, row_start, height, total_rows, polar):
@@ -461,13 +490,16 @@
         jnp.where(position[:, None] == table_ids[None, :], cutoffs[None, :], 0), axis=1, dtype=jnp.int32
     )
     cut = jnp.where(capped, cut, UNCUT)
-    stages = []
-    for in_lo in range(3):
-        rows = jnp.repeat(cut[in_lo + 1 : height - 1 - in_lo], 6)
-        stages.append(jnp.pad(rows, (0, TILE_ROWS - rows.shape[0]), constant_values=UNCUT))
-    cuts = jnp.stack(stages)
-    flags = jnp.any(cuts < UNCUT, axis=1).astype(jnp.int32)
-    return coef, flags, jnp.broadcast_to(cuts[:, :, None], (3, TILE_ROWS, LANES))
+    parts = []
+    for upper in (False, True):
+        stages = []
+        for lo, hi in stage_rows(height, upper):
+            rows = jnp.repeat(cut[lo : hi + 1], 6)
+            stages.append(jnp.pad(rows, (0, TILE_ROWS - rows.shape[0]), constant_values=UNCUT))
+        cuts = jnp.stack(stages)
+        flags = jnp.any(cuts < UNCUT, axis=1).astype(jnp.int32)
+        parts.append((flags, jnp.broadcast_to(cuts[:, :, None], (3, TILE_ROWS, LANES))))
+    return coef, parts
 
 
 def body(thickness, winds, terrain, cutoffs):
@@ -500,61 +532,86 @@
     south = lax.ppermute(tail, "lat", [(i, i + 1) for i in range(bands - 1)])
     north = lax.ppermute(head, "lat", [(i + 1, i) for i in range(bands - 1)])
 
-    piece = (sectors, height * 7 * SUB, LANES)
-    packed = pl.pallas_call(
+    def piece(rows, fields):
+        return jax.ShapeDtypeStruct((sectors, rows * fields * SUB, LANES), jnp.float32)
+
+    packed_low, packed_high = pl.pallas_call(
         functools.partial(pack_kernel, bands),
-        out_shape=jax.ShapeDtypeStruct(piece, jnp.float32),
+        out_shape=(piece(CUT, 7), piece(height - CUT, 7)),
         in_specs=[smem] + [vmem] * 3,
-        out_specs=hbm,
-        scratch_shapes=[pltpu.VMEM(piece, jnp.float32), pltpu.SemaphoreType.DMA((sectors,))],
-        compiler_params=pltpu.CompilerParams(vmem_limit_bytes=16 << 20),
-        cost_estimate=pl.CostEstimate(flops=0, bytes_accessed=16 << 20, transcendentals=0),
+        out_specs=(hbm, hbm),
+        scratch_shapes=[
+            pltpu.VMEM(piece(height, 7).shape, jnp.float32),
+            pltpu.SemaphoreType.DMA((2, sectors)),
+        ],
+        compiler_params=pltpu.CompilerParams(vmem_limit_bytes=56 << 20),
+        cost_estimate=pl.CostEstimate(flops=0, bytes_accessed=12 << 20, transcendentals=0),
         name="pack",
     )(lat.reshape(1).astype(jnp.int32), thickness, flat, terrain)
-    packed = pl.pallas_call(
-        rim_kernel,
-        out_shape=jax.ShapeDtypeStruct(piece, jnp.float32),
-        in_specs=[vmem, vmem, hbm],
-        out_specs=hbm,
-        scratch_shapes=[pltpu.SemaphoreType.DMA((2,))],
-        input_output_aliases={2: 0},
-        name="rim",
-    )(south, north, packed)
-    circles = lax.all_to_all(packed, "lon", 0, 0)
+
+    def rimmed(packed, rows, group, start):
+        return pl.pallas_call(
+            functools.partial(rim_kernel, group, start),
+            out_shape=jax.ShapeDtypeStruct(packed.shape, jnp.float32),
+            in_specs=[vmem, hbm],
+            out_specs=hbm,
+            scratch_shapes=[pltpu.SemaphoreType.DMA],
+            input_output_aliases={1: 0},
+            name="rim",
+        )(rows, packed)
+
+    packed_low = rimmed(packed_low, south, 0, 0)
+    packed_high = rimmed(packed_high, north, sectors - 1, (HALO + own - CUT) * 7 * SUB)
+    circles_low = lax.all_to_all(packed_low, "lon", 0, 0)
+    circles_high = lax.all_to_all(packed_high, "lon", 0, 0)
 
     row_start = lat * row_count + lax.axis_index("lon") * own
-    coef, flags, cuts = row_tables(cutoffs, row_start, height, total_rows, polar)
+    coef, parts = row_tables(cutoffs, row_start, height, total_rows, polar)
     tables = [jnp.asarray(t) for t in filter_tables()]
-    stepped = pl.pallas_call(
-        functools.partial(step_kernel, merid_step, step_size),
-        out_shape=jax.ShapeDtypeStruct((sectors, 6 * own, SUB, LANES), jnp.float32),
-        in_specs=[smem, smem, hbm] + [vmem] * 7,
-        out_specs=hbm,
-        scratch_shapes=[
-            pltpu.VMEM((sectors, 7 * height, SUB, LANES), jnp.float32),
-            pltpu.VMEM((sectors, 6 * height, SUB, LANES), jnp.float32),
-            pltpu.VMEM((sectors, 6 * own, SUB, LANES), jnp.float32),
-            pltpu.VMEM((sectors * TILE_ROWS * SUB, LANES), jnp.float32),
-            pltpu.SemaphoreType.DMA((3,)),
-            pltpu.SemaphoreType.DMA((2,)),
-        ]
-        + [pltpu.VMEM((height * 2 * sectors, SUB, LANES), jnp.float32)] * 4
-        + [pltpu.VMEM(((HALF + 1) * PAIR, 2 * LANES), jnp.float32)] * UNITS,
-        compiler_params=pltpu.CompilerParams(vmem_limit_bytes=56 << 20),
-        name="step",
-    )(coef, flags, circles.reshape(sectors, 7 * height, SUB, LANES), cuts, *tables)
-    returned = lax.all_to_all(stepped.reshape(sectors, 6 * own * SUB, LANES), "lon", 0, 0)
+    edges = jax.ShapeDtypeStruct((sectors, 12, SUB, LANES), jnp.float32)
+
+    def step(upper, states, saved):
+        lo, hi = stage_rows(height, upper)[2]
+        out = jax.ShapeDtypeStruct((sectors, 6 * (hi - lo + 1), SUB, LANES), jnp.float32)
+        flags, cuts = parts[upper]
+        states = [x.reshape(sectors, -1, SUB, LANES) for x in states]
+        return pl.pallas_call(
+            functools.partial(step_kernel, upper, height, merid_step, step_size),
+            out_shape=out if upper else (out, edges, edges),
+            in_specs=[smem, smem] + [hbm] * len(states + saved) + [vmem] * 7,
+            out_specs=hbm if upper else (hbm, hbm, hbm),
+            scratch_shapes=[
+                pltpu.VMEM((sectors, 7 * height, SUB, LANES), jnp.float32),
+                pltpu.VMEM((sectors, 6 * height, SUB, LANES), jnp.float32),
+                pltpu.VMEM((sectors, 6 * height, SUB, LANES), jnp.float32),
+                pltpu.VMEM(out.shape, jnp.float32),
+                pltpu.VMEM((sectors * TILE_ROWS * SUB, LANES), jnp.float32),
+                pltpu.SemaphoreType.DMA((3,)),
+                pltpu.SemaphoreType.DMA((2,)),
+                pltpu.SemaphoreType.DMA((2,)),
+            ]
+            + [pltpu.VMEM((height * 2 * sectors, SUB, LANES), jnp.float32)] * 4
+            + [pltpu.VMEM(((HALF + 1) * PAIR, 2 * LANES), jnp.float32)] * UNITS,
+            compiler_params=pltpu.CompilerParams(vmem_limit_bytes=57 << 20),
+            cost_estimate=pl.CostEstimate(flops=0, bytes_accessed=64 << 20, transcendentals=0),
+            name="step_high" if upper else "step_low",
+        )(coef, flags, *states, *saved, cuts, *tables)
+
+    new_low, *saved = step(False, [circles_low], [])
+    returned_low = lax.all_to_all(new_low.reshape(sectors, -1, LANES), "lon", 0, 0)
+    new_high = step(True, [circles_low, circles_high], saved)
+    returned_high = lax.all_to_all(new_high.reshape(sectors, -1, LANES), "lon", 0, 0)
     new_thickness, new_winds = pl.pallas_call(
         unpack_kernel,
         out_shape=(
             jax.ShapeDtypeStruct(thickness.shape, jnp.float32),
             jax.ShapeDtypeStruct(flat.shape, jnp.float32),
         ),
-        in_specs=[vmem],
+        in_specs=[vmem, vmem],
         out_specs=(vmem, vmem),
         compiler_params=pltpu.CompilerParams(vmem_limit_bytes=40 << 20),
         name="unpack",
-    )(returned)
+    )(returned_low, returned_high)
     return new_thickness, new_winds.reshape(winds.shape)
 
 

time: 171 us -> 152 us (0.89)
  waiting for transfers between devices: 55.7 us -> 33.8 us
  blocking collectives: 42.3 us -> 30 us
  starting transfers between devices: 11.2 us -> 20.7 us
  Pallas kernels: 52.6 us -> 59.3 us
  local copies, waits for them, and re-layouts: 6.72 us -> 4.52 us
    all_to_all x1 -> x3, waiting for transfers between devices: 55.7 us -> 28.8 us  [the longest x1 24.9 us: body(): circles_low = lax.all_to_all(packed_low, 'lon', 0, 0)]
    all_to_all x1, blocking collectives: 42.3 us -> 30 us  [body(): lax.all_to_all(new_high.reshape(sectors, -1, LANES), 'lon', 0, 0)]
    all_to_all x1 -> x3, starting transfers between devices: 5.48 us -> 15 us  [the longest x1 5.56 us: body(): circles_low = lax.all_to_all(packed_low, 'lon', 0, 0)]
    pallas_call x3 -> x5, Pallas kernels: 48 us -> 55 us  [the longest x2 47.6 us: step(): pl.pallas_call(functools.partial(step_kernel, upper, height, merid_step,...]
    ppermute x1, waiting for transfers between devices: 0.01 us -> 5.03 us  [body(): north = lax.ppermute(head, 'lat', [(i + 1, i) for i in range(bands - 1)])]
    unnamed x14 -> x10, local copies, waits for them, and re-layouts: 4.59 us -> 1.28 us
  transfers between devices with their start and end apart: 3 -> 5, of which waited for: 1 -> 3; matrix products, arithmetic and copies ran while one was open for 1% -> 3% of each run, Pallas kernels for 1% -> 35%
where the time goes in v3:
time: 152 us; the launch traced here: 151 us
  Pallas kernels  59.3 us (39%)
  waiting for transfers between devices  33.8 us (22%)
  blocking collectives  30 us (20%)
  starting transfers between devices  20.7 us (14%)
  local copies, waits for them, and re-layouts  4.52 us (3%)
  other arithmetic  1.75 us (1%)
    pallas_call x2, Pallas kernels, step(): pl.pallas_call(functools.partial(step_kernel, upper, height, merid_step,...  47.6 us
    all_to_all x1, blocking collectives, body(): lax.all_to_all(new_high.reshape(sectors, -1, LANES), 'lon', 0, 0)  30 us
    all_to_all x1, waiting for transfers between devices, body(): circles_low = lax.all_to_all(packed_low, 'lon', 0, 0)  24.9 us
    all_to_all x1, starting transfers between devices, body(): circles_low = lax.all_to_all(packed_low, 'lon', 0, 0)  5.56 us
    all_to_all x1, starting transfers between devices, body(): circles_high = lax.all_to_all(packed_high, 'lon', 0, 0)  5.13 us
    ppermute x1, waiting for transfers between devices, body(): north = lax.ppermute(head, 'lat', [(i + 1, i) for i in range(bands - 1)])  5.03 us
    ppermute x1, starting transfers between devices, body(): south = lax.ppermute(tail, 'lat', [(i, i + 1) for i in range(bands - 1)])  4.38 us
    pallas_call x1, Pallas kernels, body(): pl.pallas_call(functools.partial(pack_kernel, bands), out_shape=(piece(CU...  4.37 us
  transfers between devices with their start and end apart: 5, of which 3 were waited for; matrix products, arithmetic and copies ran while one was open for 3% of the time, Pallas kernels for 35%

profile of v3, /device:TPU:1, one launch (start us, length us, event | category | flops | bytes accessed | tf_op | source)
XLA Modules:
  0.0 151.0 jit_solution(16835784135675066248)
XLA Ops:
  0.6 1.8 %edge.1 = (f32[168,128]{1,0:T(8,128)}, f32[168,128]{1,0:T(8,128)}) custom-call(f32[2,128,1024]{2,1,0:T(8,128)} %th_ref.3, f32[4,128,1024]{2,1,0:T(8,128)} %bitcast.21, f32[128,1024]{1,0:T(8,128)} %te_ref.3), custom_call_target="tpu_custom_call" | custom-call | tf_op jit(solution)/shard_map/edge/pallas_call | solution.py:521
  2.4 4.4 %collective-permute-start = (f32[168,128]{1,0:T(8,128)}, f32[168,128]{1,0:T(8,128)S(1)}, u32[]{:S(2)}, u32[]{:S(2)}) collective-permute-start(f32[168,128]{1,0:T(8,128)} %get-tuple-element.11), channel_id=1, source_target_pairs={{0,8},{8,16},{16,24},{24,32},{32,40},{40,48},{48,56},{56,64},{64,7... | collective-permute-start | bytes 258056 | tf_op jit(solution)/shard_map/ppermute | solution.py:532
  6.8 4.4 %pack.1 = (f32[8,672,128]{2,1,0:T(8,128)}, f32[8,560,128]{2,1,0:T(8,128)}) custom-call(s32[1]{0:T(128)} %bitcast.4.lat_ref, f32[2,128,1024]{2,1,0:T(8,128)} %th_ref.3, f32[4,128,1024]{2,1,0:T(8,128)} %bitcast.22, f32[128,1024]{1,0:T(8,128)} %te_ref.3), custom_call_target="tpu_custom_call" | custom-call | bytes 12582912 | tf_op jit(solution)/shard_map/pack/pallas_call | solution.py:538
  11.2 0.6 copy-done.1
  11.8 1.5 %rim.2 = f32[8,672,128]{2,1,0:T(8,128)} custom-call(f32[168,128]{1,0:T(8,128)} %copy-done.1, f32[8,672,128]{2,1,0:T(8,128)} %get-tuple-element.12.packed_ref), custom_call_target="tpu_custom_call", output_to_operand_aliasing={{}: (1, {})} | custom-call | tf_op jit(solution)/shard_map/rim/pallas_call | solution.py:553
  13.4 5.6 %all-to-all-start = ((f32[8,672,128]{2,1,0:T(8,128)}), f32[8,672,128]{2,1,0:T(8,128)S(1)}, u32[]{:S(2)}, u32[]{:S(2)}) async-start(f32[8,672,128]{2,1,0:T(8,128)} %rim.2), calls=%async_computation | async-start | bytes 5505024 | tf_op jit(solution)/shard_map/all_to_all | solution.py:565
  18.9 1.3 collective-permute-start.1
  20.2 5.0 %collective-permute-done.1.rim_ref = f32[168,128]{1,0:T(8,128)S(1)} collective-permute-done((f32[168,128]{1,0:T(8,128)S(1)}, f32[168,128]{1,0:T(8,128)S(1)}, u32[]{:S(2)}, u32[]{:S(2)}) %collective-permute-start.1) | collective-permute-done | bytes 86048 | tf_op jit(solution)/shard_map/ppermute | solution.py:533
  25.2 0.6 copy-done.2
  25.9 1.5 %rim.3 = f32[8,560,128]{2,1,0:T(8,128)} custom-call(f32[168,128]{1,0:T(8,128)} %copy-done.2, f32[8,560,128]{2,1,0:T(8,128)} %get-tuple-element.15.packed_ref), custom_call_target="tpu_custom_call", output_to_operand_aliasing={{}: (1, {})} | custom-call | tf_op jit(solution)/shard_map/rim/pallas_call | solution.py:553
  27.4 24.9 %all-to-all-done = f32[8,672,128]{2,1,0:T(8,128)S(1)} async-done(((f32[8,672,128]{2,1,0:T(8,128)}), f32[8,672,128]{2,1,0:T(8,128)S(1)}, u32[]{:S(2)}, u32[]{:S(2)}) %all-to-all-start) | async-done | bytes 2752544 | tf_op jit(solution)/shard_map/all_to_all | solution.py:565
  52.3 5.1 %all-to-all-start.2 = ((f32[8,560,128]{2,1,0:T(8,128)}), f32[8,560,128]{2,1,0:T(8,128)}, u32[]{:S(2)}, u32[]{:S(2)}) async-start(f32[8,560,128]{2,1,0:T(8,128)} %rim.3), calls=%async_computation.2 | async-start | bytes 4587520 | tf_op jit(solution)/shard_map/all_to_all | solution.py:566
  57.4 0.2 select_reduce_fusion
  57.8 0.1 reshape.135
  58.0 0.1 reshape.134
  58.2 0.1 reshape.133
  58.3 0.1 compare_reduce_fusion.1
  58.5 0.5 convert_element_type.34.flags
  59.2 0.6 stack.34.coef
  59.8 0.7 broadcast_in_dim.64.refs_1_
  60.5 21.5 %step_low.1 = (f32[8,36,8,128]{3,2,1,0:T(8,128)}, f32[8,12,8,128]{3,2,1,0:T(8,128)}, f32[8,12,8,128]{3,2,1,0:T(8,128)}) custom-call(f32[7,22]{1,0:T(8,128)} %stack.34.coef, s32[3]{0:T(128)} %convert_element_type.34.flags, f32[8,84,8,128]{3,2,1,0:T(8,128)} %bitcast.19, s32[3,64,128]{2,1,0:T(8,128)} %broadcast_in_dim.64.refs_1_, ...), custom_call_target="tpu_custom_call" | custom-call | bytes 67108864 | tf_op jit(solution)/shard_map/step_low/pallas_call | solution.py:578
  82.0 3.9 %all-to-all-done.2 = f32[8,560,128]{2,1,0:T(8,128)} async-done(((f32[8,560,128]{2,1,0:T(8,128)}), f32[8,560,128]{2,1,0:T(8,128)}, u32[]{:S(2)}, u32[]{:S(2)}) %all-to-all-start.2) | async-done | bytes 2293792 | tf_op jit(solution)/shard_map/all_to_all | solution.py:566
  86.0 4.3 %all-to-all-start.1 = ((f32[8,288,128]{2,1,0:T(8,128)}), f32[8,288,128]{2,1,0:T(8,128)S(1)}, u32[]{:S(2)}, u32[]{:S(2)}) async-start(f32[8,288,128]{2,1,0:T(8,128)} %bitcast.24), calls=%async_computation.1 | async-start | bytes 2359296 | tf_op jit(solution)/shard_map/all_to_all | solution.py:601
  90.4 0.1 reshape.142
  90.5 0.1 reshape.141
  90.7 0.1 reshape.140
  90.8 0.1 compare_reduce_fusion
  90.9 0.6 convert_element_type.35.flags
  91.5 0.7 broadcast_in_dim.68.refs_4_
  92.3 26.1 %step_high.1 = f32[8,60,8,128]{3,2,1,0:T(8,128)} custom-call(f32[7,22]{1,0:T(8,128)} %stack.34.coef, s32[3]{0:T(128)} %convert_element_type.35.flags, f32[8,84,8,128]{3,2,1,0:T(8,128)} %bitcast.20, f32[8,70,8,128]{3,2,1,0:T(8,128)} %bitcast.10.refs_1_, f32[8,12,8,128]{3,2,1,0:T(8,128)} %get-tuple-element.16.refs_2_, ...), custom_call_target="tpu_custom_call" | custom-call | bytes 67108864 | tf_op jit(solution)/shard_map/step_high/pallas_call | solution.py:578
  118.3 30.0 %all_to_all.20.b_ref = f32[8,480,128]{2,1,0:T(8,128)S(1)} all-to-all(f32[8,480,128]{2,1,0:T(8,128)} %bitcast.23), channel_id=1, replica_groups=mesh['lat'=16,'lon'=8] {'lon'}, dimensions={0} | all-to-all | bytes 3932160 | tf_op jit(solution)/shard_map/all_to_all | solution.py:603
  148.4 2.6 %unpack.1 = (f32[2,128,1024]{2,1,0:T(8,128)}, f32[4,128,1024]{2,1,0:T(8,128)}) custom-call(f32[8,288,128]{2,1,0:T(8,128)S(1)} %all-to-all-done.1.a_ref, f32[8,480,128]{2,1,0:T(8,128)S(1)} %all_to_all.20.b_ref), custom_call_target="tpu_custom_call" | custom-call | tf_op jit(solution)/shard_map/unpack/pallas_call | solution.py:604
  (31 shorter events, 0.9 us)
Async XLA Ops:
  2.4 8.8 %collective-permute-start = (f32[168,128]{1,0:T(8,128)}, f32[168,128]{1,0:T(8,128)S(1)}, u32[]{:S(2)}, u32[]{:S(2)}) collective-permute-start(f32[168,128]{1,0:T(8,128)} %get-tuple-element.11), channel_id=1, source_target_pairs={{0,8},{8,16},{16,24},{24,32},{32,40},{40,48},{48,56},{56,64},{64,7... | collective-permute-start | bytes 258056 | tf_op jit(solution)/shard_map/ppermute | solution.py:532
  11.2 0.6 copy-start.1
  13.3 5.6 %copy-start.4 = (f32[168,128]{1,0:T(8,128)S(1)}, f32[168,128]{1,0:T(8,128)}, u32[]{:S(2)}) copy-start(f32[168,128]{1,0:T(8,128)} %get-tuple-element.14) | copy-start | bytes 258052
  13.4 38.9 %all-to-all-start = ((f32[8,672,128]{2,1,0:T(8,128)}), f32[8,672,128]{2,1,0:T(8,128)S(1)}, u32[]{:S(2)}, u32[]{:S(2)}) async-start(f32[8,672,128]{2,1,0:T(8,128)} %rim.2), calls=%async_computation | async-start | bytes 5505024 | tf_op jit(solution)/shard_map/all_to_all | solution.py:565
  18.9 6.3 %collective-permute-start.1 = (f32[168,128]{1,0:T(8,128)S(1)}, f32[168,128]{1,0:T(8,128)S(1)}, u32[]{:S(2)}, u32[]{:S(2)}) collective-permute-start(f32[168,128]{1,0:T(8,128)S(1)} %copy-done.4), channel_id=1, source_target_pairs={{8,0},{16,8},{24,16},{32,24},{40,32},{48,40},{56,48},{64,56},{72,6... | collective-permute-start | bytes 258056 | tf_op jit(solution)/shard_map/ppermute | solution.py:533
  25.2 0.6 copy-start.2
  27.4 30.0 %copy-start.3 = (s32[682]{0:T(1024)S(1)}, s32[682]{0:T(1024)}, u32[]{:S(2)}) copy-start(s32[682]{0:T(1024)} %param.13) | copy-start | bytes 8188
  52.3 5.1 %copy-start = (f32[8,672,128]{2,1,0:T(8,128)}, f32[8,672,128]{2,1,0:T(8,128)S(1)}, u32[]{:S(2)}) copy-start(f32[8,672,128]{2,1,0:T(8,128)S(1)} %all-to-all-done) | copy-start | bytes 8257540
  52.3 33.7 %all-to-all-start.2 = ((f32[8,560,128]{2,1,0:T(8,128)}), f32[8,560,128]{2,1,0:T(8,128)}, u32[]{:S(2)}, u32[]{:S(2)}) async-start(f32[8,560,128]{2,1,0:T(8,128)} %rim.3), calls=%async_computation.2 | async-start | bytes 4587520 | tf_op jit(solution)/shard_map/all_to_all | solution.py:566
  86.0 32.4 %all-to-all-start.1 = ((f32[8,288,128]{2,1,0:T(8,128)}), f32[8,288,128]{2,1,0:T(8,128)S(1)}, u32[]{:S(2)}, u32[]{:S(2)}) async-start(f32[8,288,128]{2,1,0:T(8,128)} %bitcast.24), calls=%async_computation.1 | async-start | bytes 2359296 | tf_op jit(solution)/shard_map/all_to_all | solution.py:601

commit v4 on v3

--- a/solution.py
+++ b/solution.py
@@ -17,11 +17,11 @@
 RADIX = 64
 HALF = RADIX // 2
 UNCUT = 1 << 20
-TILE_ROWS = 64
+TILE_ROWS = 96
 PAIR = 16
 UNITS = 3
 BLOCK = 11
-CUT = 12
+CUT = 14
 
 
 def twisted(real, imag, k, n):
@@ -126,11 +126,19 @@
                 ]
 
 
-def pack_kernel(bands, lat_ref, th_ref, wi_ref, te_ref, a_hbm, b_hbm, piece_ref, sems):
+def pack_kernel(bands, lat_ref, th_hbm, wi_hbm, te_hbm, a_hbm, b_hbm, th_ref, wi_ref, te_ref, piece_ref, in_sems, sems):
     groups = piece_ref.shape[0]
     height = piece_ref.shape[1] // (7 * SUB)
     own = height - 2 * HALO
     split = CUT * 7 * SUB
+
+    def arrivals(g):
+        rows = pl.ds(g * own, own)
+        return (
+            pltpu.make_async_copy(th_hbm.at[:, rows], th_ref.at[:, rows], in_sems.at[0, g]),
+            pltpu.make_async_copy(wi_hbm.at[:, rows], wi_ref.at[:, rows], in_sems.at[1, g]),
+            pltpu.make_async_copy(te_hbm.at[rows], te_ref.at[rows], in_sems.at[2, g]),
+        )
 
     def departures(g):
         a_first = 0 if g > 0 else HALO * 7 * SUB
@@ -142,6 +150,14 @@
         )
 
     for g in range(groups):
+        for copy in arrivals(g):
+            copy.start()
+    for copy in arrivals(0):
+        copy.wait()
+    for g in range(groups):
+        if g < groups - 1:
+            for copy in arrivals(g + 1):
+                copy.wait()
         for f in range(7):
             src = th_ref.at[f] if f < 2 else wi_ref.at[f - 2] if f < 6 else te_ref
 
@@ -178,22 +194,26 @@
     copy.wait()
 
 
-def unpack_kernel(a_ref, b_ref, th_ref, wi_ref):
-    groups = a_ref.shape[0]
-    spans = [(r.shape[1] // (6 * SUB), r) for r in (a_ref, b_ref)]
-    own = spans[0][0] + spans[1][0]
+def unpack_kernel(first, *refs):
+    in_ref, th_hbm, wi_hbm, tile_ref, sems = refs if first == 0 else (refs[0], *refs[3:])
+    groups = in_ref.shape[0]
+    rows = in_ref.shape[1] // (6 * SUB)
+
+    def departure(f, g):
+        dst = th_hbm.at[f] if f < 2 else wi_hbm.at[f - 2]
+        block = pl.ds(g * 2 * rows + first, rows)
+        return pltpu.make_async_copy(tile_ref.at[f, g], dst.at[block], sems.at[f, g])
+
     for f in range(6):
-        dst = th_ref.at[f] if f < 2 else wi_ref.at[f - 2]
         for g in range(groups):
-            row = g * own
-            for rows, src in spans:
-                for first in range(0, rows, SUB):
-                    count = min(SUB, rows - first)
-                    for s in range(SUB):
-                        dst[pl.ds(row + first, count), s * LANES : (s + 1) * LANES] = src[
-                            g, pl.ds((first * 6 + f) * SUB + s, count, stride=6 * SUB), :
-                        ]
-                row += rows
+            for s in range(SUB):
+                tile_ref[f, g, :, s * LANES : (s + 1) * LANES] = in_ref[
+                    g, pl.ds(f * SUB + s, rows, stride=6 * SUB), :
+                ]
+            departure(f, g).start()
+    for f in range(6):
+        for g in range(groups):
+            departure(f, g).wait()
 
 
 def stage_rows(height, upper):
@@ -252,8 +272,10 @@
         ]
         in_edges = (CUT, CUT + half, height)
     else:
-        arrivals = [x_copy(i, x_low, i * CUT // 3, i * CUT // 3, CUT // 3) for i in range(3)]
-        in_edges = tuple((i + 1) * CUT // 3 for i in range(3))
+        in_edges = (CUT // 3, 2 * CUT // 3, CUT)
+        arrivals = [
+            x_copy(i, x_low, lo, lo, hi - lo) for i, (lo, hi) in enumerate(zip((0, *in_edges), in_edges))
+        ]
 
     def departure(i):
         rows = pl.ds(i * (out_rows // 2) * 6, (out_rows // 2) * 6)
@@ -354,7 +376,7 @@
         lax.fori_loop(lo, hi + 1, tendencies, 0)
 
         total = -(-6 * count // PAIR)
-        units = 3 if total % 3 == 0 else 2
+        units = 2 if total == 4 else 3
 
         def circle_filter(p, carry):
             wave = lax.broadcasted_iota(jnp.int32, (PAIR, 2 * LANES), 1)
@@ -367,7 +389,7 @@
 
             def cut_of(unit):
                 at = pl.multiple_of((p * units + unit) * PAIR, PAIR)
-                return cut_ref[index, pl.ds(at, PAIR), :]
+                return cut_ref[3 * upper + index, pl.ds(at, PAIR), :]
 
             def analyse(unit, half):
                 re, im = real_fft([t_ref[place(unit, a, half), :] for a in range(RADIX)])
@@ -433,7 +455,7 @@
                     synthesise(unit, half)
             return carry
 
-        @pl.when(flags[index] > 0)
+        @pl.when(flags[3 * upper + index] > 0)
         def _():
             lax.fori_loop(0, -(-total // units), circle_filter, 0)
 
@@ -490,16 +512,14 @@
         jnp.where(position[:, None] == table_ids[None, :], cutoffs[None, :], 0), axis=1, dtype=jnp.int32
     )
     cut = jnp.where(capped, cut, UNCUT)
-    parts = []
+    stages = []
     for upper in (False, True):
-        stages = []
         for lo, hi in stage_rows(height, upper):
             rows = jnp.repeat(cut[lo : hi + 1], 6)
             stages.append(jnp.pad(rows, (0, TILE_ROWS - rows.shape[0]), constant_values=UNCUT))
-        cuts = jnp.stack(stages)
-        flags = jnp.any(cuts < UNCUT, axis=1).astype(jnp.int32)
-        parts.append((flags, jnp.broadcast_to(cuts[:, :, None], (3, TILE_ROWS, LANES))))
-    return coef, parts
+    cuts = jnp.stack(stages)
+    flags = jnp.any(cuts < UNCUT, axis=1).astype(jnp.int32)
+    return coef, flags, jnp.broadcast_to(cuts[:, :, None], (6, TILE_ROWS, LANES))
 
 
 def body(thickness, winds, terrain, cutoffs):
@@ -538,10 +558,14 @@
     packed_low, packed_high = pl.pallas_call(
         functools.partial(pack_kernel, bands),
         out_shape=(piece(CUT, 7), piece(height - CUT, 7)),
-        in_specs=[smem] + [vmem] * 3,
+        in_specs=[smem] + [hbm] * 3,
         out_specs=(hbm, hbm),
         scratch_shapes=[
+            pltpu.VMEM(thickness.shape, jnp.float32),
+            pltpu.VMEM(flat.shape, jnp.float32),
+            pltpu.VMEM(terrain.shape, jnp.float32),
             pltpu.VMEM(piece(height, 7).shape, jnp.float32),
+            pltpu.SemaphoreType.DMA((3, sectors)),
             pltpu.SemaphoreType.DMA((2, sectors)),
         ],
         compiler_params=pltpu.CompilerParams(vmem_limit_bytes=56 << 20),
@@ -553,7 +577,7 @@
         return pl.pallas_call(
             functools.partial(rim_kernel, group, start),
             out_shape=jax.ShapeDtypeStruct(packed.shape, jnp.float32),
-            in_specs=[vmem, hbm],
+            in_specs=[pl.BlockSpec(memory_space=pl.ANY), hbm],
             out_specs=hbm,
             scratch_shapes=[pltpu.SemaphoreType.DMA],
             input_output_aliases={1: 0},
@@ -566,14 +590,13 @@
     circles_high = lax.all_to_all(packed_high, "lon", 0, 0)
 
     row_start = lat * row_count + lax.axis_index("lon") * own
-    coef, parts = row_tables(cutoffs, row_start, height, total_rows, polar)
+    coef, flags, cuts = row_tables(cutoffs, row_start, height, total_rows, polar)
     tables = [jnp.asarray(t) for t in filter_tables()]
     edges = jax.ShapeDtypeStruct((sectors, 12, SUB, LANES), jnp.float32)
 
     def step(upper, states, saved):
         lo, hi = stage_rows(height, upper)[2]
         out = jax.ShapeDtypeStruct((sectors, 6 * (hi - lo + 1), SUB, LANES), jnp.float32)
-        flags, cuts = parts[upper]
         states = [x.reshape(sectors, -1, SUB, LANES) for x in states]
         return pl.pallas_call(
             functools.partial(step_kernel, upper, height, merid_step, step_size),
@@ -592,7 +615,7 @@
             ]
             + [pltpu.VMEM((height * 2 * sectors, SUB, LANES), jnp.float32)] * 4
             + [pltpu.VMEM(((HALF + 1) * PAIR, 2 * LANES), jnp.float32)] * UNITS,
-            compiler_params=pltpu.CompilerParams(vmem_limit_bytes=57 << 20),
+            compiler_params=pltpu.CompilerParams(vmem_limit_bytes=50 << 20),
             cost_estimate=pl.CostEstimate(flops=0, bytes_accessed=64 << 20, transcendentals=0),
             name="step_high" if upper else "step_low",
         )(coef, flags, *states, *saved, cuts, *tables)
@@ -601,17 +624,29 @@
     returned_low = lax.all_to_all(new_low.reshape(sectors, -1, LANES), "lon", 0, 0)
     new_high = step(True, [circles_low, circles_high], saved)
     returned_high = lax.all_to_all(new_high.reshape(sectors, -1, LANES), "lon", 0, 0)
-    new_thickness, new_winds = pl.pallas_call(
-        unpack_kernel,
-        out_shape=(
-            jax.ShapeDtypeStruct(thickness.shape, jnp.float32),
-            jax.ShapeDtypeStruct(flat.shape, jnp.float32),
-        ),
-        in_specs=[vmem, vmem],
-        out_specs=(vmem, vmem),
-        compiler_params=pltpu.CompilerParams(vmem_limit_bytes=40 << 20),
-        name="unpack",
-    )(returned_low, returned_high)
+
+    def unpack(first, pieces, outputs):
+        rows = pieces.shape[1] // (6 * SUB)
+        return pl.pallas_call(
+            functools.partial(unpack_kernel, first),
+            out_shape=(
+                jax.ShapeDtypeStruct(thickness.shape, jnp.float32),
+                jax.ShapeDtypeStruct(flat.shape, jnp.float32),
+            ),
+            in_specs=[vmem] + [hbm] * len(outputs),
+            out_specs=(hbm, hbm),
+            scratch_shapes=[
+                pltpu.VMEM((6, sectors, rows, col_count), jnp.float32),
+                pltpu.SemaphoreType.DMA((6, sectors)),
+            ],
+            input_output_aliases={1: 0, 2: 1} if outputs else {},
+            compiler_params=pltpu.CompilerParams(vmem_limit_bytes=40 << 20),
+            cost_estimate=pl.CostEstimate(flops=0, bytes_accessed=4 << 20, transcendentals=0),
+            name="unpack",
+        )(pieces, *outputs)
+
+    outputs = unpack(0, returned_low, ())
+    new_thickness, new_winds = unpack(own // 2, returned_high, outputs)
     return new_thickness, new_winds.reshape(winds.shape)
 
 

time: 152 us -> 145 us (0.954)
  blocking collectives: 30 us -> 0 us
  waiting for transfers between devices: 33.8 us -> 52.4 us
  starting transfers between devices: 20.7 us -> 25.5 us
  Pallas kernels: 59.3 us -> 62.3 us
  local copies, waits for them, and re-layouts: 4.52 us -> 2.66 us
    all_to_all x1 -> x0, blocking collectives: 30 us -> none  [body(): lax.all_to_all(new_high.reshape(sectors, -1, LANES), 'lon', 0, 0)]
    all_to_all x0 -> x1, waiting for transfers between devices: none -> 19.2 us  [body(): lax.all_to_all(new_high.reshape(sectors, -1, LANES), 'lon', 0, 0)]
    pallas_call x2, Pallas kernels: 3.04 us -> 7.43 us  [rimmed(): pl.pallas_call(functools.partial(rim_kernel, group, start), out_shape=jax...]
    all_to_all x0 -> x1, starting transfers between devices: none -> 4.35 us  [body(): lax.all_to_all(new_high.reshape(sectors, -1, LANES), 'lon', 0, 0)]
    all_to_all x1, waiting for transfers between devices: 3.93 us -> 0.01 us  [body(): circles_high = lax.all_to_all(packed_high, 'lon', 0, 0)]
    all_to_all x1, waiting for transfers between devices: 24.9 us -> 27.5 us  [body(): circles_low = lax.all_to_all(packed_low, 'lon', 0, 0)]
    pallas_call x1 -> x2, Pallas kernels: 2.57 us -> 3.12 us  [unpack(): pl.pallas_call(functools.partial(unpack_kernel, first), out_shape=(jax.Sh...]
  transfers between devices with their start and end apart: 5 -> 6, of which waited for: 3 -> 4; matrix products, arithmetic and copies ran while one was open for 3% -> 1% of each run, Pallas kernels for 35% -> 38%
where the time goes in v4:
time: 145 us; the launch traced here: 144 us
  Pallas kernels  62.3 us (43%)
  waiting for transfers between devices  52.4 us (36%)
  starting transfers between devices  25.5 us (18%)
  local copies, waits for them, and re-layouts  2.66 us (2%)
    pallas_call x2, Pallas kernels, step(): pl.pallas_call(functools.partial(step_kernel, upper, height, merid_step,...  46.2 us
    all_to_all x1, waiting for transfers between devices, body(): circles_low = lax.all_to_all(packed_low, 'lon', 0, 0)  27.5 us
    all_to_all x1, waiting for transfers between devices, body(): lax.all_to_all(new_high.reshape(sectors, -1, LANES), 'lon', 0, 0)  19.2 us
    pallas_call x2, Pallas kernels, rimmed(): pl.pallas_call(functools.partial(rim_kernel, group, start), out_shape=jax...  7.43 us
    all_to_all x1, starting transfers between devices, body(): circles_low = lax.all_to_all(packed_low, 'lon', 0, 0)  5.56 us
    ppermute x1, waiting for transfers between devices, body(): north = lax.ppermute(head, 'lat', [(i + 1, i) for i in range(bands - 1)])  5.14 us
    all_to_all x1, starting transfers between devices, body(): circles_high = lax.all_to_all(packed_high, 'lon', 0, 0)  5.08 us
    all_to_all x1, starting transfers between devices, body(): lax.all_to_all(new_low.reshape(sectors, -1, LANES), 'lon', 0, 0)  4.83 us
  transfers between devices with their start and end apart: 6, of which 4 were waited for; matrix products, arithmetic and copies ran while one was open for 1% of the time, Pallas kernels for 38%

profile of v4, /device:TPU:1, one launch (start us, length us, event | category | flops | bytes accessed | tf_op | source)
XLA Modules:
  0.0 144.5 jit_solution(9097682259585859194)
XLA Ops:
  0.6 1.8 %edge.1 = (f32[168,128]{1,0:T(8,128)}, f32[168,128]{1,0:T(8,128)}) custom-call(f32[2,128,1024]{2,1,0:T(8,128)} %th_hbm.1, f32[4,128,1024]{2,1,0:T(8,128)} %bitcast.19, f32[128,1024]{1,0:T(8,128)} %te_hbm.1), custom_call_target="tpu_custom_call" | custom-call | tf_op jit(solution)/shard_map/edge/pallas_call | solution.py:541
  2.4 4.4 %collective-permute-start = (f32[168,128]{1,0:T(8,128)}, f32[168,128]{1,0:T(8,128)S(1)}, u32[]{:S(2)}, u32[]{:S(2)}) collective-permute-start(f32[168,128]{1,0:T(8,128)} %get-tuple-element.13), channel_id=1, source_target_pairs={{0,8},{8,16},{16,24},{24,32},{32,40},{40,48},{48,56},{56,64},{64,7... | collective-permute-start | bytes 258056 | tf_op jit(solution)/shard_map/ppermute | solution.py:552
  6.8 3.9 %pack.1 = (f32[8,784,128]{2,1,0:T(8,128)}, f32[8,448,128]{2,1,0:T(8,128)}) custom-call(s32[1]{0:T(128)} %bitcast.7.lat_ref, f32[2,128,1024]{2,1,0:T(8,128)} %th_hbm.1, f32[4,128,1024]{2,1,0:T(8,128)} %bitcast.20, f32[128,1024]{1,0:T(8,128)} %te_hbm.1), custom_call_target="tpu_custom_call" | custom-call | bytes 12582912 | tf_op jit(solution)/shard_map/pack/pallas_call | solution.py:558
  10.7 0.6 copy-done.6
  11.3 3.7 %rim.2 = f32[8,784,128]{2,1,0:T(8,128)} custom-call(f32[168,128]{1,0:T(8,128)} %copy-done.6, f32[8,784,128]{2,1,0:T(8,128)} %get-tuple-element.14.packed_ref), custom_call_target="tpu_custom_call", output_to_operand_aliasing={{}: (1, {})} | custom-call | tf_op jit(solution)/shard_map/rim/pallas_call | solution.py:577
  15.0 5.6 %all-to-all-start = ((f32[8,784,128]{2,1,0:T(8,128)}), f32[8,784,128]{2,1,0:T(8,128)}, u32[]{:S(2)}, u32[]{:S(2)}) async-start(f32[8,784,128]{2,1,0:T(8,128)} %rim.2), calls=%async_computation | async-start | bytes 6422528 | tf_op jit(solution)/shard_map/all_to_all | solution.py:589
  20.6 1.3 collective-permute-start.1
  21.9 5.1 %collective-permute-done.1.rim_ref = f32[168,128]{1,0:T(8,128)S(1)} collective-permute-done((f32[168,128]{1,0:T(8,128)S(1)}, f32[168,128]{1,0:T(8,128)S(1)}, u32[]{:S(2)}, u32[]{:S(2)}) %collective-permute-start.1) | collective-permute-done | bytes 86048 | tf_op jit(solution)/shard_map/ppermute | solution.py:553
  27.0 0.6 copy-done.7
  27.7 3.7 %rim.3 = f32[8,448,128]{2,1,0:T(8,128)} custom-call(f32[168,128]{1,0:T(8,128)} %copy-done.7, f32[8,448,128]{2,1,0:T(8,128)} %get-tuple-element.16.packed_ref), custom_call_target="tpu_custom_call", output_to_operand_aliasing={{}: (1, {})} | custom-call | tf_op jit(solution)/shard_map/rim/pallas_call | solution.py:577
  31.5 27.5 %all-to-all-done = f32[8,784,128]{2,1,0:T(8,128)} async-done(((f32[8,784,128]{2,1,0:T(8,128)}), f32[8,784,128]{2,1,0:T(8,128)}, u32[]{:S(2)}, u32[]{:S(2)}) %all-to-all-start) | async-done | bytes 3211296 | tf_op jit(solution)/shard_map/all_to_all | solution.py:589
  59.0 5.1 %all-to-all-start.1 = ((f32[8,448,128]{2,1,0:T(8,128)}), f32[8,448,128]{2,1,0:T(8,128)}, u32[]{:S(2)}, u32[]{:S(2)}) async-start(f32[8,448,128]{2,1,0:T(8,128)} %rim.3), calls=%async_computation.1 | async-start | bytes 3670016 | tf_op jit(solution)/shard_map/all_to_all | solution.py:590
  64.1 0.2 select_reduce_fusion
  64.3 0.1 slice.19
  64.3 0.1 slice.18
  64.4 0.1 fusion.3
  64.5 0.1 reshape.137
  64.7 0.1 reshape.136
  64.8 0.1 reshape.135
  65.0 0.1 reshape.134
  65.1 0.1 reshape.132
  65.3 0.1 reshape.133
  65.5 0.1 compare_reduce_fusion
  65.8 0.1 broadcast_in_dim.61.refs_1_.refs_4_
  66.0 26.1 %step_low.1 = (f32[8,48,8,128]{3,2,1,0:T(8,128)}, f32[8,12,8,128]{3,2,1,0:T(8,128)S(1)}, f32[8,12,8,128]{3,2,1,0:T(8,128)S(1)}) custom-call(f32[7,22]{1,0:T(8,128)S(1)} %stack.31.coef, s32[6]{0:T(128)S(1)} %convert_element_type.31.flags, f32[8,98,8,128]{3,2,1,0:T(8,128)} %bitcast.8.refs_0_, s32[6,96,128]{2,1,0:T(8,128)S(1)} %broadcast_in_dim.61.refs_1_.refs_4_, ...), custom_call_target="tpu_custom_call" | custom-call | bytes 67108864 | tf_op jit(solution)/shard_map/step_low/pallas_call | solution.py:601
  92.1 4.8 %all-to-all-start.3 = ((f32[8,384,128]{2,1,0:T(8,128)}), f32[8,384,128]{2,1,0:T(8,128)S(1)}, u32[]{:S(2)}, u32[]{:S(2)}) async-start(f32[8,384,128]{2,1,0:T(8,128)} %bitcast.11), calls=%async_computation.3 | async-start | bytes 3145728 | tf_op jit(solution)/shard_map/all_to_all | solution.py:624
  96.9 20.1 %step_high.1 = f32[8,48,8,128]{3,2,1,0:T(8,128)} custom-call(f32[7,22]{1,0:T(8,128)S(1)} %stack.31.coef, s32[6]{0:T(128)S(1)} %convert_element_type.31.flags, f32[8,98,8,128]{3,2,1,0:T(8,128)} %bitcast.8.refs_0_, f32[8,56,8,128]{3,2,1,0:T(8,128)} %bitcast.9.refs_1_, f32[8,12,8,128]{3,2,1,0:T(8,128)S(1)} %get-tuple-element.17.refs_2_, ...), custom_call_target="tpu_custom_call" | custom-call | bytes 67108864 | tf_op jit(solution)/shard_map/step_high/pallas_call | solution.py:601
  117.0 0.6 all-to-all-done.3.refs_0_
  117.7 4.4 %all-to-all-start.2 = ((f32[8,384,128]{2,1,0:T(8,128)}), f32[8,384,128]{2,1,0:T(8,128)S(1)}, u32[]{:S(2)}, u32[]{:S(2)}) async-start(f32[8,384,128]{2,1,0:T(8,128)} %bitcast.10), calls=%async_computation.2 | async-start | bytes 3145728 | tf_op jit(solution)/shard_map/all_to_all | solution.py:626
  122.0 1.6 %unpack.2 = (f32[2,128,1024]{2,1,0:T(8,128)}, f32[4,128,1024]{2,1,0:T(8,128)}) custom-call(f32[8,384,128]{2,1,0:T(8,128)S(1)} %all-to-all-done.3.refs_0_), custom_call_target="tpu_custom_call" | custom-call | bytes 4194304 | tf_op jit(solution)/shard_map/unpack/pallas_call | solution.py:630
  123.6 19.2 %all-to-all-done.2.refs_0_ = f32[8,384,128]{2,1,0:T(8,128)S(1)} async-done(((f32[8,384,128]{2,1,0:T(8,128)}), f32[8,384,128]{2,1,0:T(8,128)S(1)}, u32[]{:S(2)}, u32[]{:S(2)}) %all-to-all-start.2) | async-done | bytes 1572896 | tf_op jit(solution)/shard_map/all_to_all | solution.py:626
  142.7 1.6 %unpack.3 = (f32[2,128,1024]{2,1,0:T(8,128)}, f32[4,128,1024]{2,1,0:T(8,128)}) custom-call(f32[8,384,128]{2,1,0:T(8,128)S(1)} %all-to-all-done.2.refs_0_, f32[2,128,1024]{2,1,0:T(8,128)} %get-tuple-element.20.refs_1_, f32[4,128,1024]{2,1,0:T(8,128)} %get-tuple-element.21.refs_2_), custom_call_target="tpu_custom_call", output_to_operand_aliasing={{0}: (1, {}), {1}: (2, {})} | custom-call | bytes 4194304 | tf_op jit(solution)/shard_map/unpack/pallas_call | solution.py:630
  (38 shorter events, 0.7 us)
Async XLA Ops:
  2.4 8.3 %collective-permute-start = (f32[168,128]{1,0:T(8,128)}, f32[168,128]{1,0:T(8,128)S(1)}, u32[]{:S(2)}, u32[]{:S(2)}) collective-permute-start(f32[168,128]{1,0:T(8,128)} %get-tuple-element.13), channel_id=1, source_target_pairs={{0,8},{8,16},{16,24},{24,32},{32,40},{40,48},{48,56},{56,64},{64,7... | collective-permute-start | bytes 258056 | tf_op jit(solution)/shard_map/ppermute | solution.py:552
  10.7 0.6 copy-start.6
  15.0 5.6 %copy-start.9 = (f32[168,128]{1,0:T(8,128)S(1)}, f32[168,128]{1,0:T(8,128)}, u32[]{:S(2)}) copy-start(f32[168,128]{1,0:T(8,128)} %get-tuple-element.15) | copy-start | bytes 258052
  15.0 43.9 %all-to-all-start = ((f32[8,784,128]{2,1,0:T(8,128)}), f32[8,784,128]{2,1,0:T(8,128)}, u32[]{:S(2)}, u32[]{:S(2)}) async-start(f32[8,784,128]{2,1,0:T(8,128)} %rim.2), calls=%async_computation | async-start | bytes 6422528 | tf_op jit(solution)/shard_map/all_to_all | solution.py:589
  20.6 6.4 %collective-permute-start.1 = (f32[168,128]{1,0:T(8,128)S(1)}, f32[168,128]{1,0:T(8,128)S(1)}, u32[]{:S(2)}, u32[]{:S(2)}) collective-permute-start(f32[168,128]{1,0:T(8,128)S(1)} %copy-done.9), channel_id=1, source_target_pairs={{8,0},{16,8},{24,16},{32,24},{40,32},{48,40},{56,48},{64,56},{72,6... | collective-permute-start | bytes 258056 | tf_op jit(solution)/shard_map/ppermute | solution.py:553
  27.0 0.6 copy-start.7
  31.4 32.7 %copy-start.8 = (s32[682]{0:T(1024)S(1)}, s32[682]{0:T(1024)}, u32[]{:S(2)}) copy-start(s32[682]{0:T(1024)} %param.13) | copy-start | bytes 8188
  31.4 34.6 %copy-start = (bf16[256,256]{1,0:T(8,128)(2,1)S(1)}, bf16[256,256]{1,0:T(8,128)(2,1)}, u32[]{:S(2)}) copy-start(bf16[256,256]{1,0:T(8,128)(2,1)} %constant.61.clone.refs_5_.refs_8_) | copy-start | bytes 393220
  31.4 34.6 %copy-start.1 = (bf16[256,256]{1,0:T(8,128)(2,1)S(1)}, bf16[256,256]{1,0:T(8,128)(2,1)}, u32[]{:S(2)}) copy-start(bf16[256,256]{1,0:T(8,128)(2,1)} %constant.60.clone.refs_4_.refs_7_) | copy-start | bytes 393220
  31.4 34.5 %copy-start.2 = (bf16[256,256]{1,0:T(8,128)(2,1)S(1)}, bf16[256,256]{1,0:T(8,128)(2,1)}, u32[]{:S(2)}) copy-start(bf16[256,256]{1,0:T(8,128)(2,1)} %constant.59.clone.refs_3_.refs_6_) | copy-start | bytes 393220
  31.4 34.5 %copy-start.3 = (bf16[256,256]{1,0:T(8,128)(2,1)S(1)}, bf16[256,256]{1,0:T(8,128)(2,1)}, u32[]{:S(2)}) copy-start(bf16[256,256]{1,0:T(8,128)(2,1)} %constant.58.clone.refs_2_.refs_5_) | copy-start | bytes 393220
  31.4 34.5 %copy-start.4 = (f32[40,128]{1,0:T(8,128)S(1)}, f32[40,128]{1,0:T(8,128)}, u32[]{:S(2)}) copy-start(f32[40,128]{1,0:T(8,128)} %constant.63.clone.refs_7_.refs_10_) | copy-start | bytes 61444
  31.4 34.5 %copy-start.5 = (f32[40,128]{1,0:T(8,128)S(1)}, f32[40,128]{1,0:T(8,128)}, u32[]{:S(2)}) copy-start(f32[40,128]{1,0:T(8,128)} %constant.62.clone.refs_6_.refs_9_) | copy-start | bytes 61444
  59.0 33.1 %all-to-all-start.1 = ((f32[8,448,128]{2,1,0:T(8,128)}), f32[8,448,128]{2,1,0:T(8,128)}, u32[]{:S(2)}, u32[]{:S(2)}) async-start(f32[8,448,128]{2,1,0:T(8,128)} %rim.3), calls=%async_computation.1 | async-start | bytes 3670016 | tf_op jit(solution)/shard_map/all_to_all | solution.py:590
  92.1 25.6 %all-to-all-start.3 = ((f32[8,384,128]{2,1,0:T(8,128)}), f32[8,384,128]{2,1,0:T(8,128)S(1)}, u32[]{:S(2)}, u32[]{:S(2)}) async-start(f32[8,384,128]{2,1,0:T(8,128)} %bitcast.11), calls=%async_computation.3 | async-start | bytes 3145728 | tf_op jit(solution)/shard_map/all_to_all | solution.py:624
  117.7 25.1 %all-to-all-start.2 = ((f32[8,384,128]{2,1,0:T(8,128)}), f32[8,384,128]{2,1,0:T(8,128)S(1)}, u32[]{:S(2)}, u32[]{:S(2)}) async-start(f32[8,384,128]{2,1,0:T(8,128)} %bitcast.10), calls=%async_computation.2 | async-start | bytes 3145728 | tf_op jit(solution)/shard_map/all_to_all | solution.py:626

commit v5 on v4

--- a/solution.py
+++ b/solution.py
@@ -21,7 +21,7 @@
 PAIR = 16
 UNITS = 3
 BLOCK = 11
-CUT = 14
+INNER = 14
 
 
 def twisted(real, imag, k, n):
@@ -130,8 +130,6 @@
     groups = piece_ref.shape[0]
     height = piece_ref.shape[1] // (7 * SUB)
     own = height - 2 * HALO
-    split = CUT * 7 * SUB
-
     def arrivals(g):
         rows = pl.ds(g * own, own)
         return (
@@ -141,13 +139,15 @@
         )
 
     def departures(g):
-        a_first = 0 if g > 0 else HALO * 7 * SUB
-        b_last = (height if g < groups - 1 else HALO + own) * 7 * SUB
-        a, b = pl.ds(a_first, split - a_first), pl.ds(split, b_last - split)
-        return (
-            pltpu.make_async_copy(piece_ref.at[g, a], a_hbm.at[g, a], sems.at[0, g]),
-            pltpu.make_async_copy(piece_ref.at[g, b], b_hbm.at[g, pl.ds(0, b_last - split)], sems.at[1, g]),
-        )
+        def copy(i, dst, src_row, dst_row, count):
+            src = piece_ref.at[g, pl.ds(src_row * 7 * SUB, count * 7 * SUB)]
+            dst = dst.at[g, pl.ds(dst_row * 7 * SUB, count * 7 * SUB)]
+            return pltpu.make_async_copy(src, dst, sems.at[i, g])
+
+        top = HALO + INNER
+        last = height if g < groups - 1 else HALO + own
+        copies = [copy(0, a_hbm, HALO, 0, INNER), copy(1, b_hbm, top, HALO, last - top)]
+        return copies + ([copy(2, b_hbm, 0, 0, HALO)] if g > 0 else [])
 
     for g in range(groups):
         for copy in arrivals(g):
@@ -188,55 +188,64 @@
             copy.wait()
 
 
-def rim_kernel(group, start, rim_ref, packed_ref, out_ref, sem):
-    copy = pltpu.make_async_copy(rim_ref, out_ref.at[group, pl.ds(start, rim_ref.shape[0])], sem)
-    copy.start()
-    copy.wait()
-
-
-def unpack_kernel(first, *refs):
-    in_ref, th_hbm, wi_hbm, tile_ref, sems = refs if first == 0 else (refs[0], *refs[3:])
-    groups = in_ref.shape[0]
-    rows = in_ref.shape[1] // (6 * SUB)
-
-    def departure(f, g):
+def rim_kernel(south_ref, north_ref, packed_ref, out_ref, sems):
+    groups, length = out_ref.shape[0], out_ref.shape[1]
+    rim = HALO * 7 * SUB
+    low = pltpu.make_async_copy(south_ref, out_ref.at[0, pl.ds(0, rim)], sems.at[0])
+    high = pltpu.make_async_copy(north_ref, out_ref.at[groups - 1, pl.ds(length - rim, rim)], sems.at[1])
+    low.start()
+    high.start()
+    low.wait()
+    high.wait()
+
+
+def unpack_kernel(low_ref, high_ref, th_hbm, wi_hbm, tile_ref, sems):
+    groups = low_ref.shape[0]
+    low_rows, high_rows = (r.shape[1] // (6 * SUB) for r in (low_ref, high_ref))
+    own = low_rows + high_rows
+    spans = (
+        (low_ref, 0, HALO, low_rows),
+        (high_ref, 0, 0, HALO),
+        (high_ref, HALO, HALO + low_rows, high_rows - HALO),
+    )
+
+    def departure(f):
         dst = th_hbm.at[f] if f < 2 else wi_hbm.at[f - 2]
-        block = pl.ds(g * 2 * rows + first, rows)
-        return pltpu.make_async_copy(tile_ref.at[f, g], dst.at[block], sems.at[f, g])
+        return pltpu.make_async_copy(tile_ref.at[f], dst, sems.at[f])
 
     for f in range(6):
         for g in range(groups):
-            for s in range(SUB):
-                tile_ref[f, g, :, s * LANES : (s + 1) * LANES] = in_ref[
-                    g, pl.ds(f * SUB + s, rows, stride=6 * SUB), :
-                ]
-            departure(f, g).start()
+            for src, src_row, row, count in spans:
+                for s in range(SUB):
+                    tile_ref[f, pl.ds(g * own + row, count), s * LANES : (s + 1) * LANES] = src[
+                        g, pl.ds((src_row * 6 + f) * SUB + s, count, stride=6 * SUB), :
+                    ]
+        departure(f).start()
     for f in range(6):
-        for g in range(groups):
-            departure(f, g).wait()
-
-
-def stage_rows(height, upper):
-    if upper:
-        return [(CUT - 1 - k, height - 2 - k) for k in range(3)]
-    return [(1 + k, CUT - 2 - k) for k in range(3)]
-
-
-def step_kernel(upper, height, merid_step, step_size, coef, flags, *refs):
-    if upper:
+        departure(f).wait()
+
+
+def stage_rows(height, outer):
+    top = HALO + INNER
+    if outer:
+        return [((1 + k, HALO + k), (top - 1 - k, height - 2 - k)) for k in range(3)]
+    return [((HALO + 1 + k, top - 2 - k),) for k in range(3)]
+
+
+def step_kernel(outer, height, merid_step, step_size, coef, flags, *refs):
+    if outer:
         x_low, x_high, s1_hbm, s2_hbm, *refs = refs
     else:
         x_low, *refs = refs
     cut_ref, wfh_ref, wfl_ref, wbh_ref, wbl_ref, twc_ref, tws_ref, *refs = refs
     out_hbm, *refs = refs
-    if not upper:
+    if not outer:
         s1_hbm, s2_hbm, *refs = refs
     x_ref, s1_ref, s2_ref, out_ref, t_ref, in_sems, out_sems, edge_sems, *refs = refs
     e_ref, z_ref, uu_ref, vv_ref, *y_refs = refs
     chunks = x_ref.shape[0]
-    ranges = stage_rows(height, upper)
-    out_lo, out_hi = ranges[2]
-    out_rows = out_hi - out_lo + 1
+    ranges = stage_rows(height, outer)
+    top = HALO + INNER
     lane = lax.broadcasted_iota(jnp.int32, (SUB, LANES), 1)
     sub = lax.broadcasted_iota(jnp.int32, (SUB, LANES), 0)
     last_lane, first_lane = lane == LANES - 1, lane == 0
@@ -263,42 +272,42 @@
             src.at[:, pl.ds(src_row * 7, count * 7)], x_ref.at[:, pl.ds(row * 7, count * 7)], in_sems.at[i]
         )
 
-    if upper:
-        half = (height - CUT) // 2
+    if outer:
         arrivals = [
-            x_copy(0, x_low, CUT - HALO, CUT - HALO, HALO),
-            x_copy(1, x_high, 0, CUT, half),
-            x_copy(2, x_high, half, CUT + half, height - CUT - half),
+            [x_copy(0, x_high, 0, 0, HALO), x_copy(1, x_low, 0, HALO, HALO)],
+            [x_copy(2, x_low, INNER - HALO, top - HALO, HALO), x_copy(3, x_high, HALO, top, height - top)],
         ]
-        in_edges = (CUT, CUT + half, height)
+        out_edges = (0, HALO, height - 2 * HALO - (INNER - 6))
     else:
-        in_edges = (CUT // 3, 2 * CUT // 3, CUT)
+        bounds = (0, INNER // 3, 2 * INNER // 3, INNER)
         arrivals = [
-            x_copy(i, x_low, lo, lo, hi - lo) for i, (lo, hi) in enumerate(zip((0, *in_edges), in_edges))
+            [x_copy(i, x_low, lo, HALO + lo, hi - lo)] for i, (lo, hi) in enumerate(zip(bounds, bounds[1:]))
         ]
+        out_edges = (0, (INNER - 6) // 2, INNER - 6)
 
     def departure(i):
-        rows = pl.ds(i * (out_rows // 2) * 6, (out_rows // 2) * 6)
+        rows = pl.ds(out_edges[i] * 6, (out_edges[i + 1] - out_edges[i]) * 6)
         return pltpu.make_async_copy(out_ref.at[:, rows], out_hbm.at[:, rows], out_sems.at[i])
 
-    def edge(i):
-        hbm, ref = ((s1_hbm, s1_ref), (s2_hbm, s2_ref))[i]
-        ref = ref.at[:, pl.ds((CUT - 3 - i) * 6, 12)]
-        src, dst = (hbm, ref) if upper else (ref, hbm)
-        return pltpu.make_async_copy(src, dst, edge_sems.at[i])
-
-    for copy in arrivals:
+    def edges(index):
+        hbm, ref = ((s1_hbm, s1_ref), (s2_hbm, s2_ref))[index]
+        copies = []
+        for i, row in enumerate((HALO + 1 + index, top - 3 - index)):
+            src, dst = hbm.at[:, pl.ds(i * 12, 12)], ref.at[:, pl.ds(row * 6, 12)]
+            src, dst = (src, dst) if outer else (dst, src)
+            copies.append(pltpu.make_async_copy(src, dst, edge_sems.at[index, i]))
+        return copies
+
+    for copy in sum(arrivals, []):
         copy.start()
-    if upper:
-        edge(0).start()
-        edge(1).start()
+    if outer:
+        for copy in edges(0) + edges(1):
+            copy.start()
 
     def stage(src, dst, index, fraction):
         fields = 7 if index == 0 else 6
         final = index == 2
-        lo, hi = ranges[index]
-        in_lo, in_hi = lo - 1, hi + 1
-        count = hi - lo + 1
+        count = sum(hi - lo + 1 for lo, hi in ranges[index])
 
         def get(f, r):
             return [src[d, r * fields + f] for d in range(chunks)]
@@ -306,7 +315,7 @@
         def terrain(r):
             return [x_ref[d, r * 7 + 6] for d in range(chunks)]
 
-        def corners(r, carry):
+        def corners(in_lo, in_hi, r, carry):
             rn = jnp.minimum(r + 1, in_hi)
             rs = jnp.maximum(r - 1, in_lo)
             c_half, cn_half = coef[0, r] * dy_inv, coef[0, rn] * dy_inv
@@ -327,19 +336,7 @@
                     z_ref[at] = sine + curl * e_inv
             return carry
 
-        if index == 0:
-            first = in_lo
-            for i in range(3):
-                arrivals[i].wait()
-                last = in_edges[i] - 1 if i < 2 else in_edges[i]
-                lax.fori_loop(first, last, corners, 0)
-                first = last
-        else:
-            if upper:
-                edge(index - 1).wait()
-            lax.fori_loop(in_lo, in_hi + 1, corners, 0)
-
-        def tendencies(r, carry):
+        def tendencies(shift, r, carry):
             c_inv = coef[1, r]
             fn, fs = coef[4, r] * (0.5 * dy_inv), coef[4, r - 1] * (0.5 * dy_inv)
             live = coef[5, r]
@@ -349,7 +346,7 @@
                     return [ref[(row * 2 + k) * chunks + d] for d in range(chunks)]
 
                 def put(f, d, value):
-                    start = (d * TILE_ROWS + (r - lo) * 6 + f) * SUB
+                    start = (d * TILE_ROWS + (r - shift) * 6 + f) * SUB
                     t_ref[pl.ds(pl.multiple_of(start, SUB), SUB), :] = value
 
                 h, hn, hs = get(k, r), get(k, r + 1), get(k, r - 1)
@@ -373,7 +370,27 @@
                     put(4 + k, d, live * (dy_inv * (ec[d] - en[d]) - turn))
             return carry
 
-        lax.fori_loop(lo, hi + 1, tendencies, 0)
+        if index > 0 and outer:
+            for copy in edges(index - 1):
+                copy.wait()
+        base = 0
+        for i, (lo, hi) in enumerate(ranges[index]):
+            calc = functools.partial(corners, lo - 1, hi + 1)
+            if index > 0:
+                lax.fori_loop(lo - 1, hi + 2, calc, 0)
+            elif outer:
+                for copy in arrivals[i]:
+                    copy.wait()
+                lax.fori_loop(lo - 1, hi + 2, calc, 0)
+            else:
+                first = lo - 1
+                for j, (copy,) in enumerate(arrivals):
+                    copy.wait()
+                    last = HALO + bounds[j + 1] - (1 if j < 2 else 0)
+                    lax.fori_loop(first, last, calc, 0)
+                    first = last
+            lax.fori_loop(lo, hi + 1, functools.partial(tendencies, lo - base), 0)
+            base += hi - lo + 1
 
         total = -(-6 * count // PAIR)
         units = 2 if total == 4 else 3
@@ -389,7 +406,7 @@
 
             def cut_of(unit):
                 at = pl.multiple_of((p * units + unit) * PAIR, PAIR)
-                return cut_ref[3 * upper + index, pl.ds(at, PAIR), :]
+                return cut_ref[3 * outer + index, pl.ds(at, PAIR), :]
 
             def analyse(unit, half):
                 re, im = real_fft([t_ref[place(unit, a, half), :] for a in range(RADIX)])
@@ -455,39 +472,45 @@
                     synthesise(unit, half)
             return carry
 
-        @pl.when(flags[3 * upper + index] > 0)
+        @pl.when(flags[3 * outer + index] > 0)
         def _():
             lax.fori_loop(0, -(-total // units), circle_filter, 0)
 
-        def update(r, carry):
+        def update(shift, r, carry):
             inside = coef[6, r]
             for f in range(6):
                 for d in range(chunks):
-                    start = (d * TILE_ROWS + (r - lo) * 6 + f) * SUB
+                    start = (d * TILE_ROWS + (r - shift) * 6 + f) * SUB
                     change = t_ref[pl.ds(pl.multiple_of(start, SUB), SUB), :]
                     value = inside * (x_ref[d, r * 7 + f] + (fraction * step_size) * change)
                     if final:
-                        out_ref[d, (r - lo) * 6 + f] = value
+                        out_ref[d, (r - shift) * 6 + f] = value
                     else:
                         dst[d, r * 6 + f] = value
             return carry
 
-        if final:
-            for i in range(2):
-                lax.fori_loop(lo + i * (count // 2), lo + (i + 1) * (count // 2), update, 0)
+        spans = ranges[index]
+        if final and not outer:
+            (lo, hi), middle = spans[0], spans[0][0] + out_edges[1]
+            spans = ((lo, middle - 1), (middle, hi))
+        base = 0
+        for i, (lo, hi) in enumerate(spans):
+            lax.fori_loop(lo, hi + 1, functools.partial(update, lo - base), 0)
+            base += hi - lo + 1
+            if final:
                 departure(i).start()
-        else:
-            lax.fori_loop(lo, hi + 1, update, 0)
-            if not upper:
-                edge(index).start()
+        if not final and not outer:
+            for copy in edges(index):
+                copy.start()
 
     stage(x_ref, s1_ref, 0, 1.0 / 3.0)
     stage(s1_ref, s2_ref, 1, 0.5)
     stage(s2_ref, None, 2, 1.0)
     for i in range(2):
         departure(i).wait()
-        if not upper:
-            edge(i).wait()
+        if not outer:
+            for copy in edges(i):
+                copy.wait()
 
 
 def row_tables(cutoffs, row_start, height, total_rows, polar):
@@ -513,9 +536,9 @@
     )
     cut = jnp.where(capped, cut, UNCUT)
     stages = []
-    for upper in (False, True):
-        for lo, hi in stage_rows(height, upper):
-            rows = jnp.repeat(cut[lo : hi + 1], 6)
+    for outer in (False, True):
+        for spans in stage_rows(height, outer):
+            rows = jnp.repeat(jnp.concatenate([cut[lo : hi + 1] for lo, hi in spans]), 6)
             stages.append(jnp.pad(rows, (0, TILE_ROWS - rows.shape[0]), constant_values=UNCUT))
     cuts = jnp.stack(stages)
     flags = jnp.any(cuts < UNCUT, axis=1).astype(jnp.int32)
@@ -557,7 +580,7 @@
 
     packed_low, packed_high = pl.pallas_call(
         functools.partial(pack_kernel, bands),
-        out_shape=(piece(CUT, 7), piece(height - CUT, 7)),
+        out_shape=(piece(INNER, 7), piece(height - INNER, 7)),
         in_specs=[smem] + [hbm] * 3,
         out_specs=(hbm, hbm),
         scratch_shapes=[
@@ -566,87 +589,77 @@
             pltpu.VMEM(terrain.shape, jnp.float32),
             pltpu.VMEM(piece(height, 7).shape, jnp.float32),
             pltpu.SemaphoreType.DMA((3, sectors)),
-            pltpu.SemaphoreType.DMA((2, sectors)),
+            pltpu.SemaphoreType.DMA((3, sectors)),
         ],
         compiler_params=pltpu.CompilerParams(vmem_limit_bytes=56 << 20),
         cost_estimate=pl.CostEstimate(flops=0, bytes_accessed=12 << 20, transcendentals=0),
         name="pack",
     )(lat.reshape(1).astype(jnp.int32), thickness, flat, terrain)
 
-    def rimmed(packed, rows, group, start):
-        return pl.pallas_call(
-            functools.partial(rim_kernel, group, start),
-            out_shape=jax.ShapeDtypeStruct(packed.shape, jnp.float32),
-            in_specs=[pl.BlockSpec(memory_space=pl.ANY), hbm],
-            out_specs=hbm,
-            scratch_shapes=[pltpu.SemaphoreType.DMA],
-            input_output_aliases={1: 0},
-            name="rim",
-        )(rows, packed)
-
-    packed_low = rimmed(packed_low, south, 0, 0)
-    packed_high = rimmed(packed_high, north, sectors - 1, (HALO + own - CUT) * 7 * SUB)
+    packed_high = pl.pallas_call(
+        rim_kernel,
+        out_shape=jax.ShapeDtypeStruct(packed_high.shape, jnp.float32),
+        in_specs=[vmem, vmem, hbm],
+        out_specs=hbm,
+        scratch_shapes=[pltpu.SemaphoreType.DMA((2,))],
+        input_output_aliases={2: 0},
+        name="rim",
+    )(south, north, packed_high)
     circles_low = lax.all_to_all(packed_low, "lon", 0, 0)
     circles_high = lax.all_to_all(packed_high, "lon", 0, 0)
 
     row_start = lat * row_count + lax.axis_index("lon") * own
     coef, flags, cuts = row_tables(cutoffs, row_start, height, total_rows, polar)
     tables = [jnp.asarray(t) for t in filter_tables()]
-    edges = jax.ShapeDtypeStruct((sectors, 12, SUB, LANES), jnp.float32)
-
-    def step(upper, states, saved):
-        lo, hi = stage_rows(height, upper)[2]
-        out = jax.ShapeDtypeStruct((sectors, 6 * (hi - lo + 1), SUB, LANES), jnp.float32)
+    edges = jax.ShapeDtypeStruct((sectors, 24, SUB, LANES), jnp.float32)
+
+    def step(outer, states, saved):
+        rows = sum(hi - lo + 1 for lo, hi in stage_rows(height, outer)[2])
+        out = jax.ShapeDtypeStruct((sectors, 6 * rows, SUB, LANES), jnp.float32)
         states = [x.reshape(sectors, -1, SUB, LANES) for x in states]
         return pl.pallas_call(
-            functools.partial(step_kernel, upper, height, merid_step, step_size),
-            out_shape=out if upper else (out, edges, edges),
+            functools.partial(step_kernel, outer, height, merid_step, step_size),
+            out_shape=out if outer else (out, edges, edges),
             in_specs=[smem, smem] + [hbm] * len(states + saved) + [vmem] * 7,
-            out_specs=hbm if upper else (hbm, hbm, hbm),
+            out_specs=hbm if outer else (hbm, hbm, hbm),
             scratch_shapes=[
                 pltpu.VMEM((sectors, 7 * height, SUB, LANES), jnp.float32),
                 pltpu.VMEM((sectors, 6 * height, SUB, LANES), jnp.float32),
                 pltpu.VMEM((sectors, 6 * height, SUB, LANES), jnp.float32),
                 pltpu.VMEM(out.shape, jnp.float32),
                 pltpu.VMEM((sectors * TILE_ROWS * SUB, LANES), jnp.float32),
-                pltpu.SemaphoreType.DMA((3,)),
+                pltpu.SemaphoreType.DMA((4,)),
                 pltpu.SemaphoreType.DMA((2,)),
-                pltpu.SemaphoreType.DMA((2,)),
+                pltpu.SemaphoreType.DMA((2, 2)),
             ]
             + [pltpu.VMEM((height * 2 * sectors, SUB, LANES), jnp.float32)] * 4
             + [pltpu.VMEM(((HALF + 1) * PAIR, 2 * LANES), jnp.float32)] * UNITS,
-            compiler_params=pltpu.CompilerParams(vmem_limit_bytes=50 << 20),
+            compiler_params=pltpu.CompilerParams(vmem_limit_bytes=53 << 20),
             cost_estimate=pl.CostEstimate(flops=0, bytes_accessed=64 << 20, transcendentals=0),
-            name="step_high" if upper else "step_low",
+            name="step_outer" if outer else "step_inner",
         )(coef, flags, *states, *saved, cuts, *tables)
 
     new_low, *saved = step(False, [circles_low], [])
     returned_low = lax.all_to_all(new_low.reshape(sectors, -1, LANES), "lon", 0, 0)
     new_high = step(True, [circles_low, circles_high], saved)
+    returned_low, new_high = lax.optimization_barrier((returned_low, new_high))
     returned_high = lax.all_to_all(new_high.reshape(sectors, -1, LANES), "lon", 0, 0)
 
-    def unpack(first, pieces, outputs):
-        rows = pieces.shape[1] // (6 * SUB)
-        return pl.pallas_call(
-            functools.partial(unpack_kernel, first),
-            out_shape=(
-                jax.ShapeDtypeStruct(thickness.shape, jnp.float32),
-                jax.ShapeDtypeStruct(flat.shape, jnp.float32),
-            ),
-            in_specs=[vmem] + [hbm] * len(outputs),
-            out_specs=(hbm, hbm),
-            scratch_shapes=[
-                pltpu.VMEM((6, sectors, rows, col_count), jnp.float32),
-                pltpu.SemaphoreType.DMA((6, sectors)),
-            ],
-            input_output_aliases={1: 0, 2: 1} if outputs else {},
-            compiler_params=pltpu.CompilerParams(vmem_limit_bytes=40 << 20),
-            cost_estimate=pl.CostEstimate(flops=0, bytes_accessed=4 << 20, transcendentals=0),
-            name="unpack",
-        )(pieces, *outputs)
-
-    outputs = unpack(0, returned_low, ())
-    new_thickness, new_winds = unpack(own // 2, returned_high, outputs)
+    new_thickness, new_winds = pl.pallas_call(
+        unpack_kernel,
+        out_shape=(
+            jax.ShapeDtypeStruct(thickness.shape, jnp.float32),
+            jax.ShapeDtypeStruct(flat.shape, jnp.float32),
+        ),
+        in_specs=[vmem, vmem],
+        out_specs=(hbm, hbm),
+        scratch_shapes=[
+            pltpu.VMEM((6, row_count, col_count), jnp.float32),
+            pltpu.SemaphoreType.DMA((6,)),
+        ],
+        compiler_params=pltpu.CompilerParams(vmem_limit_bytes=40 << 20),
+        name="unpack",
+    )(returned_low, returned_high)
     return new_thickness, new_winds.reshape(winds.shape)
 
 

time: 145 us -> 136 us (0.938)
  blocking collectives: 0 us -> 25.6 us
  waiting for transfers between devices: 52.4 us -> 29 us
  Pallas kernels: 62.3 us -> 56.4 us
  starting transfers between devices: 25.5 us -> 20.7 us
    all_to_all x0 -> x1, blocking collectives: none -> 25.6 us  [body(): lax.all_to_all(new_high.reshape(sectors, -1, LANES), 'lon', 0, 0)]
    all_to_all x1 -> x0, waiting for transfers between devices: 19.2 us -> none  [body(): lax.all_to_all(new_high.reshape(sectors, -1, LANES), 'lon', 0, 0)]
    pallas_call x7 -> x5, Pallas kernels: 60.6 us -> 54.7 us  [the longest x2 46.9 us: step(): pl.pallas_call(functools.partial(step_kernel, outer, height, merid_step,...]
    all_to_all x1 -> x0, starting transfers between devices: 4.35 us -> none  [body(): lax.all_to_all(new_high.reshape(sectors, -1, LANES), 'lon', 0, 0)]
    all_to_all x1, waiting for transfers between devices: 27.5 us -> 24.3 us  [body(): circles_low = lax.all_to_all(packed_low, 'lon', 0, 0)]
  transfers between devices with their start and end apart: 6 -> 5, of which waited for: 4 -> 3; matrix products, arithmetic and copies ran while one was open for 1% -> 2% of each run, Pallas kernels for 38% -> 37%
where the time goes in v5:
time: 136 us
  Pallas kernels  56.4 us (41%)
  waiting for transfers between devices  29 us (21%)
  blocking collectives  25.6 us (19%)
  starting transfers between devices  20.7 us (15%)
  local copies, waits for them, and re-layouts  2.16 us (2%)
    pallas_call x2, Pallas kernels, step(): pl.pallas_call(functools.partial(step_kernel, outer, height, merid_step,...  46.9 us
    all_to_all x1, blocking collectives, body(): lax.all_to_all(new_high.reshape(sectors, -1, LANES), 'lon', 0, 0)  25.6 us
    all_to_all x1, waiting for transfers between devices, body(): circles_low = lax.all_to_all(packed_low, 'lon', 0, 0)  24.3 us
    all_to_all x1, starting transfers between devices, body(): circles_low = lax.all_to_all(packed_low, 'lon', 0, 0)  5.98 us
    all_to_all x1, starting transfers between devices, body(): circles_high = lax.all_to_all(packed_high, 'lon', 0, 0)  5.07 us
    all_to_all x1, starting transfers between devices, body(): lax.all_to_all(new_low.reshape(sectors, -1, LANES), 'lon', 0, 0)  4.83 us
    ppermute x1, waiting for transfers between devices, body(): north = lax.ppermute(head, 'lat', [(i + 1, i) for i in range(bands - 1)])  4.19 us
    pallas_call x1, Pallas kernels, body(): pl.pallas_call(functools.partial(pack_kernel, bands), out_shape=(piece(IN...  3.91 us
  transfers between devices with their start and end apart: 5, of which 3 were waited for; matrix products, arithmetic and copies ran while one was open for 2% of the time, Pallas kernels for 37%

profile of v5, /device:TPU:1, one launch (start us, length us, event | category | flops | bytes accessed | tf_op | source)
XLA Modules:
  0.0 135.6 jit_solution(18326961461766526319)
XLA Ops:
  0.6 3.9 %pack.1 = (f32[8,784,128]{2,1,0:T(8,128)}, f32[8,448,128]{2,1,0:T(8,128)}) custom-call(s32[1]{0:T(128)} %bitcast.6.lat_ref, f32[2,128,1024]{2,1,0:T(8,128)} %th_ref.1, f32[4,128,1024]{2,1,0:T(8,128)} %bitcast.19, f32[128,1024]{1,0:T(8,128)} %te_ref.1), custom_call_target="tpu_custom_call" | custom-call | bytes 12582912 | tf_op jit(solution)/shard_map/pack/pallas_call | solution.py:581
  4.6 6.0 %all-to-all-start = ((f32[8,784,128]{2,1,0:T(8,128)}), f32[8,784,128]{2,1,0:T(8,128)}, u32[]{:S(2)}, u32[]{:S(2)}) async-start(f32[8,784,128]{2,1,0:T(8,128)} %get-tuple-element.13), calls=%async_computation | async-start | bytes 6422528 | tf_op jit(solution)/shard_map/all_to_all | solution.py:608
  10.5 1.8 %edge.1 = (f32[168,128]{1,0:T(8,128)}, f32[168,128]{1,0:T(8,128)}) custom-call(f32[2,128,1024]{2,1,0:T(8,128)} %th_ref.1, f32[4,128,1024]{2,1,0:T(8,128)} %bitcast.20, f32[128,1024]{1,0:T(8,128)} %te_ref.1), custom_call_target="tpu_custom_call" | custom-call | tf_op jit(solution)/shard_map/edge/pallas_call | solution.py:564
  12.3 3.5 %collective-permute-start = (f32[168,128]{1,0:T(8,128)}, f32[168,128]{1,0:T(8,128)S(1)}, u32[]{:S(2)}, u32[]{:S(2)}) collective-permute-start(f32[168,128]{1,0:T(8,128)} %get-tuple-element.15), channel_id=1, source_target_pairs={{0,8},{8,16},{16,24},{24,32},{32,40},{40,48},{48,56},{56,64},{64,7... | collective-permute-start | bytes 258056 | tf_op jit(solution)/shard_map/ppermute | solution.py:575
  15.8 1.3 collective-permute-start.1
  17.2 0.2 select_reduce_fusion
  17.4 0.1 slice.29
  17.5 0.1 slice.28
  17.6 0.5 collective-permute-done.south_ref
  18.1 4.2 %collective-permute-done.1.north_ref = f32[168,128]{1,0:T(8,128)S(1)} collective-permute-done((f32[168,128]{1,0:T(8,128)}, f32[168,128]{1,0:T(8,128)S(1)}, u32[]{:S(2)}, u32[]{:S(2)}) %collective-permute-start.1) | collective-permute-done | bytes 86048 | tf_op jit(solution)/shard_map/ppermute | solution.py:576
  22.3 0.6 copy-done.7
  22.9 1.6 %rim.1 = f32[8,448,128]{2,1,0:T(8,128)} custom-call(f32[168,128]{1,0:T(8,128)} %copy-done.6, f32[168,128]{1,0:T(8,128)} %copy-done.7, f32[8,448,128]{2,1,0:T(8,128)} %get-tuple-element.17.packed_ref), custom_call_target="tpu_custom_call", output_to_operand_aliasing={{}: (2, {})} | custom-call | tf_op jit(solution)/shard_map/rim/pallas_call | solution.py:599
  24.6 24.3 %all-to-all-done = f32[8,784,128]{2,1,0:T(8,128)} async-done(((f32[8,784,128]{2,1,0:T(8,128)}), f32[8,784,128]{2,1,0:T(8,128)}, u32[]{:S(2)}, u32[]{:S(2)}) %all-to-all-start) | async-done | bytes 3211296 | tf_op jit(solution)/shard_map/all_to_all | solution.py:608
  48.9 5.1 %all-to-all-start.2 = ((f32[8,448,128]{2,1,0:T(8,128)}), f32[8,448,128]{2,1,0:T(8,128)}, u32[]{:S(2)}, u32[]{:S(2)}) async-start(f32[8,448,128]{2,1,0:T(8,128)} %rim.1), calls=%async_computation.2 | async-start | bytes 3670016 | tf_op jit(solution)/shard_map/all_to_all | solution.py:609
  54.0 0.1 fusion.4
  54.1 0.1 fusion.3
  54.1 0.1 pad_add_fusion
  54.3 0.1 reshape.135
  54.4 0.1 pad_add_fusion.2
  54.4 0.1 broadcast_in_dim.60
  54.5 0.1 reshape.137
  54.7 0.1 reshape.134
  54.8 0.1 reshape.136
  55.0 0.1 reshape.132
  55.1 0.1 reshape.133
  55.3 0.1 compare_reduce_fusion
  55.6 0.1 broadcast_in_dim.61.refs_1_.refs_4_
  55.8 26.0 %step_inner.1 = (f32[8,48,8,128]{3,2,1,0:T(8,128)}, f32[8,24,8,128]{3,2,1,0:T(8,128)}, f32[8,24,8,128]{3,2,1,0:T(8,128)}) custom-call(f32[7,22]{1,0:T(8,128)S(1)} %stack.31.coef, s32[6]{0:T(128)S(1)} %convert_element_type.31.flags, f32[8,98,8,128]{3,2,1,0:T(8,128)} %bitcast.8.refs_0_, s32[6,96,128]{2,1,0:T(8,128)S(1)} %broadcast_in_dim.61.refs_1_.refs_4_, ...), custom_call_target="tpu_custom_call" | custom-call | bytes 67108864 | tf_op jit(solution)/shard_map/step_inner/pallas_call | solution.py:620
  81.9 4.8 %all-to-all-start.1 = ((f32[8,384,128]{2,1,0:T(8,128)}), f32[8,384,128]{2,1,0:T(8,128)S(1)}, u32[]{:S(2)}, u32[]{:S(2)}) async-start(f32[8,384,128]{2,1,0:T(8,128)} %bitcast.22), calls=%async_computation.1 | async-start | bytes 3145728 | tf_op jit(solution)/shard_map/all_to_all | solution.py:643
  86.7 20.9 %step_outer.1 = f32[8,48,8,128]{3,2,1,0:T(8,128)} custom-call(f32[7,22]{1,0:T(8,128)S(1)} %stack.31.coef, s32[6]{0:T(128)S(1)} %convert_element_type.31.flags, f32[8,98,8,128]{3,2,1,0:T(8,128)} %bitcast.8.refs_0_, f32[8,56,8,128]{3,2,1,0:T(8,128)} %bitcast.10.refs_1_, f32[8,24,8,128]{3,2,1,0:T(8,128)} %get-tuple-element.18.refs_2_, ...), custom_call_target="tpu_custom_call" | custom-call | bytes 67108864 | tf_op jit(solution)/shard_map/step_outer/pallas_call | solution.py:620
  107.6 25.6 %all_to_all.20.high_ref = f32[8,384,128]{2,1,0:T(8,128)S(1)} all-to-all(f32[8,384,128]{2,1,0:T(8,128)} %bitcast.21), channel_id=1, replica_groups=mesh['lat'=16,'lon'=8] {'lon'}, dimensions={0} | all-to-all | bytes 3145728 | tf_op jit(solution)/shard_map/all_to_all | solution.py:646
  133.2 2.2 %unpack.1 = (f32[2,128,1024]{2,1,0:T(8,128)}, f32[4,128,1024]{2,1,0:T(8,128)}) custom-call(f32[8,384,128]{2,1,0:T(8,128)S(1)} %all-to-all-done.1.low_ref, f32[8,384,128]{2,1,0:T(8,128)S(1)} %all_to_all.20.high_ref), custom_call_target="tpu_custom_call" | custom-call | tf_op jit(solution)/shard_map/unpack/pallas_call | solution.py:648
  (38 shorter events, 0.7 us)
Async XLA Ops:
  4.6 44.4 %all-to-all-start = ((f32[8,784,128]{2,1,0:T(8,128)}), f32[8,784,128]{2,1,0:T(8,128)}, u32[]{:S(2)}, u32[]{:S(2)}) async-start(f32[8,784,128]{2,1,0:T(8,128)} %get-tuple-element.13), calls=%async_computation | async-start | bytes 6422528 | tf_op jit(solution)/shard_map/all_to_all | solution.py:608
  10.5 6.6 %copy-start.8 = (s32[682]{0:T(1024)S(1)}, s32[682]{0:T(1024)}, u32[]{:S(2)}) copy-start(s32[682]{0:T(1024)} %param.13) | copy-start | bytes 8188
  12.3 5.8 %collective-permute-start = (f32[168,128]{1,0:T(8,128)}, f32[168,128]{1,0:T(8,128)S(1)}, u32[]{:S(2)}, u32[]{:S(2)}) collective-permute-start(f32[168,128]{1,0:T(8,128)} %get-tuple-element.15), channel_id=1, source_target_pairs={{0,8},{8,16},{16,24},{24,32},{32,40},{40,48},{48,56},{56,64},{64,7... | collective-permute-start | bytes 258056 | tf_op jit(solution)/shard_map/ppermute | solution.py:575
  15.8 6.4 %collective-permute-start.1 = (f32[168,128]{1,0:T(8,128)}, f32[168,128]{1,0:T(8,128)S(1)}, u32[]{:S(2)}, u32[]{:S(2)}) collective-permute-start(f32[168,128]{1,0:T(8,128)} %get-tuple-element.16), channel_id=1, source_target_pairs={{8,0},{16,8},{24,16},{32,24},{40,32},{48,40},{56,48},{64,56},{72,6... | collective-permute-start | bytes 258056 | tf_op jit(solution)/shard_map/ppermute | solution.py:576
  18.1 4.2 %copy-start.6 = (f32[168,128]{1,0:T(8,128)}, f32[168,128]{1,0:T(8,128)S(1)}, u32[]{:S(2)}) copy-start(f32[168,128]{1,0:T(8,128)S(1)} %collective-permute-done.south_ref) | copy-start | bytes 258052
  22.3 0.6 copy-start.7
  24.5 31.2 %copy-start = (bf16[256,256]{1,0:T(8,128)(2,1)S(1)}, bf16[256,256]{1,0:T(8,128)(2,1)}, u32[]{:S(2)}) copy-start(bf16[256,256]{1,0:T(8,128)(2,1)} %constant.61.clone.refs_5_.refs_8_) | copy-start | bytes 393220
  24.6 31.2 %copy-start.1 = (bf16[256,256]{1,0:T(8,128)(2,1)S(1)}, bf16[256,256]{1,0:T(8,128)(2,1)}, u32[]{:S(2)}) copy-start(bf16[256,256]{1,0:T(8,128)(2,1)} %constant.60.clone.refs_4_.refs_7_) | copy-start | bytes 393220
  24.6 31.2 %copy-start.2 = (bf16[256,256]{1,0:T(8,128)(2,1)S(1)}, bf16[256,256]{1,0:T(8,128)(2,1)}, u32[]{:S(2)}) copy-start(bf16[256,256]{1,0:T(8,128)(2,1)} %constant.59.clone.refs_3_.refs_6_) | copy-start | bytes 393220
  24.6 31.2 %copy-start.3 = (bf16[256,256]{1,0:T(8,128)(2,1)S(1)}, bf16[256,256]{1,0:T(8,128)(2,1)}, u32[]{:S(2)}) copy-start(bf16[256,256]{1,0:T(8,128)(2,1)} %constant.58.clone.refs_2_.refs_5_) | copy-start | bytes 393220
  24.6 31.2 %copy-start.4 = (f32[40,128]{1,0:T(8,128)S(1)}, f32[40,128]{1,0:T(8,128)}, u32[]{:S(2)}) copy-start(f32[40,128]{1,0:T(8,128)} %constant.63.clone.refs_7_.refs_10_) | copy-start | bytes 61444
  24.6 31.2 %copy-start.5 = (f32[40,128]{1,0:T(8,128)S(1)}, f32[40,128]{1,0:T(8,128)}, u32[]{:S(2)}) copy-start(f32[40,128]{1,0:T(8,128)} %constant.62.clone.refs_6_.refs_9_) | copy-start | bytes 61444
  48.9 33.0 %all-to-all-start.2 = ((f32[8,448,128]{2,1,0:T(8,128)}), f32[8,448,128]{2,1,0:T(8,128)}, u32[]{:S(2)}, u32[]{:S(2)}) async-start(f32[8,448,128]{2,1,0:T(8,128)} %rim.1), calls=%async_computation.2 | async-start | bytes 3670016 | tf_op jit(solution)/shard_map/all_to_all | solution.py:609
  81.9 25.8 %all-to-all-start.1 = ((f32[8,384,128]{2,1,0:T(8,128)}), f32[8,384,128]{2,1,0:T(8,128)S(1)}, u32[]{:S(2)}, u32[]{:S(2)}) async-start(f32[8,384,128]{2,1,0:T(8,128)} %bitcast.22), calls=%async_computation.1 | async-start | bytes 3145728 | tf_op jit(solution)/shard_map/all_to_all | solution.py:643

commit v6 on v5

--- a/solution.py
+++ b/solution.py
@@ -126,10 +126,11 @@
                 ]
 
 
-def pack_kernel(bands, lat_ref, th_hbm, wi_hbm, te_hbm, a_hbm, b_hbm, th_ref, wi_ref, te_ref, piece_ref, in_sems, sems):
+def pack_kernel(outer, bands, lat_ref, th_hbm, wi_hbm, te_hbm, out_hbm, th_ref, wi_ref, te_ref, piece_ref, in_sems, sems):
     groups = piece_ref.shape[0]
-    height = piece_ref.shape[1] // (7 * SUB)
-    own = height - 2 * HALO
+    own = te_ref.shape[0] // groups
+    tail = own - INNER
+
     def arrivals(g):
         rows = pl.ds(g * own, own)
         return (
@@ -138,16 +139,11 @@
             pltpu.make_async_copy(te_hbm.at[rows], te_ref.at[rows], in_sems.at[2, g]),
         )
 
-    def departures(g):
-        def copy(i, dst, src_row, dst_row, count):
-            src = piece_ref.at[g, pl.ds(src_row * 7 * SUB, count * 7 * SUB)]
-            dst = dst.at[g, pl.ds(dst_row * 7 * SUB, count * 7 * SUB)]
-            return pltpu.make_async_copy(src, dst, sems.at[i, g])
-
-        top = HALO + INNER
-        last = height if g < groups - 1 else HALO + own
-        copies = [copy(0, a_hbm, HALO, 0, INNER), copy(1, b_hbm, top, HALO, last - top)]
-        return copies + ([copy(2, b_hbm, 0, 0, HALO)] if g > 0 else [])
+    def departure(g):
+        first = 0 if not outer or g > 0 else HALO
+        last = INNER if not outer else HALO + tail + (HALO if g < groups - 1 else 0)
+        rows = pl.ds(first * 7 * SUB, (last - first) * 7 * SUB)
+        return pltpu.make_async_copy(piece_ref.at[g, rows], out_hbm.at[g, rows], sems.at[g])
 
     for g in range(groups):
         for copy in arrivals(g):
@@ -167,25 +163,26 @@
                         pl.ds(start, count), s * LANES : (s + 1) * LANES
                     ]
 
-            for m in range(own // SUB):
-                put(HALO + m * SUB, g * own + m * SUB, SUB)
+            if not outer:
+                for m in range(0, INNER, SUB):
+                    put(m, g * own + m, min(SUB, INNER - m))
+                continue
             if g > 0:
                 put(0, g * own - HALO, HALO)
+            put(HALO, g * own + INNER, tail)
             if g < groups - 1:
-                put(HALO + own, (g + 1) * own, HALO)
-        if g == groups - 1:
+                put(HALO + tail, (g + 1) * own, HALO)
+        if outer and g == groups - 1:
 
             @pl.when(lat_ref[0] == bands - 1)
             def _():
                 for f in (4, 5):
-                    at = pl.ds(((HALO + own - 1) * 7 + f) * SUB, SUB)
+                    at = pl.ds(((HALO + tail - 1) * 7 + f) * SUB, SUB)
                     piece_ref[g, at, :] = jnp.zeros((SUB, LANES), jnp.float32)
 
-        for copy in departures(g):
-            copy.start()
+        departure(g).start()
     for g in range(groups):
-        for copy in departures(g):
-            copy.wait()
+        departure(g).wait()
 
 
 def rim_kernel(south_ref, north_ref, packed_ref, out_ref, sems):
@@ -578,24 +575,28 @@
     def piece(rows, fields):
         return jax.ShapeDtypeStruct((sectors, rows * fields * SUB, LANES), jnp.float32)
 
-    packed_low, packed_high = pl.pallas_call(
-        functools.partial(pack_kernel, bands),
-        out_shape=(piece(INNER, 7), piece(height - INNER, 7)),
-        in_specs=[smem] + [hbm] * 3,
-        out_specs=(hbm, hbm),
-        scratch_shapes=[
-            pltpu.VMEM(thickness.shape, jnp.float32),
-            pltpu.VMEM(flat.shape, jnp.float32),
-            pltpu.VMEM(terrain.shape, jnp.float32),
-            pltpu.VMEM(piece(height, 7).shape, jnp.float32),
-            pltpu.SemaphoreType.DMA((3, sectors)),
-            pltpu.SemaphoreType.DMA((3, sectors)),
-        ],
-        compiler_params=pltpu.CompilerParams(vmem_limit_bytes=56 << 20),
-        cost_estimate=pl.CostEstimate(flops=0, bytes_accessed=12 << 20, transcendentals=0),
-        name="pack",
-    )(lat.reshape(1).astype(jnp.int32), thickness, flat, terrain)
-
+    def pack(outer):
+        out = piece(height - INNER if outer else INNER, 7)
+        return pl.pallas_call(
+            functools.partial(pack_kernel, outer, bands),
+            out_shape=out,
+            in_specs=[smem] + [hbm] * 3,
+            out_specs=hbm,
+            scratch_shapes=[
+                pltpu.VMEM(thickness.shape, jnp.float32),
+                pltpu.VMEM(flat.shape, jnp.float32),
+                pltpu.VMEM(terrain.shape, jnp.float32),
+                pltpu.VMEM(out.shape, jnp.float32),
+                pltpu.SemaphoreType.DMA((3, sectors)),
+                pltpu.SemaphoreType.DMA((sectors,)),
+            ],
+            compiler_params=pltpu.CompilerParams(vmem_limit_bytes=56 << 20),
+            cost_estimate=pl.CostEstimate(flops=0, bytes_accessed=12 << 20, transcendentals=0),
+            name="pack_outer" if outer else "pack_inner",
+        )(lat.reshape(1).astype(jnp.int32), thickness, flat, terrain)
+
+    packed_low = pack(False)
+    packed_high = pack(True)
     packed_high = pl.pallas_call(
         rim_kernel,
         out_shape=jax.ShapeDtypeStruct(packed_high.shape, jnp.float32),
@@ -605,11 +606,12 @@
         input_output_aliases={2: 0},
         name="rim",
     )(south, north, packed_high)
+    row_start = lat * row_count + lax.axis_index("lon") * own
+    coef, flags, cuts = row_tables(cutoffs, row_start, height, total_rows, polar)
+    packed_high, coef, flags, cuts = lax.optimization_barrier((packed_high, coef, flags, cuts))
     circles_low = lax.all_to_all(packed_low, "lon", 0, 0)
     circles_high = lax.all_to_all(packed_high, "lon", 0, 0)
 
-    row_start = lat * row_count + lax.axis_index("lon") * own
-    coef, flags, cuts = row_tables(cutoffs, row_start, height, total_rows, polar)
     tables = [jnp.asarray(t) for t in filter_tables()]
     edges = jax.ShapeDtypeStruct((sectors, 24, SUB, LANES), jnp.float32)
 
@@ -634,7 +636,7 @@
             ]
             + [pltpu.VMEM((height * 2 * sectors, SUB, LANES), jnp.float32)] * 4
             + [pltpu.VMEM(((HALF + 1) * PAIR, 2 * LANES), jnp.float32)] * UNITS,
-            compiler_params=pltpu.CompilerParams(vmem_limit_bytes=53 << 20),
+            compiler_params=pltpu.CompilerParams(vmem_limit_bytes=51 << 20),
             cost_estimate=pl.CostEstimate(flops=0, bytes_accessed=64 << 20, transcendentals=0),
             name="step_outer" if outer else "step_inner",
         )(coef, flags, *states, *saved, cuts, *tables)

time: 136 us -> 138 us (1.015)
  waiting for transfers between devices: 29 us -> 23.4 us
  local copies, waits for them, and re-layouts: 2.16 us -> 6.4 us
  Pallas kernels: 56.4 us -> 59.6 us
    unnamed x18 -> x26, local copies, waits for them, and re-layouts: 0.67 us -> 4.91 us
    ppermute x1, waiting for transfers between devices: 4.19 us -> 0.01 us  [body(): north = lax.ppermute(head, 'lat', [(i + 1, i) for i in range(bands - 1)])]
    pallas_call x1 -> x2, Pallas kernels: 3.91 us -> 6.46 us  [pack(): pl.pallas_call(functools.partial(pack_kernel, outer, bands), out_shape=ou...]
  transfers between devices with their start and end apart: 5 -> 5, of which waited for: 3 -> 1; matrix products, arithmetic and copies ran while one was open for 2% -> 2% of each run, Pallas kernels for 37% -> 39%
where the time goes in v6:
time: 138 us
  Pallas kernels  59.6 us (43%)
  blocking collectives  25.6 us (19%)
  waiting for transfers between devices  23.4 us (17%)
  starting transfers between devices  20.7 us (15%)
  local copies, waits for them, and re-layouts  6.4 us (5%)
    pallas_call x2, Pallas kernels, step(): pl.pallas_call(functools.partial(step_kernel, outer, height, merid_step,...  47.6 us
    all_to_all x1, blocking collectives, body(): lax.all_to_all(new_high.reshape(sectors, -1, LANES), 'lon', 0, 0)  25.6 us
    all_to_all x1, waiting for transfers between devices, body(): circles_low = lax.all_to_all(packed_low, 'lon', 0, 0)  23.4 us
    pallas_call x2, Pallas kernels, pack(): pl.pallas_call(functools.partial(pack_kernel, outer, bands), out_shape=ou...  6.46 us
    all_to_all x1, starting transfers between devices, body(): circles_low = lax.all_to_all(packed_low, 'lon', 0, 0)  5.98 us
    all_to_all x1, starting transfers between devices, body(): circles_high = lax.all_to_all(packed_high, 'lon', 0, 0)  5.08 us
    unnamed x26, local copies, waits for them, and re-layouts  4.91 us
    all_to_all x1, starting transfers between devices, body(): lax.all_to_all(new_low.reshape(sectors, -1, LANES), 'lon', 0, 0)  4.83 us
  transfers between devices with their start and end apart: 5, of which 1 were waited for; matrix products, arithmetic and copies ran while one was open for 2% of the time, Pallas kernels for 39%

profile of v6, /device:TPU:1, one launch (start us, length us, event | category | flops | bytes accessed | tf_op | source)
XLA Modules:
  0.0 137.5 jit_solution(15537408991724576499)
XLA Ops:
  0.6 3.3 %pack_inner.1 = f32[8,784,128]{2,1,0:T(8,128)} custom-call(s32[1]{0:T(128)} %bitcast.1.lat_ref, f32[2,128,1024]{2,1,0:T(8,128)} %th_hbm.3, f32[4,128,1024]{2,1,0:T(8,128)} %bitcast.19, f32[128,1024]{1,0:T(8,128)} %te_hbm.3), custom_call_target="tpu_custom_call" | custom-call | bytes 12582912 | tf_op jit(solution)/shard_map/pack_inner/pallas_call | solution.py:580
  4.0 6.0 %all-to-all-start = ((f32[8,784,128]{2,1,0:T(8,128)}), f32[8,784,128]{2,1,0:T(8,128)}, u32[]{:S(2)}, u32[]{:S(2)}) async-start(f32[8,784,128]{2,1,0:T(8,128)} %pack_inner.1), calls=%async_computation | async-start | bytes 6422528 | tf_op jit(solution)/shard_map/all_to_all | solution.py:612
  10.0 1.8 %edge.1 = (f32[168,128]{1,0:T(8,128)}, f32[168,128]{1,0:T(8,128)}) custom-call(f32[2,128,1024]{2,1,0:T(8,128)} %th_hbm.3, f32[4,128,1024]{2,1,0:T(8,128)} %bitcast.20, f32[128,1024]{1,0:T(8,128)} %te_hbm.3), custom_call_target="tpu_custom_call" | custom-call | tf_op jit(solution)/shard_map/edge/pallas_call | solution.py:561
  11.7 3.5 %collective-permute-start = (f32[168,128]{1,0:T(8,128)}, f32[168,128]{1,0:T(8,128)S(1)}, u32[]{:S(2)}, u32[]{:S(2)}) collective-permute-start(f32[168,128]{1,0:T(8,128)} %get-tuple-element.15), channel_id=1, source_target_pairs={{0,8},{8,16},{16,24},{24,32},{32,40},{40,48},{48,56},{56,64},{64,7... | collective-permute-start | bytes 258056 | tf_op jit(solution)/shard_map/ppermute | solution.py:572
  15.3 1.3 collective-permute-start.1
  16.6 0.2 select_reduce_fusion
  16.8 0.1 slice.29
  17.0 3.1 %pack_outer.1.packed_ref = f32[8,448,128]{2,1,0:T(8,128)} custom-call(s32[1]{0:T(128)} %bitcast.1.lat_ref, f32[2,128,1024]{2,1,0:T(8,128)} %th_hbm.3, f32[4,128,1024]{2,1,0:T(8,128)} %bitcast.21, f32[128,1024]{1,0:T(8,128)} %te_hbm.3), custom_call_target="tpu_custom_call" | custom-call | bytes 12582912 | tf_op jit(solution)/shard_map/pack_outer/pallas_call | solution.py:580
  20.3 0.1 pad_add_fusion
  20.5 0.1 reshape.138
  20.5 0.1 pad_add_fusion.2
  20.7 0.1 reshape.140
  20.8 0.1 reshape.137
  21.0 0.1 reshape.139
  21.1 0.1 reshape.135
  21.3 0.1 reshape.136
  21.5 0.1 compare_reduce_fusion
  21.8 0.6 copy-done.10
  22.5 0.6 copy-done.11
  23.1 1.6 %rim.1 = f32[8,448,128]{2,1,0:T(8,128)} custom-call(f32[168,128]{1,0:T(8,128)} %copy-done.10, f32[168,128]{1,0:T(8,128)} %copy-done.11, f32[8,448,128]{2,1,0:T(8,128)} %pack_outer.1.packed_ref), custom_call_target="tpu_custom_call", output_to_operand_aliasing={{}: (2, {})} | custom-call | tf_op jit(solution)/shard_map/rim/pallas_call | solution.py:600
  24.7 0.1 broadcast_in_dim.61.refs_1_.refs_4_
  24.9 23.4 %all-to-all-done = f32[8,784,128]{2,1,0:T(8,128)} async-done(((f32[8,784,128]{2,1,0:T(8,128)}), f32[8,784,128]{2,1,0:T(8,128)}, u32[]{:S(2)}, u32[]{:S(2)}) %all-to-all-start) | async-done | bytes 3211296 | tf_op jit(solution)/shard_map/all_to_all | solution.py:612
  48.3 5.1 %all-to-all-start.2 = ((f32[8,448,128]{2,1,0:T(8,128)}), f32[8,448,128]{2,1,0:T(8,128)}, u32[]{:S(2)}, u32[]{:S(2)}) async-start(f32[8,448,128]{2,1,0:T(8,128)} %rim.1), calls=%async_computation.2 | async-start | bytes 3670016 | tf_op jit(solution)/shard_map/all_to_all | solution.py:613
  53.5 26.5 %step_inner.1 = (f32[8,48,8,128]{3,2,1,0:T(8,128)}, f32[8,24,8,128]{3,2,1,0:T(8,128)S(1)}, f32[8,24,8,128]{3,2,1,0:T(8,128)S(1)}) custom-call(f32[7,22]{1,0:T(8,128)S(1)} %stack.31.coef, s32[6]{0:T(128)S(1)} %convert_element_type.31.flags, f32[8,98,8,128]{3,2,1,0:T(8,128)} %bitcast.8.refs_0_, s32[6,96,128]{2,1,0:T(8,128)S(1)} %broadcast_in_dim.61.refs_1_.refs_4_, ...), custom_call_target="tpu_custom_call" | custom-call | bytes 67108864 | tf_op jit(solution)/shard_map/step_inner/pallas_call | solution.py:622
  80.0 4.8 %all-to-all-start.1 = ((f32[8,384,128]{2,1,0:T(8,128)}), f32[8,384,128]{2,1,0:T(8,128)S(1)}, u32[]{:S(2)}, u32[]{:S(2)}) async-start(f32[8,384,128]{2,1,0:T(8,128)} %bitcast.23), calls=%async_computation.1 | async-start | bytes 3145728 | tf_op jit(solution)/shard_map/all_to_all | solution.py:645
  84.8 0.9 copy-done.1
  85.7 0.9 copy-done.3
  86.6 0.9 copy-done.5
  87.5 0.9 copy-done.7
  88.4 21.1 %step_outer.1 = f32[8,48,8,128]{3,2,1,0:T(8,128)} custom-call(f32[7,22]{1,0:T(8,128)S(1)} %stack.31.coef, s32[6]{0:T(128)S(1)} %convert_element_type.31.flags, f32[8,98,8,128]{3,2,1,0:T(8,128)} %bitcast.8.refs_0_, f32[8,56,8,128]{3,2,1,0:T(8,128)} %bitcast.10.refs_1_, f32[8,24,8,128]{3,2,1,0:T(8,128)S(1)} %get-tuple-element.22.refs_2_, ...), custom_call_target="tpu_custom_call" | custom-call | bytes 67108864 | tf_op jit(solution)/shard_map/step_outer/pallas_call | solution.py:622
  109.6 25.6 %all_to_all.20.high_ref = f32[8,384,128]{2,1,0:T(8,128)S(1)} all-to-all(f32[8,384,128]{2,1,0:T(8,128)} %bitcast.22), channel_id=1, replica_groups=mesh['lat'=16,'lon'=8] {'lon'}, dimensions={0} | all-to-all | bytes 3145728 | tf_op jit(solution)/shard_map/all_to_all | solution.py:648
  135.1 2.2 %unpack.1 = (f32[2,128,1024]{2,1,0:T(8,128)}, f32[4,128,1024]{2,1,0:T(8,128)}) custom-call(f32[8,384,128]{2,1,0:T(8,128)S(1)} %all-to-all-done.1.low_ref, f32[8,384,128]{2,1,0:T(8,128)S(1)} %all_to_all.20.high_ref), custom_call_target="tpu_custom_call" | custom-call | tf_op jit(solution)/shard_map/unpack/pallas_call | solution.py:650
  (47 shorter events, 1.0 us)
Async XLA Ops:
  4.0 44.4 %all-to-all-start = ((f32[8,784,128]{2,1,0:T(8,128)}), f32[8,784,128]{2,1,0:T(8,128)}, u32[]{:S(2)}, u32[]{:S(2)}) async-start(f32[8,784,128]{2,1,0:T(8,128)} %pack_inner.1), calls=%async_computation | async-start | bytes 6422528 | tf_op jit(solution)/shard_map/all_to_all | solution.py:612
  10.0 6.6 %copy-start.12 = (s32[682]{0:T(1024)S(1)}, s32[682]{0:T(1024)}, u32[]{:S(2)}) copy-start(s32[682]{0:T(1024)} %param.13) | copy-start | bytes 8188
  11.7 10.1 %collective-permute-start = (f32[168,128]{1,0:T(8,128)}, f32[168,128]{1,0:T(8,128)S(1)}, u32[]{:S(2)}, u32[]{:S(2)}) collective-permute-start(f32[168,128]{1,0:T(8,128)} %get-tuple-element.15), channel_id=1, source_target_pairs={{0,8},{8,16},{16,24},{24,32},{32,40},{40,48},{48,56},{56,64},{64,7... | collective-permute-start | bytes 258056 | tf_op jit(solution)/shard_map/ppermute | solution.py:572
  15.3 6.5 %collective-permute-start.1 = (f32[168,128]{1,0:T(8,128)}, f32[168,128]{1,0:T(8,128)S(1)}, u32[]{:S(2)}, u32[]{:S(2)}) collective-permute-start(f32[168,128]{1,0:T(8,128)} %get-tuple-element.16), channel_id=1, source_target_pairs={{8,0},{16,8},{24,16},{32,24},{40,32},{48,40},{56,48},{64,56},{72,6... | collective-permute-start | bytes 258056 | tf_op jit(solution)/shard_map/ppermute | solution.py:573
  21.8 0.6 copy-start.10
  22.5 0.6 copy-start.11
  24.8 28.6 %copy-start = (bf16[256,256]{1,0:T(8,128)(2,1)S(1)}, bf16[256,256]{1,0:T(8,128)(2,1)}, u32[]{:S(2)}) copy-start(bf16[256,256]{1,0:T(8,128)(2,1)} %constant.61.clone.refs_5_.refs_8_) | copy-start | bytes 393220
  24.9 28.6 %copy-start.2 = (bf16[256,256]{1,0:T(8,128)(2,1)S(1)}, bf16[256,256]{1,0:T(8,128)(2,1)}, u32[]{:S(2)}) copy-start(bf16[256,256]{1,0:T(8,128)(2,1)} %constant.60.clone.refs_4_.refs_7_) | copy-start | bytes 393220
  24.9 28.6 %copy-start.4 = (bf16[256,256]{1,0:T(8,128)(2,1)S(1)}, bf16[256,256]{1,0:T(8,128)(2,1)}, u32[]{:S(2)}) copy-start(bf16[256,256]{1,0:T(8,128)(2,1)} %constant.59.clone.refs_3_.refs_6_) | copy-start | bytes 393220
  24.9 28.6 %copy-start.6 = (bf16[256,256]{1,0:T(8,128)(2,1)S(1)}, bf16[256,256]{1,0:T(8,128)(2,1)}, u32[]{:S(2)}) copy-start(bf16[256,256]{1,0:T(8,128)(2,1)} %constant.58.clone.refs_2_.refs_5_) | copy-start | bytes 393220
  24.9 28.6 %copy-start.8 = (f32[40,128]{1,0:T(8,128)S(1)}, f32[40,128]{1,0:T(8,128)}, u32[]{:S(2)}) copy-start(f32[40,128]{1,0:T(8,128)} %constant.63.clone.refs_7_.refs_10_) | copy-start | bytes 61444
  24.9 28.5 %copy-start.9 = (f32[40,128]{1,0:T(8,128)S(1)}, f32[40,128]{1,0:T(8,128)}, u32[]{:S(2)}) copy-start(f32[40,128]{1,0:T(8,128)} %constant.62.clone.refs_6_.refs_9_) | copy-start | bytes 61444
  48.3 31.6 %all-to-all-start.2 = ((f32[8,448,128]{2,1,0:T(8,128)}), f32[8,448,128]{2,1,0:T(8,128)}, u32[]{:S(2)}, u32[]{:S(2)}) async-start(f32[8,448,128]{2,1,0:T(8,128)} %rim.1), calls=%async_computation.2 | async-start | bytes 3670016 | tf_op jit(solution)/shard_map/all_to_all | solution.py:613
  80.0 29.6 %all-to-all-start.1 = ((f32[8,384,128]{2,1,0:T(8,128)}), f32[8,384,128]{2,1,0:T(8,128)S(1)}, u32[]{:S(2)}, u32[]{:S(2)}) async-start(f32[8,384,128]{2,1,0:T(8,128)} %bitcast.23), calls=%async_computation.1 | async-start | bytes 3145728 | tf_op jit(solution)/shard_map/all_to_all | solution.py:645
  84.8 0.9 copy-start.1
  85.7 0.9 copy-start.3
  86.6 0.9 copy-start.5
  87.5 0.9 copy-start.7

commit v7 on v6

--- a/solution.py
+++ b/solution.py
@@ -636,7 +636,7 @@
             ]
             + [pltpu.VMEM((height * 2 * sectors, SUB, LANES), jnp.float32)] * 4
             + [pltpu.VMEM(((HALF + 1) * PAIR, 2 * LANES), jnp.float32)] * UNITS,
-            compiler_params=pltpu.CompilerParams(vmem_limit_bytes=51 << 20),
+            compiler_params=pltpu.CompilerParams(vmem_limit_bytes=54 << 20),
             cost_estimate=pl.CostEstimate(flops=0, bytes_accessed=64 << 20, transcendentals=0),
             name="step_outer" if outer else "step_inner",
         )(coef, flags, *states, *saved, cuts, *tables)

time: 138 us -> 135 us (0.978)
  local copies, waits for them, and re-layouts: 6.4 us -> 4.06 us
  waiting for transfers between devices: 23.4 us -> 21.5 us
    unnamed x26 -> x8, local copies, waits for them, and re-layouts: 4.91 us -> 1.26 us
    all_to_all x1, waiting for transfers between devices: 23.4 us -> 21.5 us  [body(): circles_low = lax.all_to_all(packed_low, 'lon', 0, 0)]
  transfers between devices with their start and end apart: 5 -> 5, of which waited for: 1 -> 1; matrix products, arithmetic and copies ran while one was open for 2% -> 3% of each run, Pallas kernels for 39% -> 41%
where the time goes in v7:
time: 135 us; the launch traced here: 134 us
  Pallas kernels  60.1 us (45%)
  blocking collectives  25.6 us (19%)
  waiting for transfers between devices  21.5 us (16%)
  starting transfers between devices  20.7 us (15%)
  local copies, waits for them, and re-layouts  4.06 us (3%)
    pallas_call x2, Pallas kernels, step(): pl.pallas_call(functools.partial(step_kernel, outer, height, merid_step,...  48.1 us
    all_to_all x1, blocking collectives, body(): lax.all_to_all(new_high.reshape(sectors, -1, LANES), 'lon', 0, 0)  25.6 us
    all_to_all x1, waiting for transfers between devices, body(): circles_low = lax.all_to_all(packed_low, 'lon', 0, 0)  21.5 us
    pallas_call x2, Pallas kernels, pack(): pl.pallas_call(functools.partial(pack_kernel, outer, bands), out_shape=ou...  6.41 us
    all_to_all x1, starting transfers between devices, body(): circles_low = lax.all_to_all(packed_low, 'lon', 0, 0)  5.98 us
    all_to_all x1, starting transfers between devices, body(): circles_high = lax.all_to_all(packed_high, 'lon', 0, 0)  5.07 us
    all_to_all x1, starting transfers between devices, body(): lax.all_to_all(new_low.reshape(sectors, -1, LANES), 'lon', 0, 0)  4.84 us
    ppermute x1, starting transfers between devices, body(): south = lax.ppermute(tail, 'lat', [(i, i + 1) for i in range(bands - 1)])  3.55 us
  transfers between devices with their start and end apart: 5, of which 1 were waited for; matrix products, arithmetic and copies ran while one was open for 3% of the time, Pallas kernels for 41%

profile of v7, /device:TPU:1, one launch (start us, length us, event | category | flops | bytes accessed | tf_op | source)
XLA Modules:
  0.0 134.2 jit_solution(7101624825223455391)
XLA Ops:
  0.6 3.3 %pack_inner.1 = f32[8,784,128]{2,1,0:T(8,128)} custom-call(s32[1]{0:T(128)} %bitcast.1.lat_ref, f32[2,128,1024]{2,1,0:T(8,128)} %th_hbm.3, f32[4,128,1024]{2,1,0:T(8,128)} %bitcast.21, f32[128,1024]{1,0:T(8,128)} %te_hbm.3), custom_call_target="tpu_custom_call" | custom-call | bytes 12582912 | tf_op jit(solution)/shard_map/pack_inner/pallas_call | solution.py:580
  3.9 6.0 %all-to-all-start = ((f32[8,784,128]{2,1,0:T(8,128)}), f32[8,784,128]{2,1,0:T(8,128)S(1)}, u32[]{:S(2)}, u32[]{:S(2)}) async-start(f32[8,784,128]{2,1,0:T(8,128)} %pack_inner.1), calls=%async_computation | async-start | bytes 6422528 | tf_op jit(solution)/shard_map/all_to_all | solution.py:612
  9.9 1.8 %edge.1 = (f32[168,128]{1,0:T(8,128)}, f32[168,128]{1,0:T(8,128)}) custom-call(f32[2,128,1024]{2,1,0:T(8,128)} %th_hbm.3, f32[4,128,1024]{2,1,0:T(8,128)} %bitcast.22, f32[128,1024]{1,0:T(8,128)} %te_hbm.3), custom_call_target="tpu_custom_call" | custom-call | tf_op jit(solution)/shard_map/edge/pallas_call | solution.py:561
  11.7 3.5 %collective-permute-start = (f32[168,128]{1,0:T(8,128)}, f32[168,128]{1,0:T(8,128)S(1)}, u32[]{:S(2)}, u32[]{:S(2)}) collective-permute-start(f32[168,128]{1,0:T(8,128)} %get-tuple-element.15), channel_id=1, source_target_pairs={{0,8},{8,16},{16,24},{24,32},{32,40},{40,48},{48,56},{56,64},{64,7... | collective-permute-start | bytes 258056 | tf_op jit(solution)/shard_map/ppermute | solution.py:572
  15.2 1.3 collective-permute-start.1
  16.6 0.2 select_reduce_fusion
  16.7 0.1 slice.29
  17.0 3.1 %pack_outer.1.packed_ref = f32[8,448,128]{2,1,0:T(8,128)} custom-call(s32[1]{0:T(128)} %bitcast.1.lat_ref, f32[2,128,1024]{2,1,0:T(8,128)} %th_hbm.3, f32[4,128,1024]{2,1,0:T(8,128)} %bitcast.23, f32[128,1024]{1,0:T(8,128)} %te_hbm.3), custom_call_target="tpu_custom_call" | custom-call | bytes 12582912 | tf_op jit(solution)/shard_map/pack_outer/pallas_call | solution.py:580
  20.1 0.1 fusion.4
  20.3 0.1 pad_add_fusion
  20.4 0.1 reshape.138
  20.5 0.1 pad_add_fusion.2
  20.6 0.1 broadcast_in_dim.60
  20.6 0.1 reshape.140
  20.8 0.1 reshape.137
  20.9 0.1 reshape.139
  21.1 0.1 reshape.135
  21.3 0.1 reshape.136
  21.4 0.1 compare_reduce_fusion
  21.5 0.6 convert_element_type.31.flags
  22.3 0.6 stack.31.coef
  22.9 0.6 copy-done.1
  23.6 0.6 copy-done.2
  24.2 1.6 %rim.1 = f32[8,448,128]{2,1,0:T(8,128)} custom-call(f32[168,128]{1,0:T(8,128)} %copy-done.1, f32[168,128]{1,0:T(8,128)} %copy-done.2, f32[8,448,128]{2,1,0:T(8,128)} %pack_outer.1.packed_ref), custom_call_target="tpu_custom_call", output_to_operand_aliasing={{}: (2, {})} | custom-call | tf_op jit(solution)/shard_map/rim/pallas_call | solution.py:600
  25.8 0.8 broadcast_in_dim.61.refs_1_.refs_4_
  26.7 21.5 %all-to-all-done = f32[8,784,128]{2,1,0:T(8,128)S(1)} async-done(((f32[8,784,128]{2,1,0:T(8,128)}), f32[8,784,128]{2,1,0:T(8,128)S(1)}, u32[]{:S(2)}, u32[]{:S(2)}) %all-to-all-start) | async-done | bytes 3211296 | tf_op jit(solution)/shard_map/all_to_all | solution.py:612
  48.2 5.1 %all-to-all-start.2 = ((f32[8,448,128]{2,1,0:T(8,128)}), f32[8,448,128]{2,1,0:T(8,128)}, u32[]{:S(2)}, u32[]{:S(2)}) async-start(f32[8,448,128]{2,1,0:T(8,128)} %rim.1), calls=%async_computation.2 | async-start | bytes 3670016 | tf_op jit(solution)/shard_map/all_to_all | solution.py:613
  53.3 26.7 %step_inner.1 = (f32[8,48,8,128]{3,2,1,0:T(8,128)}, f32[8,24,8,128]{3,2,1,0:T(8,128)}, f32[8,24,8,128]{3,2,1,0:T(8,128)}) custom-call(f32[7,22]{1,0:T(8,128)} %stack.31.coef, s32[6]{0:T(128)} %convert_element_type.31.flags, f32[8,98,8,128]{3,2,1,0:T(8,128)} %bitcast.19, s32[6,96,128]{2,1,0:T(8,128)} %broadcast_in_dim.61.refs_1_.refs_4_, ...), custom_call_target="tpu_custom_call" | custom-call | bytes 67108864 | tf_op jit(solution)/shard_map/step_inner/pallas_call | solution.py:622
  80.0 4.8 %all-to-all-start.1 = ((f32[8,384,128]{2,1,0:T(8,128)}), f32[8,384,128]{2,1,0:T(8,128)S(1)}, u32[]{:S(2)}, u32[]{:S(2)}) async-start(f32[8,384,128]{2,1,0:T(8,128)} %bitcast.25), calls=%async_computation.1 | async-start | bytes 3145728 | tf_op jit(solution)/shard_map/all_to_all | solution.py:645
  84.8 21.4 %step_outer.1 = f32[8,48,8,128]{3,2,1,0:T(8,128)} custom-call(f32[7,22]{1,0:T(8,128)} %stack.31.coef, s32[6]{0:T(128)} %convert_element_type.31.flags, f32[8,98,8,128]{3,2,1,0:T(8,128)} %bitcast.20, f32[8,56,8,128]{3,2,1,0:T(8,128)} %bitcast.10.refs_1_, f32[8,24,8,128]{3,2,1,0:T(8,128)} %get-tuple-element.22.refs_2_, ...), custom_call_target="tpu_custom_call" | custom-call | bytes 67108864 | tf_op jit(solution)/shard_map/step_outer/pallas_call | solution.py:622
  106.2 25.6 %all_to_all.20.high_ref = f32[8,384,128]{2,1,0:T(8,128)S(1)} all-to-all(f32[8,384,128]{2,1,0:T(8,128)} %bitcast.24), channel_id=1, replica_groups=mesh['lat'=16,'lon'=8] {'lon'}, dimensions={0} | all-to-all | bytes 3145728 | tf_op jit(solution)/shard_map/all_to_all | solution.py:648
  131.8 2.2 %unpack.1 = (f32[2,128,1024]{2,1,0:T(8,128)}, f32[4,128,1024]{2,1,0:T(8,128)}) custom-call(f32[8,384,128]{2,1,0:T(8,128)S(1)} %all-to-all-done.1.low_ref, f32[8,384,128]{2,1,0:T(8,128)S(1)} %all_to_all.20.high_ref), custom_call_target="tpu_custom_call" | custom-call | tf_op jit(solution)/shard_map/unpack/pallas_call | solution.py:650
  (29 shorter events, 0.8 us)
Async XLA Ops:
  3.9 44.3 %all-to-all-start = ((f32[8,784,128]{2,1,0:T(8,128)}), f32[8,784,128]{2,1,0:T(8,128)S(1)}, u32[]{:S(2)}, u32[]{:S(2)}) async-start(f32[8,784,128]{2,1,0:T(8,128)} %pack_inner.1), calls=%async_computation | async-start | bytes 6422528 | tf_op jit(solution)/shard_map/all_to_all | solution.py:612
  9.9 6.6 %copy-start.3 = (s32[682]{0:T(1024)S(1)}, s32[682]{0:T(1024)}, u32[]{:S(2)}) copy-start(s32[682]{0:T(1024)} %param.13) | copy-start | bytes 8188
  11.7 11.3 %collective-permute-start = (f32[168,128]{1,0:T(8,128)}, f32[168,128]{1,0:T(8,128)S(1)}, u32[]{:S(2)}, u32[]{:S(2)}) collective-permute-start(f32[168,128]{1,0:T(8,128)} %get-tuple-element.15), channel_id=1, source_target_pairs={{0,8},{8,16},{16,24},{24,32},{32,40},{40,48},{48,56},{56,64},{64,7... | collective-permute-start | bytes 258056 | tf_op jit(solution)/shard_map/ppermute | solution.py:572
  15.2 7.7 %collective-permute-start.1 = (f32[168,128]{1,0:T(8,128)}, f32[168,128]{1,0:T(8,128)S(1)}, u32[]{:S(2)}, u32[]{:S(2)}) collective-permute-start(f32[168,128]{1,0:T(8,128)} %get-tuple-element.16), channel_id=1, source_target_pairs={{8,0},{16,8},{24,16},{32,24},{40,32},{48,40},{56,48},{64,56},{72,6... | collective-permute-start | bytes 258056 | tf_op jit(solution)/shard_map/ppermute | solution.py:573
  22.9 0.6 copy-start.1
  23.6 0.6 copy-start.2
  48.2 5.1 %copy-start = (f32[8,784,128]{2,1,0:T(8,128)}, f32[8,784,128]{2,1,0:T(8,128)S(1)}, u32[]{:S(2)}) copy-start(f32[8,784,128]{2,1,0:T(8,128)S(1)} %all-to-all-done) | copy-start | bytes 9633796
  48.2 31.8 %all-to-all-start.2 = ((f32[8,448,128]{2,1,0:T(8,128)}), f32[8,448,128]{2,1,0:T(8,128)}, u32[]{:S(2)}, u32[]{:S(2)}) async-start(f32[8,448,128]{2,1,0:T(8,128)} %rim.1), calls=%async_computation.2 | async-start | bytes 3670016 | tf_op jit(solution)/shard_map/all_to_all | solution.py:613
  80.0 26.3 %all-to-all-start.1 = ((f32[8,384,128]{2,1,0:T(8,128)}), f32[8,384,128]{2,1,0:T(8,128)S(1)}, u32[]{:S(2)}, u32[]{:S(2)}) async-start(f32[8,384,128]{2,1,0:T(8,128)} %bitcast.25), calls=%async_computation.1 | async-start | bytes 3145728 | tf_op jit(solution)/shard_map/all_to_all | solution.py:645
